TPU v7x, 32 devices: a whole 2x2x4 slice. The times are simulated.
32 devices in a mesh: row: 4 (over y, core), col: 8 (over z, x).
Axes of the slice: x: 2, y: 2, z: 4, core: 2. Of those that a mesh axis runs over, the one named last changes fastest.
Arguments:
- inputs: bfloat16 [8192, 2048], P('row', 'col'), may hold values from -6 to 6
- prefix_len: int32 [4], P('row'), may hold values from 204 to 1024
- w_qkv: bfloat16 [2048, 16, 384], P('row', 'col'), may hold values from -0.125 to 0.125
- w_out: bfloat16 [2048, 2048], P('col', 'row'), may hold values from -1.5 to 1.5
- w_up_gate: bfloat16 [2048, 2, 8192], P('row', None, 'col'), may hold values from -0.125 to 0.125
- w_down: bfloat16 [8192, 2048], P('col', 'row'), may hold values from -0.0625 to 0.0625
- cotangent: bfloat16 [8192, 2048], P('row', 'col'), may hold values from -6 to 6
Outputs:
- outputs: bfloat16 [8192, 2048], P('row', 'col')
- input_grad: float32 [8192, 2048], P('row', 'col')
- grad_qkv: float32 [2048, 16, 384], P('row', 'col')
- grad_out: float32 [2048, 2048], P('col', 'row')
- grad_up_gate: float32 [2048, 2, 8192], P('row', None, 'col')
- grad_down: float32 [8192, 2048], P('col', 'row')
Inputs may be any that keep to these rules, and one draw needn't show every extreme that they name: prefix_len gives, for each sequence, how many of its first tokens attend to each other in both directions.
All inputs are finite; a program needn't handle non-finite values.
Results may differ from a plain program's by a relative error of at most 0.014.
Values may be sent and summed in bfloat16 or wider, within the bound.
A program may use at most 192 MiB of HBM per device.

v0:
```python
import jax
import jax.numpy as jnp
from jax import lax
from jax.sharding import PartitionSpec as P

QBLOCK = 512


EPSILON = 1e-05
NEGATIVE = -1e30


def full_norm(values):
    center = values - jnp.mean(values, axis=-1, keepdims=True)
    inv_std = lax.rsqrt(jnp.mean(center * center, axis=-1, keepdims=True) + EPSILON)
    return (center * inv_std, inv_std)


def norm_back(grad_in, normed, inv_std, grad_total, cross_total, model_width):
    return inv_std * (grad_in - grad_total / model_width - normed * (cross_total / model_width))


def scatter_norm_back(partial_value, normed_part, inv_std, model_width):
    grad_part = lax.psum_scatter(partial_value, "col", scatter_dimension=1, tiled=True)
    grad_total, cross_total = lax.psum(
        (
            jnp.sum(grad_part, axis=1, keepdims=True),
            jnp.sum(grad_part * normed_part, axis=1, keepdims=True),
        ),
        "col",
    )
    return norm_back(grad_part, normed_part, inv_std, grad_total, cross_total, model_width)


def rope_tables(count, seq_len, head_dim):
    positions = (jnp.arange(count, dtype=jnp.int32) % seq_len).astype(jnp.float32)
    frequency = 10000.0 ** (-(jnp.arange(head_dim // 2).astype(jnp.float32) * 2.0 / head_dim))
    angles = positions[:, None] * frequency[None, :]
    return (jnp.cos(angles)[:, None, :], jnp.sin(angles)[:, None, :])


def rotate(values, cosine_table, sine_table):
    half_dim = values.shape[-1] // 2
    first_half = values[..., :half_dim]
    second_half = values[..., half_dim:]
    return jnp.concatenate(
        [
            first_half * cosine_table - second_half * sine_table,
            second_half * cosine_table + first_half * sine_table,
        ],
        axis=-1,
    )


def score_block(query_block, key_rot, first_row, prefix_one):
    score_scale = query_block.shape[-1] ** (-0.5)
    scores = (
        jnp.einsum("qhe,khe->hqk", query_block, key_rot, preferred_element_type=jnp.float32)
        * score_scale
    )
    key_pos = jnp.arange(key_rot.shape[0], dtype=jnp.int32)
    query_pos = first_row + jnp.arange(query_block.shape[0], dtype=jnp.int32)
    allowed = (key_pos[None, :] <= query_pos[:, None]) | (key_pos[None, :] < prefix_one)
    return jnp.where(allowed[None], scores, NEGATIVE)


def attend_forward(query_rot, key_rot, value_rows, prefix_one):

    def block_fn(block_index):
        first_row = block_index * QBLOCK
        query_block = lax.dynamic_slice_in_dim(query_rot, first_row, QBLOCK, 0)
        scores = score_block(query_block, key_rot, first_row, prefix_one)
        row_top = jnp.max(scores, axis=-1, keepdims=True)
        exp_scores = jnp.exp(scores - row_top)
        row_total = jnp.sum(exp_scores, axis=-1, keepdims=True)
        prob_low = (exp_scores / row_total).astype(jnp.bfloat16)
        mixed_block = jnp.einsum(
            "hqk,khe->qhe", prob_low, value_rows, preferred_element_type=jnp.float32
        )
        return (mixed_block, (row_top + jnp.log(row_total))[..., 0])

    mixed_rows, log_total = lax.map(
        block_fn, jnp.arange(query_rot.shape[0] // QBLOCK, dtype=jnp.int32)
    )
    return (mixed_rows.reshape(query_rot.shape), log_total)


def attend_backward(query_rot, key_rot, value_rows, prefix_one, grad_mixed, log_total):
    score_scale = query_rot.shape[-1] ** (-0.5)

    def scan_step(carried, block_index):
        grad_keys, grad_values = carried
        first_row = block_index * QBLOCK
        query_block = lax.dynamic_slice_in_dim(query_rot, first_row, QBLOCK, 0)
        grad_block = lax.dynamic_slice_in_dim(grad_mixed, first_row, QBLOCK, 0)
        scores = score_block(query_block, key_rot, first_row, prefix_one)
        prob_rows = jnp.exp(scores - log_total[block_index][..., None])
        grad_probs = jnp.einsum(
            "qhe,khe->hqk", grad_block, value_rows, preferred_element_type=jnp.float32
        )
        grad_values = grad_values + jnp.einsum(
            "hqk,qhe->khe",
            prob_rows.astype(jnp.bfloat16),
            grad_block,
            preferred_element_type=jnp.float32,
        )
        inner_sum = jnp.sum(prob_rows * grad_probs, axis=-1, keepdims=True)
        grad_scores = (prob_rows * (grad_probs - inner_sum)).astype(jnp.bfloat16)
        grad_query = (
            jnp.einsum("hqk,khe->qhe", grad_scores, key_rot, preferred_element_type=jnp.float32)
            * score_scale
        )
        grad_keys = (
            grad_keys
            + jnp.einsum(
                "hqk,qhe->khe", grad_scores, query_block, preferred_element_type=jnp.float32
            )
            * score_scale
        )
        return ((grad_keys, grad_values), grad_query)

    zero_rows = jnp.zeros(key_rot.shape, jnp.float32)
    (grad_keys, grad_values), grad_query = lax.scan(
        scan_step, (zero_rows, zero_rows), jnp.arange(query_rot.shape[0] // QBLOCK, dtype=jnp.int32)
    )
    return (grad_query.reshape(query_rot.shape), grad_keys, grad_values)


def local(inputs, prefix_len, w_qkv, w_out, w_up_gate, w_down, cotangent):
    col_width = inputs.shape[1]
    col_start = lax.axis_index("col") * col_width
    tokens = inputs.shape[0]
    seq_count = prefix_len.shape[0]
    seq_len = tokens // seq_count
    local_heads = w_qkv.shape[1]
    head_dim = w_qkv.shape[2] // 3
    full_in = lax.all_gather(inputs, "col", axis=1, tiled=True)
    qkv_all, out_all, up_all, down_all = (
        lax.all_gather(w_qkv, "row", axis=0, tiled=True),
        lax.all_gather(w_out, "row", axis=1, tiled=True),
        lax.all_gather(w_up_gate, "row", axis=0, tiled=True),
        lax.all_gather(w_down, "row", axis=1, tiled=True),
    )
    model_width = full_in.shape[1]
    normed_one, inv_one = full_norm(full_in.astype(jnp.float32))
    normed_in = normed_one.astype(jnp.bfloat16)
    qkv_rows = jnp.einsum("td,dhe->the", normed_in, qkv_all, preferred_element_type=jnp.float32)
    cosine_table, sine_table = rope_tables(tokens, seq_len, head_dim)
    query_rot = rotate(qkv_rows[..., :head_dim], cosine_table, sine_table).astype(jnp.bfloat16)
    key_rot = rotate(qkv_rows[..., head_dim : 2 * head_dim], cosine_table, sine_table).astype(
        jnp.bfloat16
    )
    value_rows = qkv_rows[..., 2 * head_dim :].astype(jnp.bfloat16)
    shaped = (seq_count, seq_len, local_heads, head_dim)
    per_seq = (
        query_rot.reshape(shaped),
        key_rot.reshape(shaped),
        value_rows.reshape(shaped),
        prefix_len,
    )
    mixed_seq, log_total = lax.map(
        lambda packed: attend_forward(packed[0], packed[1], packed[2], packed[3]), per_seq
    )
    mixed_rows = mixed_seq.reshape(tokens, local_heads * head_dim).astype(jnp.bfloat16)
    branch_part = jnp.dot(mixed_rows, out_all, preferred_element_type=jnp.float32)
    branch = lax.psum_scatter(branch_part, "col", scatter_dimension=1, tiled=True)
    middle = inputs.astype(jnp.float32) + branch
    first_total, square_total = lax.psum(
        (jnp.sum(middle, axis=1, keepdims=True), jnp.sum(middle * middle, axis=1, keepdims=True)),
        "col",
    )
    mean_mid = first_total / model_width
    inv_two = lax.rsqrt(square_total / model_width - mean_mid * mean_mid + EPSILON)
    normed_two = (middle - mean_mid) * inv_two
    normed_mid = lax.all_gather(normed_two.astype(jnp.bfloat16), "col", axis=1, tiled=True)
    gate_up = jnp.einsum("td,dkf->tkf", normed_mid, up_all, preferred_element_type=jnp.float32)
    gate_rows = gate_up[:, 0]
    up_rows = gate_up[:, 1]
    sigmoid_gate = jax.nn.sigmoid(gate_rows)
    active = gate_rows * sigmoid_gate
    hidden = (active * up_rows).astype(jnp.bfloat16)
    down_part = jnp.dot(hidden, down_all, preferred_element_type=jnp.float32)
    outputs = (middle + lax.psum_scatter(down_part, "col", scatter_dimension=1, tiled=True)).astype(
        jnp.bfloat16
    )
    cot_full = lax.all_gather(cotangent, "col", axis=1, tiled=True)
    grad_hidden = jnp.einsum("td,fd->tf", cot_full, down_all, preferred_element_type=jnp.float32)
    grad_down = jnp.einsum("tf,td->fd", hidden, cot_full, preferred_element_type=jnp.float32)
    grad_gate = grad_hidden * up_rows * sigmoid_gate * (1.0 + gate_rows * (1.0 - sigmoid_gate))
    grad_upper = grad_hidden * active
    grad_gate_up = jnp.stack([grad_gate, grad_upper], axis=1).astype(jnp.bfloat16)
    grad_up_gate = jnp.einsum(
        "td,tkf->dkf", normed_mid, grad_gate_up, preferred_element_type=jnp.float32
    )
    mid_part = jnp.einsum("tkf,dkf->td", grad_gate_up, up_all, preferred_element_type=jnp.float32)
    grad_middle = cotangent.astype(jnp.float32) + scatter_norm_back(
        mid_part, normed_two, inv_two, model_width
    )
    grad_branch = lax.all_gather(grad_middle.astype(jnp.bfloat16), "col", axis=1, tiled=True)
    grad_out = jnp.einsum("tc,td->cd", mixed_rows, grad_branch, preferred_element_type=jnp.float32)
    grad_mixed = (
        jnp.einsum("td,cd->tc", grad_branch, out_all, preferred_element_type=jnp.float32)
        .astype(jnp.bfloat16)
        .reshape(shaped)
    )
    per_back = (per_seq[0], per_seq[1], per_seq[2], per_seq[3], grad_mixed, log_total)
    grad_query, grad_key, grad_value = lax.map(
        lambda packed: attend_backward(
            packed[0], packed[1], packed[2], packed[3], packed[4], packed[5]
        ),
        per_back,
    )
    flat_shape = (tokens, local_heads, head_dim)
    grad_qkv_rows = jnp.concatenate(
        [
            rotate(grad_query.reshape(flat_shape), cosine_table, -sine_table),
            rotate(grad_key.reshape(flat_shape), cosine_table, -sine_table),
            grad_value.reshape(flat_shape),
        ],
        axis=-1,
    ).astype(jnp.bfloat16)
    grad_qkv = jnp.einsum(
        "td,the->dhe", normed_in, grad_qkv_rows, preferred_element_type=jnp.float32
    )
    in_part = jnp.einsum("the,dhe->td", grad_qkv_rows, qkv_all, preferred_element_type=jnp.float32)
    normed_part = lax.dynamic_slice_in_dim(normed_one, col_start, col_width, 1)
    input_grad = grad_middle + scatter_norm_back(in_part, normed_part, inv_one, model_width)
    reduced = (
        lax.psum_scatter(grad_qkv, "row", scatter_dimension=0, tiled=True),
        lax.psum_scatter(grad_out, "row", scatter_dimension=1, tiled=True),
        lax.psum_scatter(grad_up_gate, "row", scatter_dimension=0, tiled=True),
        lax.psum_scatter(grad_down, "row", scatter_dimension=1, tiled=True),
    )
    return (outputs, input_grad, reduced[0], reduced[1], reduced[2], reduced[3])


def solution(mesh):
    placed = (
        P("row", "col"),
        P("row"),
        P("row", "col", None),
        P("col", "row"),
        P("row", None, "col"),
        P("col", "row"),
        P("row", "col"),
    )
    return jax.shard_map(
        local,
        mesh=mesh,
        in_specs=placed,
        out_specs=(
            P("row", "col"),
            P("row", "col"),
            P("row", "col", None),
            P("col", "row"),
            P("row", None, "col"),
            P("col", "row"),
        ),
        check_vma=False,
    )
```

profile of v0, /device:TPU:1, one launch (start us, length us, event | category | flops | bytes accessed | tf_op | source)
XLA Modules:
  0.0 2318.2 jit_solution(7709503608468907431)
XLA Ops:
  14.6 122.5 %all-gather.9.cloned.1.call-done = bf16[2048,2048]{1,0:T(8,128)(2,1)} async-done(((bf16[2048,256]{1,0:T(8,128)(2,1)}), bf16[2048,2048]{1,0:T(8,128)(2,1)}) %all-gather.9.cloned.1.call-update) | async-done | bytes 8388624 | tf_op jit(solution)/shard_map/all_gather | solution.py:137
  145.2 21.6 all-gather.11.cloned.1.call-done
  166.9 10.4 fusion.46
  181.0 51.1 %while.47 = (s32[]{:T(128)}, bf16[4,512,2,128]{3,1,2,0:T(8,128)(2,1)}, f32[4,2,512]{2,1,0:T(2,128)}, s32[4]{0:T(128)S(1)}, s32[]{:T(128)}, /*index=5*/bf16[2048,...) while((s32[]{:T(128)}, ...), condition=%wide.region_5.6_spmd, body=%wide.region_2.5_spmd.sunk | while | flops 1101006336 | bytes 40674036 | solution.py:82
  248.6 278.9 %reduce-scatter.9.cloned.1.call-done = f32[2048,256]{1,0:T(8,128)} async-done(((f32[2048,2048]{1,0:T(8,128)}), f32[2048,256]{1,0:T(8,128)}) %reduce-scatter.9.cloned.1.call-update) | async-done | bytes 2097168 | tf_op jit(solution)/shard_map/reduce_scatter | solution.py:166
  529.7 28.2 %all-reduce.2 = (f32[2048,1]{0,1:T(1,128)S(1)}, f32[2048,1]{0,1:T(1,128)S(1)}) all-reduce(f32[2048,1]{0,1:T(1,128)S(1)} %bitcast.154, f32[2048,1]{0,1:T(1,128)S(1)} %bitcast.153), channel_id=1, replica_groups=mesh['row'=4,'col'=8] {'col'}, use_global_device_ids=true, to_apply=%region_10.11 | all-reduce | flops 4096 | bytes 32768 | tf_op jit(solution)/shard_map/psum | solution.py:168
  561.0 26.3 %all-gather.17.cloned.1.call-done = bf16[2048,2,1024]{2,0,1:T(8,128)(2,1)} async-done(((bf16[512,2,1024]{2,0,1:T(8,128)(2,1)}), bf16[2048,2,1024]{2,0,1:T(8,128)(2,1)}) %all-gather.17.cloned.1.call-update) | async-done | bytes 8388624 | tf_op jit(solution)/shard_map/all_gather | solution.py:141
  587.3 127.2 %all-gather.15.cloned.1.call-done = bf16[2048,2048]{1,0:T(8,128)(2,1)} async-done(((bf16[2048,256]{1,0:T(8,128)(2,1)}), bf16[2048,2048]{1,0:T(8,128)(2,1)}) %all-gather.15.cloned.1.call-update) | async-done | bytes 8388624 | tf_op jit(solution)/shard_map/all_gather | solution.py:175
  714.5 24.4 %fusion.42 = f32[2048,2,1024]{2,0,1:T(8,128)} fusion(bf16[2048,2,1024]{2,0,1:T(8,128)(2,1)} %all-gather.17.cloned.1.call-done, bf16[2048,2048]{1,0:T(8,128)(2,1)} %all-gather.15.cloned.1.call-done), kind=kOutput, calls=%fused_computation.60 | convolution fusion | flops 17179869184 | bytes 33554432 | tf_op jit(solution)/shard_map/td,dkf->tkf/dot_general | solution.py:176
  738.9 10.8 all-gather.19.cloned.1.call-done
  749.7 126.8 %all-gather.21.cloned.1.call-done = bf16[2048,2048]{1,0:T(8,128)(2,1)} async-done(((bf16[2048,256]{1,0:T(8,128)(2,1)}), bf16[2048,2048]{1,0:T(8,128)(2,1)}) %all-gather.21.cloned.1.call-update) | async-done | bytes 8388624 | tf_op jit(solution)/shard_map/all_gather | solution.py:186
  876.5 23.6 %fusion.52 = (bf16[2048,1,1024]{2,0,1:T(8,128)(2,1)}, bf16[2048,1,1024]{2,0,1:T(8,128)(2,1)}, bf16[2048,1024]{1,0:T(8,128)(2,1)}) fusion(f32[2048,2,1024]{2,0,1:T(8,128)} %fusion.42, bf16[2048,2048]{1,0:T(8,128)(2,1)} %all-gather.21.cloned.1.call-done, bf16[1024,2048]{1,0:T(8,128)(2,1)} %all-gather.19.cloned.1.call-done), kind=kOutput, calls=%fused_computation.74 | convolution fusion | flops 8621391872 | bytes 41943040 | tf_op jit(solution)/shard_map/td,fd->tf/dot_general | solution.py:187
  900.1 24.6 %convolution_bitcast_fusion.1 = f32[2048,2048]{1,0:T(8,128)} fusion(bf16[2048,2,1024]{2,0,1:T(8,128)(2,1)} %all-gather.17.cloned.1.call-done, bf16[2048,1,1024]{2,0,1:T(8,128)(2,1)} %get-tuple-element.308, bf16[2048,1,1024]{2,0,1:T(8,128)(2,1)} %get-tuple-element.307), kind=kOutput, calls=%fused_computation.54 | convolution fusion | flops 17184063488 | bytes 33554432 | tf_op jit(solution)/shard_map/tkf,dkf->td/dot_general | solution.py:195
  924.7 15.1 fusion.73
  939.9 266.4 %reduce-scatter.13.cloned.1.call-done = f32[2048,256]{1,0:T(8,128)} async-done(((f32[2048,2048]{1,0:T(8,128)}), f32[2048,256]{1,0:T(8,128)}) %reduce-scatter.13.cloned.1.call-update) | async-done | bytes 2097168 | tf_op jit(solution)/shard_map/reduce_scatter | solution.py:24
  1208.9 29.8 %all-reduce.1 = (f32[2048,1]{0,1:T(1,128)S(1)}, f32[2048,1]{0,1:T(1,128)S(1)}) all-reduce(f32[2048,1]{0,1:T(1,128)S(1)} %bitcast.156, f32[2048,1]{0,1:T(1,128)S(1)} %bitcast.155), channel_id=1, replica_groups=mesh['row'=4,'col'=8] {'col'}, use_global_device_ids=true, to_apply=%region_16.17 | all-reduce | flops 4096 | bytes 32768 | tf_op jit(solution)/shard_map/psum | solution.py:25
  1238.7 253.5 %reduce-scatter.11.cloned.1.call-done = f32[2048,256]{1,0:T(8,128)} async-done(((f32[2048,2048]{1,0:T(8,128)}), f32[2048,256]{1,0:T(8,128)}) %reduce-scatter.11.cloned.1.call-update) | async-done | bytes 2097168 | tf_op jit(solution)/shard_map/reduce_scatter | solution.py:183
  1498.1 24.8 %fusion.40 = f32[2048,2,1024]{2,0,1:T(8,128)} fusion(bf16[2048,2048]{1,0:T(8,128)(2,1)} %all-gather.15.cloned.1.call-done, bf16[2048,1,1024]{2,0,1:T(8,128)(2,1)} %get-tuple-element.308, bf16[2048,1,1024]{2,0,1:T(8,128)(2,1)} %get-tuple-element.307), kind=kOutput, calls=%fused_computation.58 | convolution fusion | flops 17196646400 | bytes 33554432 | tf_op jit(solution)/shard_map/td,tkf->dkf/dot_general | solution.py:192
  1523.1 99.1 %all-gather.23.cloned.1.call-done = bf16[2048,2048]{1,0:T(8,128)(2,1)} async-done(((bf16[2048,256]{1,0:T(8,128)(2,1)}), bf16[2048,2048]{1,0:T(8,128)(2,1)}) %all-gather.23.cloned.1.call-update) | async-done | bytes 8388624 | tf_op jit(solution)/shard_map/all_gather | solution.py:199
  1628.9 194.9 %while.48 = (s32[]{:T(128)}, f32[2048,2,128]{0,2,1:T(8,128)}, f32[2048,2,128]{0,2,1:T(8,128)}, f32[4,512,2,128]{1,0,3,2:T(4,128)}, s32[4]{0:T(128)S(1)}, /*index...) while((s32[]{:T(128)}, f32[2048,2,128]{0,2,1:T(8,128)}, ...), condition=%wide.region_19.20_spmd.clone, body=%wide.region_17.19_spmd.clone.sunk | while | flops 2720663040 | bytes 128487816 | solution.py:123
  1656.4 11.2 dynamic_update_slice.31
  1703.1 11.1 dynamic_update_slice.31
  1751.4 11.1 dynamic_update_slice.31
  1799.3 11.1 dynamic_update_slice.31
  1845.7 12.8 fusion.44
  1860.4 12.4 convolution_bitcast_fusion
  1872.9 14.6 fusion.74
  1896.0 10.9 fusion.37
  1919.7 283.1 %reduce-scatter.15.cloned.1.call-done = f32[2048,256]{1,0:T(8,128)} async-done(((f32[2048,2048]{1,0:T(8,128)}), f32[2048,256]{1,0:T(8,128)}) %reduce-scatter.15.cloned.1.call-update) | async-done | bytes 2097168 | tf_op jit(solution)/shard_map/reduce_scatter | solution.py:24
  2205.7 28.2 %all-reduce = (f32[2048,1]{0,1:T(1,128)S(1)}, f32[2048,1]{0,1:T(1,128)S(1)}) all-reduce(f32[2048,1]{0,1:T(1,128)S(1)} %bitcast.158, f32[2048,1]{0,1:T(1,128)S(1)} %bitcast.157), channel_id=1, replica_groups=mesh['row'=4,'col'=8] {'col'}, use_global_device_ids=true, to_apply=%region_24.25 | all-reduce | flops 4096 | bytes 32768 | tf_op jit(solution)/shard_map/psum | solution.py:25
  2237.6 39.0 %reduce-scatter.23.cloned.1.call-done = f32[1024,512]{1,0:T(8,128)} async-done(((f32[1024,2048]{1,0:T(8,128)}), f32[1024,512]{1,0:T(8,128)}) %reduce-scatter.23.cloned.1.call-update) | async-done | bytes 2097168 | tf_op jit(solution)/shard_map/reduce_scatter | solution.py:232
  2276.6 34.6 %reduce-scatter.19.cloned.1.call-done = f32[256,512]{1,0:T(8,128)} async-done(((f32[256,2048]{1,0:T(8,128)}), f32[256,512]{1,0:T(8,128)}) %reduce-scatter.19.cloned.1.call-update) | async-done | bytes 524304 | tf_op jit(solution)/shard_map/reduce_scatter | solution.py:230
  (250 shorter events, 294.7 us)
Async XLA Ops:
  7.2 129.9 %all-gather.9.cloned.1.call-start = ((), (), s32[]{:S(2)}) async-start(), calls=%async_computation.8 | async-start | bytes 9437184 | tf_op jit(solution)/shard_map/all_gather | solution.py:137
  7.9 159.0 %all-gather.11.cloned.1.call-start = ((), (), s32[]{:S(2)}) async-start(), calls=%async_computation.9 | async-start | bytes 3932160 | tf_op jit(solution)/shard_map/all_gather | solution.py:139
  11.0 224.3 %all-gather.13.cloned.1.call-start = ((), (), s32[]{:S(2)}) async-start(), calls=%async_computation.10 | async-start | bytes 1310720 | tf_op jit(solution)/shard_map/all_gather | solution.py:140
  11.7 515.7 %reduce-scatter.9.cloned.1.call-start = ((), (), s32[]{:S(2)}) async-start(), calls=%async_computation.11 | async-start | bytes 18874368 | tf_op jit(solution)/shard_map/reduce_scatter | solution.py:166
  14.6 162.9 %copy-start.10 = (f32[2048,64]{0,1:T(8,128)}, f32[2048,64]{0,1:T(8,128)S(1)}, u32[]{:S(2)}) copy-start(f32[2048,64]{0,1:T(8,128)S(1)} %get-tuple-element.323) | copy-start | bytes 1572868
  142.9 34.4 %copy-start.20 = (f32[2048]{0:T(1024)}, f32[2048]{0:T(1024)S(1)}, u32[]{:S(2)}) copy-start(f32[2048]{0:T(1024)S(1)} %broadcast_multiply_fusion.5) | copy-start | bytes 24580
  145.2 32.1 %copy-start.18 = (f32[2048]{0:T(1024)}, f32[2048]{0:T(1024)S(1)}, u32[]{:S(2)}) copy-start(f32[2048]{0:T(1024)S(1)} %add_rsqrt_fusion.1) | copy-start | bytes 24580
  232.2 12.8 copy-start.1
  232.2 12.8 copy-start.4
  235.2 9.7 copy-start.7
  245.0 282.5 %copy-start.11 = (bf16[2048,256]{1,0:T(8,128)(2,1)S(1)}, bf16[2048,256]{1,0:T(8,128)(2,1)}, u32[]{:S(2)}) copy-start(bf16[2048,256]{1,0:T(8,128)(2,1)} %param.11) | copy-start | bytes 3145732
  245.0 342.3 %all-gather.17.cloned.1.call-start = ((), (), s32[]{:S(2)}) async-start(), calls=%async_computation.13 | async-start | bytes 10485760 | tf_op jit(solution)/shard_map/all_gather | solution.py:141
  248.5 466.0 %all-gather.15.cloned.1.call-start = ((), (), s32[]{:S(2)}) async-start(), calls=%async_computation.12 | async-start | bytes 9437184 | tf_op jit(solution)/shard_map/all_gather | solution.py:175
  559.5 190.2 %all-gather.19.cloned.1.call-start = ((), (), s32[]{:S(2)}) async-start(), calls=%async_computation.14 | async-start | bytes 5242880 | tf_op jit(solution)/shard_map/all_gather | solution.py:142
  560.2 316.3 %all-gather.21.cloned.1.call-start = ((), (), s32[]{:S(2)}) async-start(), calls=%async_computation.16 | async-start | bytes 9437184 | tf_op jit(solution)/shard_map/all_gather | solution.py:186
  561.0 645.4 %reduce-scatter.13.cloned.1.call-start = ((), (), s32[]{:S(2)}) async-start(), calls=%async_computation.17 | async-start | bytes 18874368 | tf_op jit(solution)/shard_map/reduce_scatter | solution.py:24
  924.7 567.5 %reduce-scatter.11.cloned.1.call-start = ((), (), s32[]{:S(2)}) async-start(), calls=%async_computation.15 | async-start | bytes 18874368 | tf_op jit(solution)/shard_map/reduce_scatter | solution.py:183
  939.9 552.4 %copy-start.12 = (bf16[2048,256]{1,0:T(8,128)(2,1)S(1)}, bf16[2048,256]{1,0:T(8,128)(2,1)}, u32[]{:S(2)}) copy-start(bf16[2048,256]{1,0:T(8,128)(2,1)} %param.17) | copy-start | bytes 3145732
  939.9 682.3 %all-gather.23.cloned.1.call-start = ((), (), s32[]{:S(2)}) async-start(), calls=%async_computation.18 | async-start | bytes 9437184 | tf_op jit(solution)/shard_map/all_gather | solution.py:199
  1498.1 408.8 %reduce-scatter.21.cloned.1.call-start = ((), (), s32[]{:S(2)}) async-start(), calls=%async_computation.22 | async-start | bytes 20971520 | tf_op jit(solution)/shard_map/reduce_scatter | solution.py:231
  1523.0 99.2 %copy-start.15 = (bf16[256,2048]{1,0:T(8,128)(2,1)S(1)}, bf16[256,2048]{1,0:T(8,128)(2,1)}, u32[]{:S(2)}) copy-start(bf16[256,2048]{1,0:T(8,128)(2,1)} %all-gather.13.cloned.1.call-done) | copy-start | bytes 3145732
  1523.0 392.9 %reduce-scatter.17.cloned.1.call-start = ((), (), s32[]{:S(2)}) async-start(), calls=%async_computation.20 | async-start | bytes 7864320 | tf_op jit(solution)/shard_map/reduce_scatter | solution.py:229
  1523.1 105.8 %copy-start.2 = (bf16[2048,2,128]{2,0,1:T(8,128)(2,1)S(1)}, bf16[2048,2,128]{2,0,1:T(8,128)(2,1)}, u32[]{:S(2)}) copy-start(bf16[2048,2,128]{2,0,1:T(8,128)(2,1)} %copy-done.1) | copy-start | bytes 3145732
  1523.1 105.8 %copy-start.5 = (bf16[2048,2,128]{2,0,1:T(8,128)(2,1)S(1)}, bf16[2048,2,128]{2,0,1:T(8,128)(2,1)}, u32[]{:S(2)}) copy-start(bf16[2048,2,128]{2,0,1:T(8,128)(2,1)} %copy-done.4) | copy-start | bytes 3145732
  1640.8 9.4 slice-start
  1641.5 8.6 slice-start.1
  1834.8 10.9 copy-start.19
  1834.8 10.9 copy-start.21
  1858.5 344.3 %reduce-scatter.15.cloned.1.call-start = ((), (), s32[]{:S(2)}) async-start(), calls=%async_computation.19 | async-start | bytes 18874368 | tf_op jit(solution)/shard_map/reduce_scatter | solution.py:24
  1872.8 403.8 %reduce-scatter.23.cloned.1.call-start = ((), (), s32[]{:S(2)}) async-start(), calls=%async_computation.23 | async-start | bytes 10485760 | tf_op jit(solution)/shard_map/reduce_scatter | solution.py:232
  1887.5 423.7 %reduce-scatter.19.cloned.1.call-start = ((), (), s32[]{:S(2)}) async-start(), calls=%async_computation.21 | async-start | bytes 2621440 | tf_op jit(solution)/shard_map/reduce_scatter | solution.py:230
  1906.9 327.0 %copy-start.9 = (f32[2048,256]{1,0:T(8,128)S(1)}, f32[2048,256]{1,0:T(8,128)}, u32[]{:S(2)}) copy-start(f32[2048,256]{1,0:T(8,128)} %get-tuple-element.301) | copy-start | bytes 6291460
  (26 other events, 107.2 us)
Sparse Core Ops, SparseCore 0:
  10.0 127.0 all-gather.8
  139.2 27.5 all-gather.10
  168.4 16.7 all-gather.12
  245.1 282.2 reduce-scatter.8
  529.5 57.7 all-gather.16
  589.9 124.4 all-gather.14
  716.1 33.5 all-gather.18
  751.9 124.5 all-gather.20
  924.8 281.4 reduce-scatter.12
  1210.0 282.1 reduce-scatter.10
  1498.2 123.9 all-gather.22
  1624.8 124.7 reduce-scatter.20
  1858.6 57.2 reduce-scatter.16
  1920.1 282.7 reduce-scatter.14
  2205.8 70.7 reduce-scatter.22
  2279.7 31.4 reduce-scatter.18
where the time goes:
time: 2330 us; the launch traced here: 2320 us
  waiting for transfers between devices  1690 us (73%)
  matrix products  319 us (14%)
  local copies, waits for them, and re-layouts  111 us (5%)
  blocking collectives  86.2 us (4%)
  other arithmetic  77.8 us (3%)
    reduce_scatter x2, waiting for transfers between devices, scatter_norm_back(): lax.psum_scatter(partial_value, 'col', scatter_dimension=1, tiled=True)  550 us
    reduce_scatter x1, waiting for transfers between devices, local(): lax.psum_scatter(branch_part, 'col', scatter_dimension=1, tiled=True)  279 us
    reduce_scatter x1, waiting for transfers between devices, local(): lax.psum_scatter(down_part, 'col', scatter_dimension=1, tiled=True)  254 us
    all_gather x1, waiting for transfers between devices, local(): lax.all_gather(normed_two.astype(jnp.bfloat16), 'col', axis=1, tiled=True)  127 us
    all_gather x1, waiting for transfers between devices, local(): cot_full = lax.all_gather(cotangent, 'col', axis=1, tiled=True)  127 us
    all_gather x1, waiting for transfers between devices, local(): full_in = lax.all_gather(inputs, 'col', axis=1, tiled=True)  123 us
    all_gather x1, waiting for transfers between devices, local(): lax.all_gather(grad_middle.astype(jnp.bfloat16), 'col', axis=1, tiled=True)  99.1 us
    psum x2, blocking collectives, scatter_norm_back(): lax.psum((jnp.sum(grad_part, axis=1, keepdims=True), jnp.sum(grad_part *...  58 us
  transfers between devices with their start and end apart: 16, of which 14 were waited for; matrix products, arithmetic and copies ran while one was open for 18% of the time, Pallas kernels for 0%

commit v1 on v0

v1 whole, which is shorter than its diff:
```python
import functools

import jax
import jax.numpy as jnp
from jax import lax
from jax.experimental import pallas as pl
from jax.experimental.pallas import tpu as pltpu
from jax.sharding import Mesh
from jax.sharding import PartitionSpec as P

EPSILON = 1e-05
NEG = -1e30
F32 = jnp.float32
BF = jnp.bfloat16
NN = (((1,), (0,)), ((), ()))
NT = (((1,), (1,)), ((), ()))
TN = (((0,), (0,)), ((), ()))
def dot(a, b, dims):
    return lax.dot_general(a, b, dims, preferred_element_type=F32)

def fwd_kernel(prefix_ref, q_ref, k_ref, v_ref, o_ref, lse_ref, *, bq, bk, scale):
    i = pl.program_id(1)
    first = i * bq
    prefix = prefix_ref[0]
    q = q_ref[...]
    limit = jnp.maximum(first + bq, prefix)
    total = (limit + bk - 1) // bk
    clear = jnp.maximum(first, prefix) // bk
    def step(masked, j, carry):
        top, tot, acc = carry
        rows = pl.ds(pl.multiple_of(j * bk, bk), bk)
        s = dot(q, k_ref[rows, :], NT) * scale
        if masked:
            kp = j * bk + lax.broadcasted_iota(jnp.int32, (bq, bk), 1)
            qp = first + lax.broadcasted_iota(jnp.int32, (bq, bk), 0)
            s = jnp.where(kp < jnp.maximum(qp + 1, prefix), s, NEG)
        new = jnp.maximum(top, jnp.max(s, axis=1, keepdims=True))
        alpha = jnp.exp(top - new)
        p = jnp.exp(s - new)
        tot = tot * alpha + jnp.sum(p, axis=1, keepdims=True)
        acc = acc * alpha + dot(p.astype(BF), v_ref[rows, :], NN)
        return new, tot, acc
    carry = (jnp.full((bq, 1), NEG, F32), jnp.zeros((bq, 1), F32), jnp.zeros((bq, q.shape[1]), F32))
    carry = lax.fori_loop(0, clear, functools.partial(step, False), carry)
    top, tot, acc = lax.fori_loop(clear, total, functools.partial(step, True), carry)
    o_ref[...] = (acc / tot).astype(o_ref.dtype)
    lse = jnp.broadcast_to(top + jnp.log(tot), (bq, 128))
    lse_ref[0] = lse.T[0:8, :]

def attend_fwd(qkv, prefix, heads, *, bq=512, bk=512, hd=128):
    seq = qkv.shape[0]
    return pl.pallas_call(
        functools.partial(fwd_kernel, bq=bq, bk=bk, scale=hd ** -0.5),
        grid_spec=pltpu.PrefetchScalarGridSpec(
            num_scalar_prefetch=1, grid=(heads, seq // bq),
            in_specs=[pl.BlockSpec((bq, hd), lambda h, i, p: (i, 3 * h)),
                      pl.BlockSpec((seq, hd), lambda h, i, p: (0, 3 * h + 1)),
                      pl.BlockSpec((seq, hd), lambda h, i, p: (0, 3 * h + 2))],
            out_specs=[pl.BlockSpec((bq, hd), lambda h, i, p: (i, h)),
                       pl.BlockSpec((1, 8, bq), lambda h, i, p: (h, 0, i))]),
        out_shape=[jax.ShapeDtypeStruct((seq, heads * hd), BF), jax.ShapeDtypeStruct((heads, 8, seq), F32)],
        cost_estimate=pl.CostEstimate(flops=4 * heads * seq * seq * hd, bytes_accessed=8 * heads * seq * hd, transcendentals=heads * seq * seq),
        name="attend_forward",
    )(prefix, qkv, qkv, qkv)

def bwd_kernel(prefix_ref, qkv_ref, o_ref, do_ref, lse_ref, cos_ref, sin_ref, out_ref, dk_ref, dv_ref, delta_ref, *, bq, bk, hd, scale):
    seq = qkv_ref.shape[0]
    prefix = prefix_ref[0]
    dk_ref[...] = jnp.zeros_like(dk_ref)
    dv_ref[...] = jnp.zeros_like(dv_ref)
    def deltas(i, _):
        rows = pl.ds(pl.multiple_of(i * bq, bq), bq)
        prod = (do_ref[rows, :].astype(F32) * o_ref[rows, :].astype(F32)).T
        delta_ref[:, rows] = jnp.broadcast_to(jnp.sum(prod, axis=0, keepdims=True), (8, bq))
        return 0
    lax.fori_loop(0, seq // bq, deltas, 0)
    def unrotate(g, rows):
        cos, sin = cos_ref[rows, :], sin_ref[rows, :]
        half = hd // 2
        a, b = g[:, :half], g[:, half:]
        return jnp.concatenate([a * cos + b * sin, b * cos - a * sin], axis=1)
    def q_step(i, _):
        first = i * bq
        qrows = pl.ds(pl.multiple_of(first, bq), bq)
        q = qkv_ref[qrows, 0:hd]
        do = do_ref[qrows, :]
        lse = lse_ref[0, 0:1, qrows]
        delta = delta_ref[0:1, qrows]
        limit = jnp.maximum(first + bq, prefix)
        total = (limit + bk - 1) // bk
        clear = jnp.maximum(first, prefix) // bk
        def step(masked, j, dq):
            krows = pl.ds(pl.multiple_of(j * bk, bk), bk)
            k = qkv_ref[krows, hd:2 * hd]
            v = qkv_ref[krows, 2 * hd:3 * hd]
            s = dot(k, q, NT) * scale
            p = jnp.exp(s - lse)
            if masked:
                kp = j * bk + lax.broadcasted_iota(jnp.int32, (bk, bq), 0)
                qp = first + lax.broadcasted_iota(jnp.int32, (bk, bq), 1)
                p = jnp.where(kp < jnp.maximum(qp + 1, prefix), p, 0.0)
            dp = dot(v, do, NT)
            dv_ref[krows, :] += dot(p.astype(BF), do, NN)
            ds = (p * (dp - delta)).astype(BF)
            dk_ref[krows, :] += dot(ds, q, NN)
            return dq + dot(ds, k, TN)
        dq = lax.fori_loop(0, clear, functools.partial(step, False), jnp.zeros((bq, hd), F32))
        dq = lax.fori_loop(clear, total, functools.partial(step, True), dq)
        out_ref[qrows, 0:hd] = unrotate(dq * scale, qrows).astype(BF)
        return 0
    lax.fori_loop(0, seq // bq, q_step, 0)
    def fin(i, _):
        rows = pl.ds(pl.multiple_of(i * bq, bq), bq)
        out_ref[rows, hd:2 * hd] = unrotate(dk_ref[rows, :] * scale, rows).astype(BF)
        out_ref[rows, 2 * hd:3 * hd] = dv_ref[rows, :].astype(BF)
        return 0
    lax.fori_loop(0, seq // bq, fin, 0)

def attend_bwd(qkv, mixed, dmixed, lse, prefix, cos, sin, heads, *, bq=512, bk=512, hd=128):
    seq = qkv.shape[0]
    return pl.pallas_call(
        functools.partial(bwd_kernel, bq=bq, bk=bk, hd=hd, scale=hd ** -0.5),
        grid_spec=pltpu.PrefetchScalarGridSpec(
            num_scalar_prefetch=1, grid=(heads,),
            in_specs=[pl.BlockSpec((seq, 3 * hd), lambda h, p: (0, h)),
                      pl.BlockSpec((seq, hd), lambda h, p: (0, h)),
                      pl.BlockSpec((seq, hd), lambda h, p: (0, h)),
                      pl.BlockSpec((1, 8, seq), lambda h, p: (h, 0, 0)),
                      pl.BlockSpec((seq, hd // 2), lambda h, p: (0, 0)),
                      pl.BlockSpec((seq, hd // 2), lambda h, p: (0, 0))],
            out_specs=[pl.BlockSpec((seq, 3 * hd), lambda h, p: (0, h))],
            scratch_shapes=[pltpu.VMEM((seq, hd), F32), pltpu.VMEM((seq, hd), F32), pltpu.VMEM((8, seq), F32)]),
        out_shape=[jax.ShapeDtypeStruct((seq, heads * 3 * hd), BF)],
        cost_estimate=pl.CostEstimate(flops=10 * heads * seq * seq * hd, bytes_accessed=20 * heads * seq * hd, transcendentals=heads * seq * seq),
        name="attend_backward",
    )(prefix, qkv, mixed, dmixed, lse, cos, sin)[0]


def rope_tables(count, head_dim):
    positions = jnp.arange(count, dtype=jnp.int32).astype(F32)
    frequency = 10000.0 ** (-(jnp.arange(head_dim // 2).astype(F32) * 2.0 / head_dim))
    angles = positions[:, None] * frequency[None, :]
    return jnp.cos(angles), jnp.sin(angles)


def rotate(values, cosine, sine):
    half = values.shape[-1] // 2
    a, b = values[..., :half], values[..., half:]
    return jnp.concatenate([a * cosine - b * sine, b * cosine + a * sine], axis=-1)


def norm(values):
    center = values - jnp.mean(values, axis=-1, keepdims=True)
    inv_std = lax.rsqrt(jnp.mean(center * center, axis=-1, keepdims=True) + EPSILON)
    return center * inv_std, inv_std


def norm_back(grad, normed, inv_std):
    mean_grad = jnp.mean(grad, axis=-1, keepdims=True)
    mean_cross = jnp.mean(grad * normed, axis=-1, keepdims=True)
    return inv_std * (grad - mean_grad - normed * mean_cross)


def mm(spec, left, right):
    return jnp.einsum(spec, left, right, preferred_element_type=F32)


def local(swap, inputs, prefix_len, w_qkv, w_out, w_up_gate, w_down, cotangent):
    rows = ("rmaj", "cmin") if swap else ("rmaj", "core")
    cols = ("cmaj", "core") if swap else ("cmaj", "cmin")

    def exchange(value):
        if not swap:
            return value
        return lax.ppermute(value, ("core", "cmin"), [(0, 0), (1, 2), (2, 1), (3, 3)])

    def scatter(value):
        return lax.psum_scatter(value.astype(BF), cols, scatter_dimension=0, tiled=True).astype(F32)

    def spread(value):
        return lax.all_to_all(value, cols, 1, 0, tiled=True)

    prefix_len = exchange(prefix_len)
    inputs, cotangent = exchange(inputs), exchange(cotangent)
    w_qkv, w_out = exchange(w_qkv), exchange(w_out)
    w_up_gate, w_down = exchange(w_up_gate), exchange(w_down)
    tokens = inputs.shape[0]
    heads, head_dim = w_qkv.shape[1], w_qkv.shape[2] // 3
    hidden_width = w_down.shape[0]
    full_in = lax.all_gather(inputs, cols, axis=1, tiled=True)
    width = full_in.shape[1]
    qkv_all = lax.all_gather(w_qkv, rows, axis=0, tiled=True).reshape(width, heads * 3 * head_dim)
    out_all = lax.all_gather(w_out, rows, axis=1, tiled=True)
    up_all = lax.all_gather(w_up_gate, rows, axis=0, tiled=True).reshape(width, 2 * hidden_width)
    down_all = lax.all_gather(w_down, rows, axis=1, tiled=True)
    cot_full = lax.all_gather(cotangent, cols, axis=1, tiled=True)
    piece = tokens // lax.axis_size(cols)
    first = lax.axis_index(cols) * piece
    own_in = lax.dynamic_slice_in_dim(full_in, first, piece, 0).astype(F32)
    own_cot = lax.dynamic_slice_in_dim(cot_full, first, piece, 0).astype(F32)

    normed_in = norm(full_in.astype(F32))[0].astype(BF)
    qkv_rows = mm("td,de->te", normed_in, qkv_all).reshape(tokens, heads, 3, head_dim)
    cosine, sine = rope_tables(tokens, head_dim)
    turned = rotate(qkv_rows[:, :, :2], cosine[:, None, None], sine[:, None, None])
    qkv = jnp.concatenate([turned, qkv_rows[:, :, 2:]], axis=2).astype(BF)
    qkv = qkv.reshape(tokens, heads * 3 * head_dim)
    mixed, lse = attend_fwd(qkv, prefix_len, heads, hd=head_dim)
    middle = own_in + scatter(mm("tc,cd->td", mixed, out_all))
    normed_two, inv_two = norm(middle)
    normed_mid = lax.all_gather(normed_two.astype(BF), cols, axis=0, tiled=True)
    gate_up = mm("td,df->tf", normed_mid, up_all)
    gate, up = gate_up[:, :hidden_width], gate_up[:, hidden_width:]
    sig = jax.nn.sigmoid(gate)
    active = gate * sig
    hidden = (active * up).astype(BF)
    outputs = middle + scatter(mm("tf,fd->td", hidden, down_all))
    outputs = exchange(spread(outputs.astype(BF)))

    grad_hidden = mm("td,fd->tf", cot_full, down_all)
    grad_gate = grad_hidden * up * sig * (1.0 + gate * (1.0 - sig))
    grad_gate_up = jnp.concatenate([grad_gate, grad_hidden * active], axis=1).astype(BF)
    grad_down = mm("tf,td->fd", hidden, cot_full).astype(BF)
    grad_down = lax.psum_scatter(grad_down, rows, scatter_dimension=1, tiled=True)
    grad_up = mm("td,tf->df", normed_mid, grad_gate_up).astype(BF)
    grad_up = lax.psum_scatter(grad_up, rows, scatter_dimension=0, tiled=True)
    grad_normed = scatter(mm("tf,df->td", grad_gate_up, up_all))
    grad_middle = own_cot + norm_back(grad_normed, normed_two, inv_two)
    grad_branch = lax.all_gather(grad_middle.astype(BF), cols, axis=0, tiled=True)
    grad_out = mm("tc,td->cd", mixed, grad_branch).astype(BF)
    grad_out = lax.psum_scatter(grad_out, rows, scatter_dimension=1, tiled=True)
    grad_mixed = mm("td,cd->tc", grad_branch, out_all).astype(BF)
    grad_rows = attend_bwd(qkv, mixed, grad_mixed, lse, prefix_len, cosine, sine, heads, hd=head_dim)
    grad_in = scatter(mm("te,de->td", grad_rows, qkv_all))
    grad_qkv = mm("td,te->de", normed_in, grad_rows).astype(BF)
    grad_qkv = lax.psum_scatter(grad_qkv, rows, scatter_dimension=0, tiled=True)
    normed_own, inv_own = norm(own_in)
    input_grad = grad_middle + norm_back(grad_in, normed_own, inv_own)
    input_grad = exchange(spread(input_grad.astype(BF))).astype(F32)
    return (
        outputs,
        input_grad,
        exchange(grad_qkv).astype(F32).reshape(-1, heads, 3 * head_dim),
        exchange(grad_out).astype(F32),
        exchange(grad_up).astype(F32).reshape(-1, 2, hidden_width),
        exchange(grad_down).astype(F32),
    )


def solution(mesh):
    row_size, col_size = mesh.shape["row"], mesh.shape["col"]
    col_major = 4
    shape = (row_size // 2, 2, col_major, col_size // col_major)
    fine = Mesh(mesh.devices.reshape(shape), ("rmaj", "core", "cmaj", "cmin"))
    row, col = ("rmaj", "core"), ("cmaj", "cmin")
    outs = (P(row, col), P(row, col), P(row, col, None), P(col, row), P(row, None, col), P(col, row))
    return jax.shard_map(
        functools.partial(local, shape[3] == 2),
        mesh=fine,
        in_specs=(P(row, col), P(row), P(row, col, None), P(col, row), P(row, None, col), P(col, row), P(row, col)),
        out_specs=outs,
        check_vma=False,
    )
```

time: 2330 us -> 1370 us (0.59)
  waiting for transfers between devices: 1690 us -> 987 us
  matrix products: 319 us -> 173 us
  blocking collectives: 86.2 us -> 0 us
  local copies, waits for them, and re-layouts: 111 us -> 42.6 us
  starting transfers between devices: 0.9 us -> 57.8 us
  Pallas kernels: 0 us -> 54.4 us
  other arithmetic: 77.8 us -> 37 us
    reduce_scatter x8, waiting for transfers between devices: 1160 us -> 477 us  [the longest x4 261 us: scatter(): lax.psum_scatter(value.astype(BF), cols, scatter_dimension=0, tiled=True)]
    all_gather x8, waiting for transfers between devices: 534 us -> 376 us  [the longest x1 85.1 us: local(): cot_full = lax.all_gather(cotangent, cols, axis=1, tiled=True)]
    dot_general x40 -> x12, matrix products: 319 us -> 173 us  [mm(): return jnp.einsum(spec, left, right, preferred_element_type=F32)]
    ppermute x0 -> x13, waiting for transfers between devices: none -> 135 us  [exchange(): lax.ppermute(value, ('core', 'cmin'), [(0, 0), (1, 2), (2, 1), (3, 3)])]
    psum x3 -> x0, blocking collectives: 86.2 us -> none  [the longest x2 58 us: scatter_norm_back(): lax.psum((jnp.sum(grad_part, axis=1, keepdims=True), jnp.sum(grad_part *...]
    pallas_call x0 -> x2, Pallas kernels: none -> 54.4 us  [the longest x1 32.4 us: attend_bwd(): pl.pallas_call(functools.partial(bwd_kernel, bq=bq, bk=bk, hd=hd, scale=h...]
    dynamic_update_slice x8 -> x0, local copies, waits for them, and re-layouts: 46 us -> none  [attend_forward(): lax.map(block_fn, jnp.arange(query_rot.shape[0] // QBLOCK, dtype=jnp.int32))]
    ppermute x0 -> x13, starting transfers between devices: none -> 42.1 us  [exchange(): lax.ppermute(value, ('core', 'cmin'), [(0, 0), (1, 2), (2, 1), (3, 3)])]
  transfers between devices with their start and end apart: 16 -> 31, of which waited for: 14 -> 21; matrix products, arithmetic and copies ran while one was open for 18% -> 12% of each run, Pallas kernels for 0% -> 2%
where the time goes in v1:
time: 1370 us
  waiting for transfers between devices  987 us (72%)
  matrix products  173 us (13%)
  starting transfers between devices  57.8 us (4%)
  Pallas kernels  54.4 us (4%)
  local copies, waits for them, and re-layouts  42.6 us (3%)
  other arithmetic  37 us (3%)
  between operations  14.6 us (1%)
    reduce_scatter x4, waiting for transfers between devices, scatter(): lax.psum_scatter(value.astype(BF), cols, scatter_dimension=0, tiled=True)  261 us
    dot_general x12, matrix products, mm(): return jnp.einsum(spec, left, right, preferred_element_type=F32)  173 us
    ppermute x13, waiting for transfers between devices, exchange(): lax.ppermute(value, ('core', 'cmin'), [(0, 0), (1, 2), (2, 1), (3, 3)])  135 us
    all_gather x1, waiting for transfers between devices, local(): cot_full = lax.all_gather(cotangent, cols, axis=1, tiled=True)  85.1 us
    all_gather x1, waiting for transfers between devices, local(): lax.all_gather(grad_middle.astype(BF), cols, axis=0, tiled=True)  82.9 us
    all_gather x1, waiting for transfers between devices, local(): full_in = lax.all_gather(inputs, cols, axis=1, tiled=True)  79.3 us
    reduce_scatter x1, waiting for transfers between devices, local(): grad_up = lax.psum_scatter(grad_up, rows, scatter_dimension=0, tiled=True)  72.6 us
    all_gather x1, waiting for transfers between devices, local(): normed_mid = lax.all_gather(normed_two.astype(BF), cols, axis=0, tiled=True)  70.9 us
  transfers between devices with their start and end apart: 31, of which 21 were waited for; matrix products, arithmetic and copies ran while one was open for 12% of the time, Pallas kernels for 2%

profile of v1, /device:TPU:1, one launch (start us, length us, event | category | flops | bytes accessed | tf_op | source)
XLA Modules:
  0.0 1367.0 jit_solution(9635116737712515043)
XLA Ops:
  11.7 9.9 collective-permute-done.2
  26.2 21.2 %collective-permute-done = bf16[2048,256]{1,0:T(8,128)(2,1)S(1)} collective-permute-done((bf16[2048,256]{1,0:T(8,128)(2,1)}, bf16[2048,256]{1,0:T(8,128)(2,1)S(1)}, u32[]{:S(2)}, u32[]{:S(2)}) %collective-permute-start) | collective-permute-done | bytes 1048608 | tf_op jit(solution)/shard_map/ppermute | solution.py:175
  66.8 7.7 all-gather.11.cloned.1.call-done
  80.4 79.3 %all-gather.9.cloned.1.call-done = bf16[2048,2048]{1,0:T(8,128)(2,1)} async-done(((bf16[2048,256]{1,0:T(8,128)(2,1)}), bf16[2048,2048]{1,0:T(8,128)(2,1)}) %all-gather.9.cloned.1.call-update) | async-done | bytes 8388624 | tf_op jit(solution)/shard_map/all_gather | solution.py:190
  178.8 22.0 %attend_forward.1 = (bf16[2048,256]{1,0:T(8,128)(2,1)}, f32[2,8,2048]{2,1,0:T(8,128)}) custom-call(s32[1]{0:T(128)} %collective-permute-done.1.prefix_ref, bf16[2048,768]{1,0:T(8,128)(2,1)} %copy.41.q_ref.k_ref.v_ref.qkv_ref, bf16[2048,768]{1,0:T(8,128)(2,1)} %copy.41.q_ref.k_ref.v_ref.qkv_ref, bf16[2048,768]{1,0:T(8,128)(2,1)} %copy.41.q_ref.k_ref.v_ref.qkv_ref), custom_call_target="tpu_custom_call" | custom-call | flops 4294967296 | bytes 4194304 | tf_op jit(solution)/shard_map/attend_forward/pallas_call | solution.py:52
  209.9 26.0 %collective-permute-done.4 = bf16[512,2,1024]{2,1,0:T(2,128)(2,1)S(1)} collective-permute-done((bf16[512,2,1024]{2,1,0:T(2,128)(2,1)}, bf16[512,2,1024]{2,1,0:T(2,128)(2,1)S(1)}, u32[]{:S(2)}, u32[]{:S(2)}) %collective-permute-start.4) | collective-permute-done | bytes 2097184 | tf_op jit(solution)/shard_map/ppermute | solution.py:175
  237.4 55.9 %reduce-scatter.9.cloned.1.call-done = bf16[256,2048]{1,0:T(8,128)(2,1)} async-done(((bf16[2048,2048]{1,0:T(8,128)(2,1)}), bf16[256,2048]{1,0:T(8,128)(2,1)}) %reduce-scatter.9.cloned.1.call-update) | async-done | bytes 1048592 | tf_op jit(solution)/shard_map/reduce_scatter | solution.py:178
  306.9 35.0 %collective-permute-done.5 = bf16[1024,512]{1,0:T(8,128)(2,1)S(1)} collective-permute-done((bf16[1024,512]{1,0:T(8,128)(2,1)S(1)}, bf16[1024,512]{1,0:T(8,128)(2,1)S(1)}, u32[]{:S(2)}, u32[]{:S(2)}) %collective-permute-start.5) | collective-permute-done | bytes 1048608 | tf_op jit(solution)/shard_map/ppermute | solution.py:175
  345.1 36.9 %collective-permute-done.7 = bf16[2048,256]{1,0:T(8,128)(2,1)S(1)} collective-permute-done((bf16[2048,256]{1,0:T(8,128)(2,1)}, bf16[2048,256]{1,0:T(8,128)(2,1)S(1)}, u32[]{:S(2)}, u32[]{:S(2)}) %collective-permute-start.7) | collective-permute-done | bytes 1048608 | tf_op jit(solution)/shard_map/ppermute | solution.py:175
  383.0 21.6 %all-gather.17.cloned.1.call-done = bf16[2048,2,1024]{2,1,0:T(2,128)(2,1)} async-done(((bf16[512,2,1024]{2,1,0:T(2,128)(2,1)}), bf16[2048,2,1024]{2,1,0:T(2,128)(2,1)}) %all-gather.17.cloned.1.call-update) | async-done | bytes 8388624 | tf_op jit(solution)/shard_map/all_gather | solution.py:194
  404.6 10.6 copy.51
  415.2 70.9 %all-gather.15.cloned.1.call-done = bf16[2048,2048]{1,0:T(8,128)(2,1)} async-done(((bf16[256,2048]{1,0:T(8,128)(2,1)}), bf16[2048,2048]{1,0:T(8,128)(2,1)}) %all-gather.15.cloned.1.call-update) | async-done | bytes 8388624 | tf_op jit(solution)/shard_map/all_gather | solution.py:211
  486.1 24.7 %fusion.28 = f32[2048,2048]{0,1:T(8,128)} fusion(bf16[2048,2048]{1,0:T(8,128)(2,1)} %all-gather.15.cloned.1.call-done, bf16[2048,2048]{1,0:T(8,128)(2,1)} %bitcast.51), kind=kOutput, calls=%fused_computation.74 | convolution fusion | flops 17179869184 | bytes 33554432 | tf_op jit(solution)/shard_map/td,df->tf/dot_general | solution.py:165
  510.9 28.4 %all-gather.19.cloned.1.call-done = bf16[1024,2048]{1,0:T(8,128)(2,1)} async-done(((bf16[1024,512]{1,0:T(8,128)(2,1)}), bf16[1024,2048]{1,0:T(8,128)(2,1)}) %all-gather.19.cloned.1.call-update) | async-done | bytes 4194320 | tf_op jit(solution)/shard_map/all_gather | solution.py:195
  539.3 85.1 %all-gather.21.cloned.1.call-done = bf16[2048,2048]{1,0:T(8,128)(2,1)} async-done(((bf16[2048,256]{1,0:T(8,128)(2,1)}), bf16[2048,2048]{1,0:T(8,128)(2,1)}) %all-gather.21.cloned.1.call-update) | async-done | bytes 8388624 | tf_op jit(solution)/shard_map/all_gather | solution.py:196
  624.4 22.1 %multiply_convert_fusion.1 = (bf16[2048,1024]{0,1:T(8,128)(2,1)}, bf16[2048,1024]{0,1:T(8,128)(2,1)}, bf16[2048,1024]{0,1:T(8,128)(2,1)}) fusion(f32[2048,2048]{0,1:T(8,128)} %fusion.28, bf16[2048,2048]{1,0:T(8,128)(2,1)} %all-gather.21.cloned.1.call-done, bf16[1024,2048]{1,0:T(8,128)(2,1)} %all-gather.19.cloned.1.call-done), kind=kOutput, calls=%fused_computation.10 | convolution fusion | flops 8621391872 | bytes 41943040 | tf_op jit(solution)/shard_map/td,fd->tf/dot_general | solution.py:165
  646.5 23.9 %convolution_convert_fusion.2 = bf16[2048,2048]{1,0:T(8,128)(2,1)} fusion(bf16[2048,2048]{1,0:T(8,128)(2,1)} %bitcast.52, bf16[2048,1024]{0,1:T(8,128)(2,1)} %get-tuple-element.21, bf16[2048,1024]{0,1:T(8,128)(2,1)} %get-tuple-element.20), kind=kOutput, calls=%fused_computation.16 | convolution fusion | flops 17200840704 | bytes 25165824 | tf_op jit(solution)/shard_map/tf,df->td/dot_general | solution.py:165
  670.5 14.0 %convolution_convert_fusion.3 = bf16[2048,2048]{1,0:T(8,128)(2,1)} fusion(bf16[2048,1024]{0,1:T(8,128)(2,1)} %get-tuple-element.22, bf16[1024,2048]{1,0:T(8,128)(2,1)} %all-gather.19.cloned.1.call-done), kind=kOutput, calls=%fused_computation.17 | convolution fusion | flops 8594128896 | bytes 16777216 | tf_op jit(solution)/shard_map/tf,fd->td/dot_general | solution.py:165
  684.6 71.2 %reduce-scatter.13.cloned.1.call-done = bf16[256,2048]{1,0:T(8,128)(2,1)} async-done(((bf16[2048,2048]{1,0:T(8,128)(2,1)}), bf16[256,2048]{1,0:T(8,128)(2,1)}) %reduce-scatter.13.cloned.1.call-update) | async-done | bytes 1048592 | tf_op jit(solution)/shard_map/reduce_scatter | solution.py:178
  758.2 87.8 %reduce-scatter.11.cloned.1.call-done = bf16[256,2048]{1,0:T(8,128)(2,1)} async-done(((bf16[2048,2048]{1,0:T(8,128)(2,1)}), bf16[256,2048]{1,0:T(8,128)(2,1)}) %reduce-scatter.11.cloned.1.call-update) | async-done | bytes 1048592 | tf_op jit(solution)/shard_map/reduce_scatter | solution.py:178
  851.7 82.9 %all-gather.23.cloned.1.call-done = bf16[2048,2048]{1,0:T(8,128)(2,1)} async-done(((bf16[256,2048]{1,0:T(8,128)(2,1)}), bf16[2048,2048]{1,0:T(8,128)(2,1)}) %all-gather.23.cloned.1.call-update) | async-done | bytes 8388624 | tf_op jit(solution)/shard_map/all_gather | solution.py:229
  941.4 32.4 %attend_backward.1 = bf16[2048,768]{1,0:T(8,128)(2,1)} custom-call(s32[1]{0:T(128)} %collective-permute-done.1.prefix_ref, bf16[2048,768]{1,0:T(8,128)(2,1)} %copy.41.q_ref.k_ref.v_ref.qkv_ref, bf16[2048,256]{1,0:T(8,128)(2,1)} %get-tuple-element.8.o_ref, bf16[2048,256]{1,0:T(8,128)(2,1)} %convolution_convert_fusion.8.do_ref, ...), custom_call_target="tpu_custom_call" | custom-call | flops 10737418240 | bytes 10485760 | tf_op jit(solution)/shard_map/attend_backward/pallas_call | solution.py:121
  973.8 10.9 convolution_convert_fusion.1
  985.2 23.6 %convolution_convert_fusion = bf16[2048,2048]{1,0:T(8,128)(2,1)} fusion(bf16[2048,2048]{1,0:T(8,128)(2,1)} %all-gather.15.cloned.1.call-done, bf16[2048,1024]{0,1:T(8,128)(2,1)} %get-tuple-element.21, bf16[2048,1024]{0,1:T(8,128)(2,1)} %get-tuple-element.20), kind=kOutput, calls=%fused_computation.14 | convolution fusion | flops 17200840704 | bytes 25165824 | tf_op jit(solution)/shard_map/td,tf->df/dot_general | solution.py:165
  1008.9 13.8 %convolution_convert_fusion.5 = bf16[1024,2048]{1,0:T(8,128)(2,1)} fusion(bf16[2048,1024]{0,1:T(8,128)(2,1)} %get-tuple-element.22, bf16[2048,2048]{1,0:T(8,128)(2,1)} %all-gather.21.cloned.1.call-done), kind=kOutput, calls=%fused_computation.19 | convolution fusion | flops 8592031744 | bytes 16777216 | tf_op jit(solution)/shard_map/tf,td->fd/dot_general | solution.py:165
  1023.4 12.3 convolution_convert_fusion.6
  1041.4 45.9 %reduce-scatter.15.cloned.1.call-done = bf16[256,2048]{1,0:T(8,128)(2,1)} async-done(((bf16[2048,2048]{1,0:T(8,128)(2,1)}), bf16[256,2048]{1,0:T(8,128)(2,1)}) %reduce-scatter.15.cloned.1.call-update) | async-done | bytes 1048592 | tf_op jit(solution)/shard_map/reduce_scatter | solution.py:178
  1093.0 9.6 all-to-all-start.1
  1109.4 72.6 %reduce-scatter.21.cloned.1.call-done = bf16[512,2048]{1,0:T(8,128)(2,1)} async-done(((bf16[2048,2048]{1,0:T(8,128)(2,1)}), bf16[512,2048]{1,0:T(8,128)(2,1)}) %reduce-scatter.21.cloned.1.call-update) | async-done | bytes 2097168 | tf_op jit(solution)/shard_map/reduce_scatter | solution.py:226
  1185.6 64.0 %reduce-scatter.23.cloned.1.call-done = bf16[1024,512]{1,0:T(8,128)(2,1)} async-done(((bf16[1024,2048]{1,0:T(8,128)(2,1)}), bf16[1024,512]{1,0:T(8,128)(2,1)}) %reduce-scatter.23.cloned.1.call-update) | async-done | bytes 1048592 | tf_op jit(solution)/shard_map/reduce_scatter | solution.py:224
  1259.7 49.5 %reduce-scatter.17.cloned.1.call-done = bf16[512,768]{1,0:T(8,128)(2,1)} async-done(((bf16[2048,768]{1,0:T(8,128)(2,1)}), bf16[512,768]{1,0:T(8,128)(2,1)}) %reduce-scatter.17.cloned.1.call-update) | async-done | bytes 786448 | tf_op jit(solution)/shard_map/reduce_scatter | solution.py:236
  1311.5 29.8 %reduce-scatter.19.cloned.1.call-done = bf16[256,512]{1,0:T(8,128)(2,1)} async-done(((bf16[256,2048]{1,0:T(8,128)(2,1)}), bf16[256,512]{1,0:T(8,128)(2,1)}) %reduce-scatter.19.cloned.1.call-update) | async-done | bytes 262160 | tf_op jit(solution)/shard_map/reduce_scatter | solution.py:231
  (154 shorter events, 150.9 us)
Async XLA Ops:
  7.2 67.4 %all-gather.11.cloned.1.call-start = ((), (), s32[]{:S(2)}) async-start(), calls=%async_computation.11 | async-start | bytes 3932160 | tf_op jit(solution)/shard_map/all_gather | solution.py:192
  7.2 14.4 %collective-permute-start.2 = (bf16[512,2,384]{2,1,0:T(2,128)(2,1)}, bf16[512,2,384]{2,1,0:T(2,128)(2,1)S(1)}, u32[]{:S(2)}, u32[]{:S(2)}) collective-permute-start(bf16[512,2,384]{2,1,0:T(2,128)(2,1)} %param.9), channel_id=1, source_target_pairs={{0,0},{1,8},{8,1},{9,9},{2,2},{3,10},{10,3},{11,11},{4,4},{5,12},{... | collective-permute-start | bytes 2359304 | tf_op jit(solution)/shard_map/ppermute | solution.py:175
  22.5 137.2 %all-gather.9.cloned.1.call-start = ((), (), s32[]{:S(2)}) async-start(), calls=%async_computation.10 | async-start | bytes 9437184 | tf_op jit(solution)/shard_map/all_gather | solution.py:190
  22.6 24.8 %collective-permute-start = (bf16[2048,256]{1,0:T(8,128)(2,1)}, bf16[2048,256]{1,0:T(8,128)(2,1)S(1)}, u32[]{:S(2)}, u32[]{:S(2)}) collective-permute-start(bf16[2048,256]{1,0:T(8,128)(2,1)} %param.7), channel_id=1, source_target_pairs={{0,0},{1,8},{8,1},{9,9},{2,2},{3,10},{10,3},{11,11},{4,4},{5,12},{... | collective-permute-start | bytes 3145736 | tf_op jit(solution)/shard_map/ppermute | solution.py:175
  48.4 152.4 %all-gather.13.cloned.1.call-start = ((), (), s32[]{:S(2)}) async-start(), calls=%async_computation.12 | async-start | bytes 1310720 | tf_op jit(solution)/shard_map/all_gather | solution.py:193
  48.4 130.4 %collective-permute-start.1 = (s32[1]{0:T(128)}, s32[1]{0:T(128)}, u32[]{:S(2)}, u32[]{:S(2)}) collective-permute-start(s32[1]{0:T(128)} %param.8), channel_id=1, source_target_pairs={{0,0},{1,8},{8,1},{9,9},{2,2},{3,10},{10,3},{11,11},{4,4},{5,12},{... | collective-permute-start | bytes 20 | tf_op jit(solution)/shard_map/ppermute | solution.py:175
  52.0 13.9 %collective-permute-start.3 = (bf16[256,512]{1,0:T(8,128)(2,1)}, bf16[256,512]{1,0:T(8,128)(2,1)S(1)}, u32[]{:S(2)}, u32[]{:S(2)}) collective-permute-start(bf16[256,512]{1,0:T(8,128)(2,1)} %param.10), channel_id=1, source_target_pairs={{0,0},{1,8},{8,1},{9,9},{2,2},{3,10},{10,3},{11,11},{4,4},{5,12},{... | collective-permute-start | bytes 786440 | tf_op jit(solution)/shard_map/ppermute | solution.py:175
  66.6 226.7 %reduce-scatter.9.cloned.1.call-start = ((), (), s32[]{:S(2)}) async-start(), calls=%async_computation.13 | async-start | bytes 9437184 | tf_op jit(solution)/shard_map/reduce_scatter | solution.py:178
  207.9 196.6 %all-gather.17.cloned.1.call-start = ((), (), s32[]{:S(2)}) async-start(), calls=%async_computation.15 | async-start | bytes 10485760 | tf_op jit(solution)/shard_map/all_gather | solution.py:194
  208.0 28.0 %collective-permute-start.4 = (bf16[512,2,1024]{2,1,0:T(2,128)(2,1)}, bf16[512,2,1024]{2,1,0:T(2,128)(2,1)S(1)}, u32[]{:S(2)}, u32[]{:S(2)}) collective-permute-start(bf16[512,2,1024]{2,1,0:T(2,128)(2,1)} %param.11), channel_id=1, source_target_pairs={{0,0},{1,8},{8,1},{9,9},{2,2},{3,10},{10,3},{11,11},{4,4},{5,12},{... | collective-permute-start | bytes 6291464 | tf_op jit(solution)/shard_map/ppermute | solution.py:175
  237.3 248.8 %all-gather.15.cloned.1.call-start = ((), (), s32[]{:S(2)}) async-start(), calls=%async_computation.14 | async-start | bytes 9437184 | tf_op jit(solution)/shard_map/all_gather | solution.py:211
  301.1 238.2 %all-gather.19.cloned.1.call-start = ((), (), s32[]{:S(2)}) async-start(), calls=%async_computation.16 | async-start | bytes 5242880 | tf_op jit(solution)/shard_map/all_gather | solution.py:195
  301.1 40.8 %collective-permute-start.5 = (bf16[1024,512]{1,0:T(8,128)(2,1)S(1)}, bf16[1024,512]{1,0:T(8,128)(2,1)S(1)}, u32[]{:S(2)}, u32[]{:S(2)}) collective-permute-start(bf16[1024,512]{1,0:T(8,128)(2,1)S(1)} %copy-done.27), channel_id=1, source_target_pairs={{0,0},{1,8},{8,1},{9,9},{2,2},{3,10},{10,3},{11,11},{4,4},{5,12},{... | collective-permute-start | bytes 3145736 | tf_op jit(solution)/shard_map/ppermute | solution.py:175
  342.9 281.5 %all-gather.21.cloned.1.call-start = ((), (), s32[]{:S(2)}) async-start(), calls=%async_computation.18 | async-start | bytes 9437184 | tf_op jit(solution)/shard_map/all_gather | solution.py:196
  343.0 39.0 %collective-permute-start.7 = (bf16[2048,256]{1,0:T(8,128)(2,1)}, bf16[2048,256]{1,0:T(8,128)(2,1)S(1)}, u32[]{:S(2)}, u32[]{:S(2)}) collective-permute-start(bf16[2048,256]{1,0:T(8,128)(2,1)} %param.13), channel_id=1, source_target_pairs={{0,0},{1,8},{8,1},{9,9},{2,2},{3,10},{10,3},{11,11},{4,4},{5,12},{... | collective-permute-start | bytes 3145736 | tf_op jit(solution)/shard_map/ppermute | solution.py:175
  382.9 372.9 %reduce-scatter.13.cloned.1.call-start = ((), (), s32[]{:S(2)}) async-start(), calls=%async_computation.19 | async-start | bytes 9437184 | tf_op jit(solution)/shard_map/reduce_scatter | solution.py:178
  670.4 175.5 %reduce-scatter.11.cloned.1.call-start = ((), (), s32[]{:S(2)}) async-start(), calls=%async_computation.17 | async-start | bytes 9437184 | tf_op jit(solution)/shard_map/reduce_scatter | solution.py:178
  684.5 250.1 %all-gather.23.cloned.1.call-start = ((), (), s32[]{:S(2)}) async-start(), calls=%async_computation.20 | async-start | bytes 9437184 | tf_op jit(solution)/shard_map/all_gather | solution.py:229
  845.9 88.7 %copy-start.17 = (bf16[256,2048]{1,0:T(8,128)(2,1)S(1)}, bf16[256,2048]{1,0:T(8,128)(2,1)}, u32[]{:S(2)}) copy-start(bf16[256,2048]{1,0:T(8,128)(2,1)} %all-gather.13.cloned.1.call-done) | copy-start | bytes 3145732
  851.5 235.8 %reduce-scatter.15.cloned.1.call-start = ((), (), s32[]{:S(2)}) async-start(), calls=%async_computation.21 | async-start | bytes 9437184 | tf_op jit(solution)/shard_map/reduce_scatter | solution.py:178
  984.7 197.3 %reduce-scatter.21.cloned.1.call-start = ((), (), s32[]{:S(2)}) async-start(), calls=%async_computation.24 | async-start | bytes 10485760 | tf_op jit(solution)/shard_map/reduce_scatter | solution.py:226
  1008.8 240.7 %reduce-scatter.23.cloned.1.call-start = ((), (), s32[]{:S(2)}) async-start(), calls=%async_computation.25 | async-start | bytes 5242880 | tf_op jit(solution)/shard_map/reduce_scatter | solution.py:224
  1022.8 286.4 %reduce-scatter.17.cloned.1.call-start = ((), (), s32[]{:S(2)}) async-start(), calls=%async_computation.22 | async-start | bytes 3932160 | tf_op jit(solution)/shard_map/reduce_scatter | solution.py:236
  1036.9 56.2 %all-to-all-start = ((bf16[256,8,256]{2,0,1:T(8,128)(2,1)}), bf16[256,8,256]{2,0,1:T(8,128)(2,1)}, u32[]{:S(2)}, u32[]{:S(2)}) async-start(bf16[256,8,256]{2,0,1:T(8,128)(2,1)} %bitcast.54), calls=%async_computation.2 | async-start | bytes 2097152 | tf_op jit(solution)/shard_map/all_to_all | solution.py:181
  1093.0 162.1 %all-to-all-start.1 = ((bf16[256,8,256]{2,0,1:T(8,128)(2,1)}), bf16[256,8,256]{2,0,1:T(8,128)(2,1)S(1)}, u32[]{:S(2)}, u32[]{:S(2)}) async-start(bf16[256,8,256]{2,0,1:T(8,128)(2,1)} %bitcast.45), calls=%async_computation.5 | async-start | bytes 2097152 | tf_op jit(solution)/shard_map/all_to_all | solution.py:181
  1102.6 238.7 %reduce-scatter.19.cloned.1.call-start = ((), (), s32[]{:S(2)}) async-start(), calls=%async_computation.23 | async-start | bytes 1310720 | tf_op jit(solution)/shard_map/reduce_scatter | solution.py:231
  1182.0 165.7 %collective-permute-start.11 = (bf16[512,2048]{1,0:T(8,128)(2,1)}, bf16[512,2048]{1,0:T(8,128)(2,1)S(1)}, u32[]{:S(2)}, u32[]{:S(2)}) collective-permute-start(bf16[512,2048]{1,0:T(8,128)(2,1)} %reduce-scatter.21.cloned.1.call-done), channel_id=1, source_target_pairs={{0,0},{1,8},{8,1},{9,9},{2,2},{3,10},{10,3},{11,11},{4,4},{5,12},{... | collective-permute-start | bytes 6291464 | tf_op jit(solution)/shard_map/ppermute | solution.py:175
  1249.6 61.9 %collective-permute-start.12 = (bf16[1024,512]{1,0:T(8,128)(2,1)}, bf16[1024,512]{1,0:T(8,128)(2,1)}, u32[]{:S(2)}, u32[]{:S(2)}) collective-permute-start(bf16[1024,512]{1,0:T(8,128)(2,1)} %reduce-scatter.23.cloned.1.call-done), channel_id=1, source_target_pairs={{0,0},{1,8},{8,1},{9,9},{2,2},{3,10},{10,3},{11,11},{4,4},{5,12},{... | collective-permute-start | bytes 3145736 | tf_op jit(solution)/shard_map/ppermute | solution.py:175
  1253.1 99.7 %collective-permute-start.6 = (bf16[2048,256]{1,0:T(8,128)(2,1)}, bf16[2048,256]{1,0:T(8,128)(2,1)}, u32[]{:S(2)}, u32[]{:S(2)}) collective-permute-start(bf16[2048,256]{1,0:T(8,128)(2,1)} %bitcast.6), channel_id=1, source_target_pairs={{0,0},{1,8},{8,1},{9,9},{2,2},{3,10},{10,3},{11,11},{4,4},{5,12},{... | collective-permute-start | bytes 3145736 | tf_op jit(solution)/shard_map/ppermute | solution.py:175
  1256.1 100.5 %collective-permute-start.8 = (bf16[2048,256]{1,0:T(8,128)(2,1)}, bf16[2048,256]{1,0:T(8,128)(2,1)S(1)}, u32[]{:S(2)}, u32[]{:S(2)}) collective-permute-start(bf16[2048,256]{1,0:T(8,128)(2,1)} %bitcast.58), channel_id=1, source_target_pairs={{0,0},{1,8},{8,1},{9,9},{2,2},{3,10},{10,3},{11,11},{4,4},{5,12},{... | collective-permute-start | bytes 3145736 | tf_op jit(solution)/shard_map/ppermute | solution.py:175
  1309.2 44.5 %collective-permute-start.9 = (bf16[512,768]{1,0:T(8,128)(2,1)}, bf16[512,768]{1,0:T(8,128)(2,1)}, u32[]{:S(2)}, u32[]{:S(2)}) collective-permute-start(bf16[512,768]{1,0:T(8,128)(2,1)} %reduce-scatter.17.cloned.1.call-done), channel_id=1, source_target_pairs={{0,0},{1,8},{8,1},{9,9},{2,2},{3,10},{10,3},{11,11},{4,4},{5,12},{... | collective-permute-start | bytes 2359304 | tf_op jit(solution)/shard_map/ppermute | solution.py:175
  1341.3 11.6 collective-permute-start.10
  (27 other events, 405.1 us)
Sparse Core Ops, SparseCore 0:
  22.6 51.8 all-gather.10
  76.7 82.9 all-gather.8
  162.1 24.2 all-gather.12
  208.1 85.1 reduce-scatter.8
  295.6 108.9 all-gather.16
  406.6 79.4 all-gather.14
  488.5 50.6 all-gather.18
  541.4 82.9 all-gather.20
  670.6 85.2 reduce-scatter.12
  757.9 87.9 reduce-scatter.10
  851.6 82.9 all-gather.22
  984.8 102.4 reduce-scatter.14
  1090.4 91.5 reduce-scatter.20
  1185.6 63.8 reduce-scatter.22
  1252.4 56.7 reduce-scatter.16
  1312.5 28.7 reduce-scatter.18

commit v2 on v1

--- a/solution.py
+++ b/solution.py
@@ -247,16 +247,470 @@
     )
 
 
+AXES = ("y", "core", "zh", "zl", "x")
+GROUP = ("core", "zl", "x")
+MESH = pl.DeviceIdType.MESH
+
+
+def place():
+    y, c, zh, zl, x = (lax.axis_index(name) for name in AXES)
+    sibling = (y, 1 - c, zh, zl, x)
+
+    def peer(dz, dx):
+        return (y, c, zh, lax.rem(zl + dz, 2), lax.rem(x + dx, 2))
+
+    def chip(dz, dx):
+        return lax.rem(zl + dz, 2) * 2 + lax.rem(x + dx, 2)
+
+    order = [2 * y + zh, 2 * y + 1 - zh, 2 * (1 - y) + zh, 2 * (1 - y) + 1 - zh]
+    return c, sibling, peer, chip, order
+
+
+def meet(devices):
+    barrier = pltpu.get_barrier_semaphore()
+    for device in devices:
+        pl.semaphore_signal(barrier, inc=1, device_id=device, device_id_type=MESH)
+    pl.semaphore_wait(barrier, len(devices))
+
+
+def span(start, size):
+    return pl.ds(pl.multiple_of(start, size), size)
+
+
+def remote(src, dst, send_sem, recv_sem, device):
+    return pltpu.make_async_remote_copy(
+        src_ref=src, dst_ref=dst, send_sem=send_sem, recv_sem=recv_sem, device_id=device, device_id_type=MESH
+    )
+
+
+def each_rows(count, body, size=32):
+    def step(i, carry):
+        body(span(i * size, size))
+        return carry
+
+    lax.fori_loop(0, count // size, step, 0)
+
+
+def row_norm(values):
+    center = values - jnp.mean(values, axis=-1, keepdims=True)
+    inv_std = lax.rsqrt(jnp.mean(center * center, axis=-1, keepdims=True) + EPSILON)
+    return center * inv_std, inv_std
+
+
+def reduce_kernel(kind, transposed, a_ref, w0, w1, w2, w3, *refs):
+    if kind == "mid":
+        base_ref, total_ref, norm_ref = refs[:3]
+        rest = refs[3:]
+    elif kind == "out":
+        base_ref, result_ref = refs[:2]
+        rest = refs[2:]
+    elif kind == "back":
+        base_ref, value_ref, total_ref, result_ref = refs[:4]
+        rest = refs[4:]
+    else:
+        base_ref, value_ref, result_ref = refs[:3]
+        rest = refs[3:]
+    (sib_out, sib_in, own, diag_out, diag_in, near_out, near_in,
+     sib_send, sib_recv, diag_send, diag_recv, near_send, near_recv) = rest
+    piece = own.shape[1]
+    half = piece // 2
+    c, sibling, peer, chip, order = place()
+    across, along = peer(0, 1), peer(1, 0)
+    meet([sibling, across, along])
+    weights = (w0, w1, w2, w3)
+    block = weights[0].shape[0] if transposed else weights[0].shape[1]
+
+    def compute(owner, out_ref):
+        left = a_ref[span(owner * piece, piece), :]
+        for weight, index in zip(weights, order):
+            part = dot(left, weight[...], NT if transposed else NN)
+            out_ref[:, span(index * block, block)] = part.astype(out_ref.dtype)
+
+    def sib_copy(step):
+        return remote(sib_out.at[step], sib_in.at[step], sib_send.at[step], sib_recv.at[step], sibling)
+
+    def diag_copy(part):
+        return remote(
+            diag_out.at[pl.ds(part * half, half)], diag_in.at[part], diag_send.at[part], diag_recv.at[part],
+            across if part == 0 else along,
+        )
+
+    def near_copy(part):
+        return remote(
+            near_out.at[part], near_in.at[part], near_send.at[part], near_recv.at[part], across if part == 0 else along
+        )
+
+    def step(s, carry):
+        target = chip(1 - lax.rem(s, 2), 1 - s // 2)
+        compute((1 - c) * 4 + target, sib_out.at[s])
+        sib_copy(s).start()
+
+        @pl.when(s == 1)
+        def _():
+            finish_diag()
+
+        @pl.when(s == 2)
+        def _():
+            finish_near(0)
+
+        @pl.when(s == 3)
+        def _():
+            finish_near(1)
+
+        compute(c * 4 + target, own.at[lax.rem(s, 2)])
+        return carry
+
+    def finish_diag():
+        sib_copy(0).wait_recv()
+
+        def body(rows):
+            diag_out[rows, :] = (own[0, rows, :] + sib_in[0, rows, :].astype(F32)).astype(BF)
+
+        each_rows(piece, body)
+        diag_copy(0).start()
+        diag_copy(1).start()
+
+    def finish_near(part):
+        step_index = part + 1
+        slot = step_index % 2
+        sib_copy(step_index).wait_recv()
+        source = 1 - part
+        diag_copy(source).wait_recv()
+        low = source * half
+
+        def plain(i, carry):
+            rows = span((1 - source) * half + i * 32, 32)
+            near_out[part, rows, :] = (own[slot, rows, :] + sib_in[step_index, rows, :].astype(F32)).astype(BF)
+            return carry
+
+        def added(i, carry):
+            rows = span(low + i * 32, 32)
+            total = own[slot, rows, :] + sib_in[step_index, rows, :].astype(F32)
+            near_out[part, rows, :] = (total + diag_in[source, span(i * 32, 32), :].astype(F32)).astype(BF)
+            return carry
+
+        lax.fori_loop(0, half // 32, plain, 0)
+        lax.fori_loop(0, half // 32, added, 0)
+        near_copy(part).start()
+
+    lax.fori_loop(0, 4, step, 0)
+    sib_copy(3).wait_recv()
+    near_copy(0).wait_recv()
+    near_copy(1).wait_recv()
+
+    def last(rows):
+        total = own[1, rows, :] + sib_in[3, rows, :].astype(F32)
+        total = total + near_in[0, rows, :].astype(F32) + near_in[1, rows, :].astype(F32)
+        if kind == "mid":
+            middle = base_ref[rows, :].astype(F32) + total
+            total_ref[rows, :] = middle
+            norm_ref[rows, :] = row_norm(middle)[0].astype(BF)
+        elif kind == "out":
+            result_ref[rows, :] = (base_ref[rows, :] + total).astype(BF)
+        else:
+            normed, inv_std = row_norm(value_ref[rows, :].astype(F32))
+            mean_grad = jnp.mean(total, axis=-1, keepdims=True)
+            mean_cross = jnp.mean(total * normed, axis=-1, keepdims=True)
+            grad = base_ref[rows, :].astype(F32) + inv_std * (total - mean_grad - normed * mean_cross)
+            if kind == "back":
+                total_ref[rows, :] = grad
+            result_ref[rows, :] = grad.astype(BF)
+
+    each_rows(piece, last, 16)
+    for s in range(4):
+        sib_copy(s).wait_send()
+    for part in range(2):
+        diag_copy(part).wait_send()
+        near_copy(part).wait_send()
+
+
+VMEM_WHOLE = pl.BlockSpec(memory_space=pltpu.VMEM)
+
+
+def reduce_call(kind, transposed, left, weights, extras, ident):
+    piece, width = extras[0].shape
+    steps = 4
+    shape = functools.partial(jax.ShapeDtypeStruct, (piece, width))
+    outs = {"mid": [shape(F32), shape(BF)], "out": [shape(BF)], "back": [shape(F32), shape(BF)], "end": [shape(BF)]}[kind]
+    tokens, depth = left.shape
+    dma = pltpu.SemaphoreType.DMA
+    return pl.pallas_call(
+        functools.partial(reduce_kernel, kind, transposed),
+        out_shape=outs,
+        in_specs=[VMEM_WHOLE] * (5 + len(extras)),
+        out_specs=[VMEM_WHOLE] * len(outs),
+        scratch_shapes=[
+            pltpu.VMEM((steps, piece, width), BF),
+            pltpu.VMEM((steps, piece, width), BF),
+            pltpu.VMEM((2, piece, width), F32),
+            pltpu.VMEM((piece, width), BF),
+            pltpu.VMEM((2, piece // 2, width), BF),
+            pltpu.VMEM((2, piece, width), BF),
+            pltpu.VMEM((2, piece, width), BF),
+            dma((steps,)), dma((steps,)), dma((2,)), dma((2,)), dma((2,)), dma((2,)),
+        ],
+        compiler_params=pltpu.CompilerParams(
+            collective_id=ident, has_side_effects=True, vmem_limit_bytes=60 << 20
+        ),
+        cost_estimate=pl.CostEstimate(
+            flops=2 * tokens * depth * width + (20 << 30), bytes_accessed=4 * tokens * width, transcendentals=0
+        ),
+        name="reduce_" + kind,
+    )(left, *weights, *extras)
+
+
+def gather_body(own_ref, full, sems, process):
+    near_send, near_recv, diag_send, diag_recv, sib_send, sib_recv = sems
+    piece = own_ref.shape[0]
+    half = piece // 2
+    c, sibling, peer, chip, order = place()
+    across, along = peer(0, 1), peer(1, 0)
+    meet([sibling, across, along])
+    mine = chip(0, 0)
+
+    def rows_of(core, target):
+        return span((core * 4 + target) * piece, piece)
+
+    def near_copy(part, target):
+        rows = rows_of(c, target)
+        return remote(full.at[rows], full.at[rows], near_send.at[part], near_recv.at[part], across if part == 0 else along)
+
+    def diag_copy(part, target):
+        rows = span((c * 4 + target) * piece + part * half, half)
+        return remote(full.at[rows], full.at[rows], diag_send.at[part], diag_recv.at[part], along if part == 0 else across)
+
+    def sib_copy(slot, core, target):
+        rows = rows_of(core, target)
+        return remote(full.at[rows], full.at[rows], sib_send.at[slot], sib_recv.at[slot], sibling)
+
+    full[rows_of(c, mine), :] = own_ref[...]
+    near_copy(0, mine).start()
+    near_copy(1, mine).start()
+    sib_copy(0, c, mine).start()
+    process(c * 4 + mine)
+    sib_copy(0, 1 - c, mine).wait_recv()
+    process((1 - c) * 4 + mine)
+    x_chip, z_chip, d_chip = chip(0, 1), chip(1, 0), chip(1, 1)
+    near_copy(0, x_chip).wait_recv()
+    diag_copy(0, x_chip).start()
+    sib_copy(1, c, x_chip).start()
+    near_copy(1, z_chip).wait_recv()
+    diag_copy(1, z_chip).start()
+    sib_copy(2, c, z_chip).start()
+    process(c * 4 + x_chip)
+    process(c * 4 + z_chip)
+    sib_copy(1, 1 - c, x_chip).wait_recv()
+    process((1 - c) * 4 + x_chip)
+    diag_copy(0, d_chip).wait_recv()
+    diag_copy(1, d_chip).wait_recv()
+    sib_copy(3, c, d_chip).start()
+    sib_copy(2, 1 - c, z_chip).wait_recv()
+    process((1 - c) * 4 + z_chip)
+    process(c * 4 + d_chip)
+    sib_copy(3, 1 - c, d_chip).wait_recv()
+    process((1 - c) * 4 + d_chip)
+    near_copy(0, mine).wait_send()
+    near_copy(1, mine).wait_send()
+    diag_copy(0, x_chip).wait_send()
+    diag_copy(1, z_chip).wait_send()
+    for slot in range(4):
+        sib_copy(slot, c, mine).wait_send()
+
+
+def gather_sems():
+    dma = pltpu.SemaphoreType.DMA
+    return [dma((2,)), dma((2,)), dma((2,)), dma((2,)), dma((4,)), dma((4,))]
+
+
+def feed_kernel(own_ref, cot_ref, u0, u1, u2, u3, d0, d1, d2, d3, full, hidden_ref, grad_ref, *sems):
+    piece = own_ref.shape[0]
+    order = place()[4]
+    block = u0.shape[0]
+    width = hidden_ref.shape[1]
+    tile = 256
+
+    def process(owner):
+        rows = span(owner * piece, piece)
+
+        def tile_step(t, carry):
+            cols, up_cols = span(t * tile, tile), span(width + t * tile, tile)
+            gate = up = grad = None
+            for u_ref, d_ref, index in zip((u0, u1, u2, u3), (d0, d1, d2, d3), order):
+                deep = span(index * block, block)
+                normed = full[rows, deep]
+                terms = (
+                    dot(normed, u_ref[:, cols], NN),
+                    dot(normed, u_ref[:, up_cols], NN),
+                    dot(cot_ref[rows, deep], d_ref[cols, :], NT),
+                )
+                gate, up, grad = terms if gate is None else (gate + terms[0], up + terms[1], grad + terms[2])
+            sig = 1.0 / (1.0 + jnp.exp(-gate))
+            active = gate * sig
+            hidden_ref[rows, cols] = (active * up).astype(BF)
+            grad_ref[rows, cols] = (grad * up * sig * (1.0 + gate * (1.0 - sig))).astype(BF)
+            grad_ref[rows, up_cols] = (grad * active).astype(BF)
+            return carry
+
+        lax.fori_loop(0, width // tile, tile_step, 0)
+
+    gather_body(own_ref, full, sems, process)
+
+
+def feed_call(own, cot, ups, downs, ident):
+    tokens, width = cot.shape
+    hidden = downs[0].shape[0]
+    return pl.pallas_call(
+        feed_kernel,
+        out_shape=[
+            jax.ShapeDtypeStruct((tokens, width), BF),
+            jax.ShapeDtypeStruct((tokens, hidden), BF),
+            jax.ShapeDtypeStruct((tokens, 2 * hidden), BF),
+        ],
+        in_specs=[VMEM_WHOLE] * 10,
+        out_specs=[VMEM_WHOLE] * 3,
+        scratch_shapes=gather_sems(),
+        compiler_params=pltpu.CompilerParams(collective_id=ident, has_side_effects=True, vmem_limit_bytes=60 << 20),
+        cost_estimate=pl.CostEstimate(
+            flops=6 * tokens * hidden * width + (20 << 30), bytes_accessed=8 * tokens * width, transcendentals=tokens * hidden
+        ),
+        name="gather_feed",
+    )(own, cot, *ups, *downs)
+
+
+def mix_kernel(own_ref, w0, w1, w2, w3, full, mixed_ref, *sems):
+    piece = own_ref.shape[0]
+    order = place()[4]
+    block = w0.shape[1]
+
+    def process(owner):
+        rows = span(owner * piece, piece)
+        total = None
+        for weight, index in zip((w0, w1, w2, w3), order):
+            part = dot(full[rows, span(index * block, block)], weight[...], NT)
+            total = part if total is None else total + part
+        mixed_ref[rows, :] = total.astype(BF)
+
+    gather_body(own_ref, full, sems, process)
+
+
+def mix_call(own, weights, tokens, ident):
+    width = own.shape[1]
+    inner = weights[0].shape[0]
+    return pl.pallas_call(
+        mix_kernel,
+        out_shape=[jax.ShapeDtypeStruct((tokens, width), BF), jax.ShapeDtypeStruct((tokens, inner), BF)],
+        in_specs=[VMEM_WHOLE] * 5,
+        out_specs=[VMEM_WHOLE] * 2,
+        scratch_shapes=gather_sems(),
+        compiler_params=pltpu.CompilerParams(collective_id=ident, has_side_effects=True, vmem_limit_bytes=60 << 20),
+        cost_estimate=pl.CostEstimate(
+            flops=2 * tokens * inner * width + (20 << 30), bytes_accessed=4 * tokens * width, transcendentals=0
+        ),
+        name="gather_mix",
+    )(own, *weights)
+
+
+def swapped(value, flip=0):
+    pairs = (
+        [(0, 0), (1, 2), (2, 1), (3, 3)],
+        [(0, 1), (1, 3), (2, 0), (3, 2)],
+        [(1, 0), (3, 1), (0, 2), (2, 3)],
+    )[flip]
+    return lax.ppermute(value, ("core", "zh"), pairs)
+
+
+def over_y(value):
+    return lax.ppermute(value, "y", [(0, 1), (1, 0)])
+
+
+def weight_blocks(weight):
+    first, second = swapped(weight, 0), swapped(weight, 1)
+    return first, second, over_y(first), over_y(second)
+
+
+def weight_scatter(grad, axis):
+    y, zh = lax.axis_index("y"), lax.axis_index("zh")
+    half = grad.shape[axis] // 2
+    other = lax.dynamic_slice_in_dim(grad, (1 - y) * half, half, axis).astype(BF)
+    mine = lax.dynamic_slice_in_dim(grad, y * half, half, axis).astype(F32)
+    total = (mine + over_y(other).astype(F32)).astype(BF)
+    block = half // 2
+    first = swapped(lax.dynamic_slice_in_dim(total, zh * block, block, axis), 0)
+    second = swapped(lax.dynamic_slice_in_dim(total, (1 - zh) * block, block, axis), 2)
+    return first.astype(F32) + second.astype(F32)
+
+
+def local_fine(inputs, prefix_len, w_qkv, w_out, w_up_gate, w_down, cotangent):
+    heads, head_dim = w_qkv.shape[1], w_qkv.shape[2] // 3
+    hidden_width = w_down.shape[0]
+    prefix_len = swapped(prefix_len)
+    inputs, cotangent = swapped(inputs), swapped(cotangent)
+    qkv_blocks = weight_blocks(w_qkv.reshape(w_qkv.shape[0], -1))
+    out_blocks = weight_blocks(w_out)
+    up_blocks = weight_blocks(w_up_gate.reshape(w_up_gate.shape[0], -1))
+    down_blocks = weight_blocks(w_down)
+    tokens = inputs.shape[0]
+    full_in = lax.all_gather(inputs, GROUP, axis=1, tiled=True)
+    cot_full = lax.all_gather(cotangent, GROUP, axis=1, tiled=True)
+    width = full_in.shape[1]
+    piece = tokens // lax.axis_size(GROUP)
+    first = lax.axis_index(GROUP) * piece
+    own_in = lax.dynamic_slice_in_dim(full_in, first, piece, 0)
+    own_cot = lax.dynamic_slice_in_dim(cot_full, first, piece, 0)
+    y, zh = lax.axis_index("y"), lax.axis_index("zh")
+    order = [2 * y + zh, 2 * y + 1 - zh, 2 * (1 - y) + zh, 2 * (1 - y) + 1 - zh]
+
+    normed_in = norm(full_in.astype(F32))[0].astype(BF)
+    block = qkv_blocks[0].shape[0]
+    qkv_rows = 0.0
+    for weight, index in zip(qkv_blocks, order):
+        qkv_rows = qkv_rows + mm("td,de->te", lax.dynamic_slice_in_dim(normed_in, index * block, block, 1), weight)
+    qkv_rows = qkv_rows.reshape(tokens, heads, 3, head_dim)
+    cosine, sine = rope_tables(tokens, head_dim)
+    turned = rotate(qkv_rows[:, :, :2], cosine[:, None, None], sine[:, None, None])
+    qkv = jnp.concatenate([turned, qkv_rows[:, :, 2:]], axis=2).astype(BF)
+    qkv = qkv.reshape(tokens, heads * 3 * head_dim)
+    mixed, lse = attend_fwd(qkv, prefix_len, heads, hd=head_dim)
+    middle, normed_own = reduce_call("mid", False, mixed, out_blocks, (own_in,), 1)
+    normed_mid, hidden, grad_gate_up = feed_call(normed_own, cot_full, up_blocks, down_blocks, 2)
+    grad_middle, branch_own = reduce_call("back", True, grad_gate_up, up_blocks, (own_cot, middle), 3)
+    grad_branch, grad_mixed = mix_call(branch_own, out_blocks, tokens, 4)
+    grad_up = weight_scatter(mm("td,tf->df", normed_mid, grad_gate_up), 0)
+    grad_down = weight_scatter(mm("tf,td->fd", hidden, cot_full), 1)
+    grad_rows = attend_bwd(qkv, mixed, grad_mixed, lse, prefix_len, cosine, sine, heads, hd=head_dim)
+    (input_grad,) = reduce_call("end", True, grad_rows, qkv_blocks, (grad_middle, own_in), 5)
+    (outputs,) = reduce_call("out", False, hidden, down_blocks, (middle,), 6)
+    grad_out = weight_scatter(mm("tc,td->cd", mixed, grad_branch), 1)
+    grad_qkv = weight_scatter(mm("td,te->de", normed_in, grad_rows), 0)
+
+    def spread(value):
+        return swapped(lax.all_to_all(value, GROUP, 1, 0, tiled=True))
+
+    return (
+        spread(outputs),
+        spread(input_grad).astype(F32),
+        grad_qkv.reshape(-1, heads, 3 * head_dim),
+        grad_out,
+        grad_up.reshape(-1, 2, hidden_width),
+        grad_down,
+    )
+
+
 def solution(mesh):
     row_size, col_size = mesh.shape["row"], mesh.shape["col"]
-    col_major = 4
-    shape = (row_size // 2, 2, col_major, col_size // col_major)
-    fine = Mesh(mesh.devices.reshape(shape), ("rmaj", "core", "cmaj", "cmin"))
-    row, col = ("rmaj", "core"), ("cmaj", "cmin")
+    fine = (row_size, col_size) == (4, 8)
+    if fine:
+        names, shape, body = AXES, (2,) * 5, local_fine
+        row, col = AXES[:2], AXES[2:]
+    else:
+        names = ("rmaj", "core", "cmaj", "cmin")
+        shape = (row_size // 2, 2, 4, col_size // 4)
+        body = functools.partial(local, shape[3] == 2)
+        row, col = names[:2], names[2:]
     outs = (P(row, col), P(row, col), P(row, col, None), P(col, row), P(row, None, col), P(col, row))
     return jax.shard_map(
-        functools.partial(local, shape[3] == 2),
-        mesh=fine,
+        body,
+        mesh=Mesh(mesh.devices.reshape(shape), names),
         in_specs=(P(row, col), P(row), P(row, col, None), P(col, row), P(row, None, col), P(col, row), P(row, col)),
         out_specs=outs,
         check_vma=False,

time: 1370 us -> 1040 us (0.76)
  waiting for transfers between devices: 987 us -> 385 us
  Pallas kernels: 54.4 us -> 389 us
  matrix products: 173 us -> 74.6 us
  starting transfers between devices: 57.8 us -> 76.3 us
    reduce_scatter x8 -> x0, waiting for transfers between devices: 477 us -> none  [the longest x4 261 us: scatter(): lax.psum_scatter(value.astype(BF), cols, scatter_dimension=0, tiled=True)]
    all_gather x8 -> x2, waiting for transfers between devices: 376 us -> 0.01 us  [the longest x1 0.01 us: local_fine(): full_in = lax.all_gather(inputs, GROUP, axis=1, tiled=True)]
    pallas_call x0 -> x6, Pallas kernels: none -> 338 us  [the longest x4 218 us: reduce_call(): pl.pallas_call(functools.partial(reduce_kernel, kind, transposed), out_sh...]
    ppermute x13 -> x33, waiting for transfers between devices: 135 us -> 385 us  [the longest x21 290 us: swapped(): return lax.ppermute(value, ('core', 'zh'), pairs)]
    dot_general x12 -> x8, matrix products: 173 us -> 74.6 us  [mm(): return jnp.einsum(spec, left, right, preferred_element_type=F32)]
    ppermute x13 -> x33, starting transfers between devices: 42.1 us -> 66.4 us  [the longest x21 52.4 us: swapped(): return lax.ppermute(value, ('core', 'zh'), pairs)]
  transfers between devices with their start and end apart: 31 -> 37, of which waited for: 21 -> 15; matrix products, arithmetic and copies ran while one was open for 12% -> 14% of each run, Pallas kernels for 2% -> 26%
where the time goes in v2:
time: 1040 us; the launch traced here: 1030 us
  Pallas kernels  389 us (37%)
  waiting for transfers between devices  385 us (37%)
  starting transfers between devices  76.3 us (7%)
  matrix products  74.6 us (7%)
  local copies, waits for them, and re-layouts  46.7 us (4%)
  other arithmetic  40.7 us (4%)
  between operations  14.8 us (1%)
    ppermute x21, waiting for transfers between devices, swapped(): return lax.ppermute(value, ('core', 'zh'), pairs)  290 us
    pallas_call x4, Pallas kernels, reduce_call(): pl.pallas_call(functools.partial(reduce_kernel, kind, transposed), out_sh...  218 us
    ppermute x12, waiting for transfers between devices, over_y(): return lax.ppermute(value, 'y', [(0, 1), (1, 0)])  95.4 us
    dot_general x8, matrix products, mm(): return jnp.einsum(spec, left, right, preferred_element_type=F32)  74.6 us
    pallas_call x1, Pallas kernels, feed_call(): pl.pallas_call(feed_kernel, out_shape=[jax.ShapeDtypeStruct((tokens, widt...  73.9 us
    ppermute x21, starting transfers between devices, swapped(): return lax.ppermute(value, ('core', 'zh'), pairs)  52.4 us
    pallas_call x1, Pallas kernels, mix_call(): pl.pallas_call(mix_kernel, out_shape=[jax.ShapeDtypeStruct((tokens, width...  46.7 us
    pallas_call x1, Pallas kernels, attend_bwd(): pl.pallas_call(functools.partial(bwd_kernel, bq=bq, bk=bk, hd=hd, scale=h...  30.3 us
  transfers between devices with their start and end apart: 37, of which 15 were waited for; matrix products, arithmetic and copies ran while one was open for 14% of the time, Pallas kernels for 26%

profile of v2, /device:TPU:1, one launch (start us, length us, event | category | flops | bytes accessed | tf_op | source)
XLA Modules:
  0.0 1027.2 jit_solution(6644993139153932738)
XLA Ops:
  7.2 5.7 collective-permute-start.1
  13.0 23.9 %collective-permute-done.1 = bf16[2048,256]{1,0:T(8,128)(2,1)S(1)} collective-permute-done((bf16[2048,256]{1,0:T(8,128)(2,1)}, bf16[2048,256]{1,0:T(8,128)(2,1)S(1)}, u32[]{:S(2)}, u32[]{:S(2)}) %collective-permute-start.1) | collective-permute-done | bytes 1048608 | tf_op jit(solution)/shard_map/ppermute | solution.py:619
  39.9 26.6 %collective-permute-done.10 = bf16[2048,256]{1,0:T(8,128)(2,1)S(1)} collective-permute-done((bf16[2048,256]{1,0:T(8,128)(2,1)}, bf16[2048,256]{1,0:T(8,128)(2,1)S(1)}, u32[]{:S(2)}, u32[]{:S(2)}) %collective-permute-start.10) | collective-permute-done | bytes 1048608 | tf_op jit(solution)/shard_map/ppermute | solution.py:619
  84.5 52.5 %collective-permute-done.2.w0 = bf16[512,768]{1,0:T(8,128)(2,1)} collective-permute-done((bf16[512,768]{1,0:T(8,128)(2,1)}, bf16[512,768]{1,0:T(8,128)(2,1)}, u32[]{:S(2)}, u32[]{:S(2)}) %collective-permute-start.2) | collective-permute-done | bytes 786464 | tf_op jit(solution)/shard_map/ppermute | solution.py:619
  158.7 5.6 fusion.8
  166.8 8.0 add_add_fusion
  174.8 21.5 %collective-permute-done.prefix_ref = s32[1]{0:T(128)} collective-permute-done((s32[1]{0:T(128)}, s32[1]{0:T(128)}, u32[]{:S(2)}, u32[]{:S(2)}) %collective-permute-start) | collective-permute-done | bytes 36 | tf_op jit(solution)/shard_map/ppermute | solution.py:619
  206.2 20.2 %attend_forward.1 = (bf16[2048,256]{1,0:T(8,128)(2,1)}, f32[2,8,2048]{2,1,0:T(8,128)}) custom-call(s32[1]{0:T(128)} %collective-permute-done.prefix_ref, bf16[2048,768]{1,0:T(8,128)(2,1)} %copy.37.q_ref.k_ref.v_ref.qkv_ref, bf16[2048,768]{1,0:T(8,128)(2,1)} %copy.37.q_ref.k_ref.v_ref.qkv_ref, bf16[2048,768]{1,0:T(8,128)(2,1)} %copy.37.q_ref.k_ref.v_ref.qkv_ref), custom_call_target="tpu_custom_call" | custom-call | flops 4294967296 | bytes 4194304 | tf_op jit(solution)/shard_map/attend_forward/pallas_call | solution.py:52
  228.7 18.7 %collective-permute-done.15.d0.w0 = bf16[1024,512]{1,0:T(8,128)(2,1)} collective-permute-done((bf16[1024,512]{1,0:T(8,128)(2,1)}, bf16[1024,512]{1,0:T(8,128)(2,1)}, u32[]{:S(2)}, u32[]{:S(2)}) %collective-permute-start.15) | collective-permute-done | bytes 1048608 | tf_op jit(solution)/shard_map/ppermute | solution.py:619
  248.7 6.0 collective-permute-done.16.d1.w1
  258.1 48.7 %reduce_mid.1 = (f32[256,2048]{1,0:T(8,128)}, bf16[256,2048]{1,0:T(8,128)(2,1)}) custom-call(bf16[2048,256]{1,0:T(8,128)(2,1)} %get-tuple-element.17.a_ref.o_ref, bf16[256,512]{1,0:T(8,128)(2,1)} %copy-done.14, bf16[256,512]{1,0:T(8,128)(2,1)} %collective-permute-done.7.w1, bf16[256,512]{1,0:T(8,128)(2,1)} %collective-permute-done.8.w2, ...), custom_call_target="tpu_custom_call" | custom-call | flops 23622320128 | bytes 16777216 | tf_op jit(solution)/shard_map/reduce_mid/pallas_call | solution.py:437
  306.8 33.6 %collective-permute-done.13.u2.w2 = bf16[512,2048]{1,0:T(8,128)(2,1)S(1)} collective-permute-done((bf16[512,2048]{1,0:T(8,128)(2,1)}, bf16[512,2048]{1,0:T(8,128)(2,1)S(1)}, u32[]{:S(2)}, u32[]{:S(2)}) %collective-permute-start.13) | collective-permute-done | bytes 2097184 | tf_op jit(solution)/shard_map/ppermute | solution.py:623
  340.4 30.9 %collective-permute-done.14.u3.w3 = bf16[512,2048]{1,0:T(8,128)(2,1)} collective-permute-done((bf16[512,2048]{1,0:T(8,128)(2,1)}, bf16[512,2048]{1,0:T(8,128)(2,1)}, u32[]{:S(2)}, u32[]{:S(2)}) %collective-permute-start.14) | collective-permute-done | bytes 2097184 | tf_op jit(solution)/shard_map/ppermute | solution.py:623
  371.2 73.9 %gather_feed.1 = (bf16[2048,2048]{1,0:T(8,128)(2,1)}, bf16[2048,1024]{1,0:T(8,128)(2,1)}, bf16[2048,2048]{1,0:T(8,128)(2,1)}) custom-call(bf16[256,2048]{1,0:T(8,128)(2,1)} %get-tuple-element.18.own_ref, bf16[2048,2048]{1,0:T(8,128)(2,1)} %all-gather.5.cloned.1.call-done.cot_ref, bf16[512,2048]{1,0:T(8,128)(2,1)} %collective-permute-done.11.u0.w0, ...), custom_call_target="tpu_custom_call" | custom-call | flops 47244640256 | bytes 33554432 | tf_op jit(solution)/shard_map/gather_feed/pallas_call | solution.py:562
  445.2 50.8 %reduce_out.1 = bf16[256,2048]{1,0:T(8,128)(2,1)} custom-call(bf16[2048,1024]{1,0:T(8,128)(2,1)} %get-tuple-element.19.a_ref, bf16[1024,512]{1,0:T(8,128)(2,1)} %collective-permute-done.15.d0.w0, bf16[1024,512]{1,0:T(8,128)(2,1)} %collective-permute-done.16.d1.w1, bf16[1024,512]{1,0:T(8,128)(2,1)} %copy-done.13, ...), custom_call_target="tpu_custom_call" | custom-call | flops 30064771072 | bytes 16777216 | tf_op jit(solution)/shard_map/reduce_out/pallas_call | solution.py:437
  498.3 5.6 all-to-all-start
  506.2 63.0 %reduce_back.1 = (f32[256,2048]{1,0:T(8,128)}, bf16[256,2048]{1,0:T(8,128)(2,1)}) custom-call(bf16[2048,2048]{1,0:T(8,128)(2,1)} %get-tuple-element.21.a_ref, bf16[512,2048]{1,0:T(8,128)(2,1)} %collective-permute-done.11.u0.w0, bf16[512,2048]{1,0:T(8,128)(2,1)} %collective-permute-done.12.u1.w1, bf16[512,2048]{1,0:T(8,128)(2,1)} %copy-done.12, ...), custom_call_target="tpu_custom_call" | custom-call | flops 38654705664 | bytes 16777216 | tf_op jit(solution)/shard_map/reduce_back/pallas_call | solution.py:437
  569.3 46.7 %gather_mix.1 = (bf16[2048,2048]{1,0:T(8,128)(2,1)}, bf16[2048,256]{1,0:T(8,128)(2,1)}) custom-call(bf16[256,2048]{1,0:T(8,128)(2,1)} %get-tuple-element.22.own_ref, bf16[256,512]{1,0:T(8,128)(2,1)} %copy-done.14, bf16[256,512]{1,0:T(8,128)(2,1)} %collective-permute-done.7.w1, bf16[256,512]{1,0:T(8,128)(2,1)} %collective-permute-done.8.w2, ...), custom_call_target="tpu_custom_call" | custom-call | flops 23622320128 | bytes 16777216 | tf_op jit(solution)/shard_map/gather_mix/pallas_call | solution.py:599
  616.0 30.3 %attend_backward.1.a_ref = bf16[2048,768]{1,0:T(8,128)(2,1)} custom-call(s32[1]{0:T(128)} %collective-permute-done.prefix_ref, bf16[2048,768]{1,0:T(8,128)(2,1)} %copy.37.q_ref.k_ref.v_ref.qkv_ref, bf16[2048,256]{1,0:T(8,128)(2,1)} %get-tuple-element.17.a_ref.o_ref, bf16[2048,256]{1,0:T(8,128)(2,1)} %get-tuple-element.23.do_ref, ...), custom_call_target="tpu_custom_call" | custom-call | flops 10737418240 | bytes 10485760 | tf_op jit(solution)/shard_map/attend_backward/pallas_call | solution.py:121
  646.3 10.8 %fusion.18 = f32[2048,768]{1,0:T(8,128)S(1)} fusion(bf16[2048,2048]{1,0:T(8,128)(2,1)} %copy-done.2, bf16[2048,768]{1,0:T(8,128)(2,1)} %attend_backward.1.a_ref), kind=kOutput, calls=%fused_computation.53 | convolution fusion | flops 6442450944 | bytes 17825792 | tf_op jit(solution)/shard_map/td,te->de/dot_general | solution.py:165
  665.9 22.5 %fusion.20 = f32[2048,2048]{1,0:T(8,128)S(1)} fusion(bf16[2048,2048]{1,0:T(8,128)(2,1)} %get-tuple-element.27, bf16[2048,2048]{1,0:T(8,128)(2,1)} %get-tuple-element.21.a_ref), kind=kOutput, calls=%fused_computation.55 | convolution fusion | flops 17179869184 | bytes 33554432 | tf_op jit(solution)/shard_map/td,tf->df/dot_general | solution.py:165
  692.3 16.1 %fusion.21 = f32[1024,2048]{1,0:T(8,128)S(1)} fusion(bf16[2048,1024]{1,0:T(8,128)(2,1)} %get-tuple-element.19.a_ref, bf16[2048,2048]{1,0:T(8,128)(2,1)} %all-gather.5.cloned.1.call-done.cot_ref), kind=kOutput, calls=%fused_computation.56 | convolution fusion | flops 8589934592 | bytes 20971520 | tf_op jit(solution)/shard_map/tf,td->fd/dot_general | solution.py:165
  713.2 55.1 %reduce_end.1 = bf16[256,2048]{1,0:T(8,128)(2,1)} custom-call(bf16[2048,768]{1,0:T(8,128)(2,1)} %attend_backward.1.a_ref, bf16[512,768]{1,0:T(8,128)(2,1)} %collective-permute-done.2.w0, bf16[512,768]{1,0:T(8,128)(2,1)} %collective-permute-done.3.w1, bf16[512,768]{1,0:T(8,128)(2,1)} %collective-permute-done.4.w2, ...), custom_call_target="tpu_custom_call" | custom-call | flops 27917287424 | bytes 16777216 | tf_op jit(solution)/shard_map/reduce_end/pallas_call | solution.py:437
  785.7 12.6 %collective-permute-done.27 = bf16[1024,2048]{1,0:T(8,128)(2,1)} collective-permute-done((bf16[1024,2048]{1,0:T(8,128)(2,1)}, bf16[1024,2048]{1,0:T(8,128)(2,1)}, u32[]{:S(2)}, u32[]{:S(2)}) %collective-permute-start.27) | collective-permute-done | bytes 4194336 | tf_op jit(solution)/shard_map/ppermute | solution.py:623
  801.0 6.2 add_convert_fusion
  813.5 11.3 %collective-permute-start.29 = (bf16[512,2048]{1,0:T(8,128)(2,1)}, bf16[512,2048]{1,0:T(8,128)(2,1)}, u32[]{:S(2)}, u32[]{:S(2)}) collective-permute-start(bf16[512,2048]{1,0:T(8,128)(2,1)} %get-tuple-element.31), channel_id=1, source_target_pairs={{4,0},{12,4},{0,8},{8,12},{5,1},{13,5},{1,9},{9,13},{6,2},{14,6},{... | collective-permute-start | bytes 6291464 | tf_op jit(solution)/shard_map/ppermute | solution.py:619
  824.8 17.8 %collective-permute-done.30 = bf16[1024,1024]{1,0:T(8,128)(2,1)} collective-permute-done((bf16[1024,1024]{1,0:T(8,128)(2,1)}, bf16[1024,1024]{1,0:T(8,128)(2,1)}, u32[]{:S(2)}, u32[]{:S(2)}) %collective-permute-start.30) | collective-permute-done | bytes 2097184 | tf_op jit(solution)/shard_map/ppermute | solution.py:623
  852.7 38.1 %collective-permute-done.22 = bf16[512,768]{1,0:T(8,128)(2,1)} collective-permute-done((bf16[512,768]{1,0:T(8,128)(2,1)}, bf16[512,768]{1,0:T(8,128)(2,1)}, u32[]{:S(2)}, u32[]{:S(2)}) %collective-permute-start.22) | collective-permute-done | bytes 786464 | tf_op jit(solution)/shard_map/ppermute | solution.py:619
  890.8 22.5 %collective-permute-done.19 = bf16[2048,256]{1,0:T(8,128)(2,1)} collective-permute-done((bf16[2048,256]{1,0:T(8,128)(2,1)}, bf16[2048,256]{1,0:T(8,128)(2,1)}, u32[]{:S(2)}, u32[]{:S(2)}) %collective-permute-start.19) | collective-permute-done | bytes 1048608 | tf_op jit(solution)/shard_map/ppermute | solution.py:619
  920.5 60.2 %collective-permute-done.20 = bf16[2048,256]{1,0:T(8,128)(2,1)} collective-permute-done((bf16[2048,256]{1,0:T(8,128)(2,1)}, bf16[2048,256]{1,0:T(8,128)(2,1)}, u32[]{:S(2)}, u32[]{:S(2)}) %collective-permute-start.20) | collective-permute-done | bytes 1048608 | tf_op jit(solution)/shard_map/ppermute | solution.py:619
  983.4 19.8 %collective-permute-done.31 = bf16[1024,512]{1,0:T(8,128)(2,1)} collective-permute-done((bf16[1024,512]{1,0:T(8,128)(2,1)S(1)}, bf16[1024,512]{1,0:T(8,128)(2,1)}, u32[]{:S(2)}, u32[]{:S(2)}) %collective-permute-start.31) | collective-permute-done | bytes 1048608 | tf_op jit(solution)/shard_map/ppermute | solution.py:619
  1011.4 6.6 reshape.110
  (137 shorter events, 140.7 us)
Async XLA Ops:
  7.2 131.3 %all-gather.3.cloned.1.call-start = ((), (), s32[]{:S(2)}) async-start(), calls=%async_computation.2 | async-start | bytes 9437184 | tf_op jit(solution)/shard_map/all_gather | solution.py:653
  37.9 333.4 %all-gather.5.cloned.1.call-start = ((), (), s32[]{:S(2)}) async-start(), calls=%async_computation.3 | async-start | bytes 9437184 | tf_op jit(solution)/shard_map/all_gather | solution.py:654
  69.6 67.4 %collective-permute-start.2 = (bf16[512,768]{1,0:T(8,128)(2,1)}, bf16[512,768]{1,0:T(8,128)(2,1)}, u32[]{:S(2)}, u32[]{:S(2)}) collective-permute-start(bf16[512,768]{1,0:T(8,128)(2,1)} %bitcast.13), channel_id=1, source_target_pairs={{0,0},{4,8},{8,4},{12,12},{1,1},{5,9},{9,5},{13,13},{2,2},{6,10},{... | collective-permute-start | bytes 2359304 | tf_op jit(solution)/shard_map/ppermute | solution.py:619
  71.5 66.8 %collective-permute-start.3 = (bf16[512,768]{1,0:T(8,128)(2,1)}, bf16[512,768]{1,0:T(8,128)(2,1)}, u32[]{:S(2)}, u32[]{:S(2)}) collective-permute-start(bf16[512,768]{1,0:T(8,128)(2,1)} %bitcast.13), channel_id=1, source_target_pairs={{0,4},{4,12},{8,0},{12,8},{1,5},{5,13},{9,1},{13,9},{2,6},{6,14},{... | collective-permute-start | bytes 2359304 | tf_op jit(solution)/shard_map/ppermute | solution.py:619
  71.6 126.7 %collective-permute-start.6 = (bf16[256,512]{1,0:T(8,128)(2,1)}, bf16[256,512]{1,0:T(8,128)(2,1)S(1)}, u32[]{:S(2)}, u32[]{:S(2)}) collective-permute-start(bf16[256,512]{1,0:T(8,128)(2,1)} %param.10), channel_id=1, source_target_pairs={{0,0},{4,8},{8,4},{12,12},{1,1},{5,9},{9,5},{13,13},{2,2},{6,10},{... | collective-permute-start | bytes 786440 | tf_op jit(solution)/shard_map/ppermute | solution.py:619
  76.1 123.1 %collective-permute-start.7 = (bf16[256,512]{1,0:T(8,128)(2,1)}, bf16[256,512]{1,0:T(8,128)(2,1)}, u32[]{:S(2)}, u32[]{:S(2)}) collective-permute-start(bf16[256,512]{1,0:T(8,128)(2,1)} %param.10), channel_id=1, source_target_pairs={{0,4},{4,12},{8,0},{12,8},{1,5},{5,13},{9,1},{13,9},{2,6},{6,14},{... | collective-permute-start | bytes 786440 | tf_op jit(solution)/shard_map/ppermute | solution.py:619
  78.1 177.8 %collective-permute-start.11 = (bf16[512,2048]{1,0:T(8,128)(2,1)}, bf16[512,2048]{1,0:T(8,128)(2,1)}, u32[]{:S(2)}, u32[]{:S(2)}) collective-permute-start(bf16[512,2048]{1,0:T(8,128)(2,1)} %bitcast.15), channel_id=1, source_target_pairs={{0,0},{4,8},{8,4},{12,12},{1,1},{5,9},{9,5},{13,13},{2,2},{6,10},{... | collective-permute-start | bytes 6291464 | tf_op jit(solution)/shard_map/ppermute | solution.py:619
  158.7 97.4 %collective-permute-start.12 = (bf16[512,2048]{1,0:T(8,128)(2,1)}, bf16[512,2048]{1,0:T(8,128)(2,1)}, u32[]{:S(2)}, u32[]{:S(2)}) collective-permute-start(bf16[512,2048]{1,0:T(8,128)(2,1)} %bitcast.15), channel_id=1, source_target_pairs={{0,4},{4,12},{8,0},{12,8},{1,5},{5,13},{9,1},{13,9},{2,6},{6,14},{... | collective-permute-start | bytes 6291464 | tf_op jit(solution)/shard_map/ppermute | solution.py:619
  164.3 32.0 %collective-permute-start = (s32[1]{0:T(128)}, s32[1]{0:T(128)}, u32[]{:S(2)}, u32[]{:S(2)}) collective-permute-start(s32[1]{0:T(128)} %param.8), channel_id=1, source_target_pairs={{0,0},{4,8},{8,4},{12,12},{1,1},{5,9},{9,5},{13,13},{2,2},{6,10},{... | collective-permute-start | bytes 20 | tf_op jit(solution)/shard_map/ppermute | solution.py:619
  196.3 51.1 %collective-permute-start.15 = (bf16[1024,512]{1,0:T(8,128)(2,1)}, bf16[1024,512]{1,0:T(8,128)(2,1)}, u32[]{:S(2)}, u32[]{:S(2)}) collective-permute-start(bf16[1024,512]{1,0:T(8,128)(2,1)} %param.12), channel_id=1, source_target_pairs={{0,0},{4,8},{8,4},{12,12},{1,1},{5,9},{9,5},{13,13},{2,2},{6,10},{... | collective-permute-start | bytes 3145736 | tf_op jit(solution)/shard_map/ppermute | solution.py:619
  198.2 56.4 %collective-permute-start.16 = (bf16[1024,512]{1,0:T(8,128)(2,1)}, bf16[1024,512]{1,0:T(8,128)(2,1)}, u32[]{:S(2)}, u32[]{:S(2)}) collective-permute-start(bf16[1024,512]{1,0:T(8,128)(2,1)} %param.12), channel_id=1, source_target_pairs={{0,4},{4,12},{8,0},{12,8},{1,5},{5,13},{9,1},{13,9},{2,6},{6,14},{... | collective-permute-start | bytes 3145736 | tf_op jit(solution)/shard_map/ppermute | solution.py:619
  204.9 52.5 %collective-permute-start.9 = (bf16[256,512]{1,0:T(8,128)(2,1)}, bf16[256,512]{1,0:T(8,128)(2,1)S(1)}, u32[]{:S(2)}, u32[]{:S(2)}) collective-permute-start(bf16[256,512]{1,0:T(8,128)(2,1)} %collective-permute-done.7.w1), channel_id=1, source_target_pairs={{0,16},{16,0},{1,17},{17,1},{2,18},{18,2},{3,19},{19,3},{4,20},{20... | collective-permute-start | bytes 786440 | tf_op jit(solution)/shard_map/ppermute | solution.py:623
  247.4 59.4 %collective-permute-start.17 = (bf16[1024,512]{1,0:T(8,128)(2,1)}, bf16[1024,512]{1,0:T(8,128)(2,1)S(1)}, u32[]{:S(2)}, u32[]{:S(2)}) collective-permute-start(bf16[1024,512]{1,0:T(8,128)(2,1)} %collective-permute-done.15.d0.w0), channel_id=1, source_target_pairs={{0,16},{16,0},{1,17},{17,1},{2,18},{18,2},{3,19},{19,3},{4,20},{20... | collective-permute-start | bytes 3145736 | tf_op jit(solution)/shard_map/ppermute | solution.py:623
  254.7 52.2 %collective-permute-start.18 = (bf16[1024,512]{1,0:T(8,128)(2,1)}, bf16[1024,512]{1,0:T(8,128)(2,1)}, u32[]{:S(2)}, u32[]{:S(2)}) collective-permute-start(bf16[1024,512]{1,0:T(8,128)(2,1)} %collective-permute-done.16.d1.w1), channel_id=1, source_target_pairs={{0,16},{16,0},{1,17},{17,1},{2,18},{18,2},{3,19},{19,3},{4,20},{20... | collective-permute-start | bytes 3145736 | tf_op jit(solution)/shard_map/ppermute | solution.py:623
  255.9 84.4 %collective-permute-start.13 = (bf16[512,2048]{1,0:T(8,128)(2,1)}, bf16[512,2048]{1,0:T(8,128)(2,1)S(1)}, u32[]{:S(2)}, u32[]{:S(2)}) collective-permute-start(bf16[512,2048]{1,0:T(8,128)(2,1)} %collective-permute-done.11.u0.w0), channel_id=1, source_target_pairs={{0,16},{16,0},{1,17},{17,1},{2,18},{18,2},{3,19},{19,3},{4,20},{20... | collective-permute-start | bytes 6291464 | tf_op jit(solution)/shard_map/ppermute | solution.py:623
  256.1 115.1 %collective-permute-start.14 = (bf16[512,2048]{1,0:T(8,128)(2,1)}, bf16[512,2048]{1,0:T(8,128)(2,1)}, u32[]{:S(2)}, u32[]{:S(2)}) collective-permute-start(bf16[512,2048]{1,0:T(8,128)(2,1)} %collective-permute-done.12.u1.w1), channel_id=1, source_target_pairs={{0,16},{16,0},{1,17},{17,1},{2,18},{18,2},{3,19},{19,3},{4,20},{20... | collective-permute-start | bytes 6291464 | tf_op jit(solution)/shard_map/ppermute | solution.py:623
  498.3 281.9 %all-to-all-start = ((bf16[256,8,256]{2,0,1:T(8,128)(2,1)}), bf16[256,8,256]{2,0,1:T(8,128)(2,1)}, u32[]{:S(2)}, u32[]{:S(2)}) async-start(bf16[256,8,256]{2,0,1:T(8,128)(2,1)} %bitcast.31), calls=%async_computation | async-start | bytes 2097152 | tf_op jit(solution)/shard_map/all_to_all | solution.py:687
  658.4 119.5 %collective-permute-start.21 = (bf16[1024,768]{1,0:T(8,128)(2,1)}, bf16[1024,768]{1,0:T(8,128)(2,1)S(1)}, u32[]{:S(2)}, u32[]{:S(2)}) collective-permute-start(bf16[1024,768]{1,0:T(8,128)(2,1)} %dynamic-slice_convert_fusion.2), channel_id=1, source_target_pairs={{0,16},{16,0},{1,17},{17,1},{2,18},{18,2},{3,19},{19,3},{4,20},{20... | collective-permute-start | bytes 4718600 | tf_op jit(solution)/shard_map/ppermute | solution.py:623
  665.2 105.3 %collective-permute-start.24 = (bf16[256,1024]{1,0:T(8,128)(2,1)}, bf16[256,1024]{1,0:T(8,128)(2,1)}, u32[]{:S(2)}, u32[]{:S(2)}) collective-permute-start(bf16[256,1024]{1,0:T(8,128)(2,1)} %dynamic-slice_convert_fusion.3), channel_id=1, source_target_pairs={{0,16},{16,0},{1,17},{17,1},{2,18},{18,2},{3,19},{19,3},{4,20},{20... | collective-permute-start | bytes 1572872 | tf_op jit(solution)/shard_map/ppermute | solution.py:623
  691.4 106.8 %collective-permute-start.27 = (bf16[1024,2048]{1,0:T(8,128)(2,1)}, bf16[1024,2048]{1,0:T(8,128)(2,1)}, u32[]{:S(2)}, u32[]{:S(2)}) collective-permute-start(bf16[1024,2048]{1,0:T(8,128)(2,1)} %dynamic-slice_convert_fusion), channel_id=1, source_target_pairs={{0,16},{16,0},{1,17},{17,1},{2,18},{18,2},{3,19},{19,3},{4,20},{20... | collective-permute-start | bytes 12582920 | tf_op jit(solution)/shard_map/ppermute | solution.py:623
  712.3 130.2 %collective-permute-start.30 = (bf16[1024,1024]{1,0:T(8,128)(2,1)}, bf16[1024,1024]{1,0:T(8,128)(2,1)}, u32[]{:S(2)}, u32[]{:S(2)}) collective-permute-start(bf16[1024,1024]{1,0:T(8,128)(2,1)} %dynamic-slice_convert_fusion.1), channel_id=1, source_target_pairs={{0,16},{16,0},{1,17},{17,1},{2,18},{18,2},{3,19},{19,3},{4,20},{20... | collective-permute-start | bytes 6291464 | tf_op jit(solution)/shard_map/ppermute | solution.py:623
  772.6 34.6 %collective-permute-start.26 = (bf16[256,512]{1,0:T(8,128)(2,1)}, bf16[256,512]{1,0:T(8,128)(2,1)}, u32[]{:S(2)}, u32[]{:S(2)}) collective-permute-start(bf16[256,512]{1,0:T(8,128)(2,1)} %get-tuple-element.37), channel_id=1, source_target_pairs={{4,0},{12,4},{0,8},{8,12},{5,1},{13,5},{1,9},{9,13},{6,2},{14,6},{... | collective-permute-start | bytes 786440 | tf_op jit(solution)/shard_map/ppermute | solution.py:619
  772.8 40.8 %collective-permute-start.25 = (bf16[256,512]{1,0:T(8,128)(2,1)}, bf16[256,512]{1,0:T(8,128)(2,1)}, u32[]{:S(2)}, u32[]{:S(2)}) collective-permute-start(bf16[256,512]{1,0:T(8,128)(2,1)} %get-tuple-element.36), channel_id=1, source_target_pairs={{0,0},{4,8},{8,4},{12,12},{1,1},{5,9},{9,5},{13,13},{2,2},{6,10},{... | collective-permute-start | bytes 786440 | tf_op jit(solution)/shard_map/ppermute | solution.py:619
  780.2 69.2 %all-to-all-start.1 = ((bf16[256,8,256]{2,0,1:T(8,128)(2,1)}), bf16[256,8,256]{2,0,1:T(8,128)(2,1)}, u32[]{:S(2)}, u32[]{:S(2)}) async-start(bf16[256,8,256]{2,0,1:T(8,128)(2,1)} %bitcast.30), calls=%async_computation.1 | async-start | bytes 2097152 | tf_op jit(solution)/shard_map/all_to_all | solution.py:687
  785.6 63.7 %collective-permute-start.23 = (bf16[512,768]{1,0:T(8,128)(2,1)}, bf16[512,768]{1,0:T(8,128)(2,1)S(1)}, u32[]{:S(2)}, u32[]{:S(2)}) collective-permute-start(bf16[512,768]{1,0:T(8,128)(2,1)} %get-tuple-element.35), channel_id=1, source_target_pairs={{4,0},{12,4},{0,8},{8,12},{5,1},{13,5},{1,9},{9,13},{6,2},{14,6},{... | collective-permute-start | bytes 2359304 | tf_op jit(solution)/shard_map/ppermute | solution.py:619
  798.3 92.5 %collective-permute-start.22 = (bf16[512,768]{1,0:T(8,128)(2,1)}, bf16[512,768]{1,0:T(8,128)(2,1)}, u32[]{:S(2)}, u32[]{:S(2)}) collective-permute-start(bf16[512,768]{1,0:T(8,128)(2,1)} %get-tuple-element.34), channel_id=1, source_target_pairs={{0,0},{4,8},{8,4},{12,12},{1,1},{5,9},{9,5},{13,13},{2,2},{6,10},{... | collective-permute-start | bytes 2359304 | tf_op jit(solution)/shard_map/ppermute | solution.py:619
  807.2 106.0 %collective-permute-start.19 = (bf16[2048,256]{1,0:T(8,128)(2,1)}, bf16[2048,256]{1,0:T(8,128)(2,1)}, u32[]{:S(2)}, u32[]{:S(2)}) collective-permute-start(bf16[2048,256]{1,0:T(8,128)(2,1)} %bitcast.3), channel_id=1, source_target_pairs={{0,0},{4,8},{8,4},{12,12},{1,1},{5,9},{9,5},{13,13},{2,2},{6,10},{... | collective-permute-start | bytes 3145736 | tf_op jit(solution)/shard_map/ppermute | solution.py:619
  813.5 192.8 %collective-permute-start.29 = (bf16[512,2048]{1,0:T(8,128)(2,1)}, bf16[512,2048]{1,0:T(8,128)(2,1)}, u32[]{:S(2)}, u32[]{:S(2)}) collective-permute-start(bf16[512,2048]{1,0:T(8,128)(2,1)} %get-tuple-element.31), channel_id=1, source_target_pairs={{4,0},{12,4},{0,8},{8,12},{5,1},{13,5},{1,9},{9,13},{6,2},{14,6},{... | collective-permute-start | bytes 6291464 | tf_op jit(solution)/shard_map/ppermute | solution.py:619
  842.6 163.7 %collective-permute-start.28 = (bf16[512,2048]{1,0:T(8,128)(2,1)}, bf16[512,2048]{1,0:T(8,128)(2,1)}, u32[]{:S(2)}, u32[]{:S(2)}) collective-permute-start(bf16[512,2048]{1,0:T(8,128)(2,1)} %get-tuple-element.30), channel_id=1, source_target_pairs={{0,0},{4,8},{8,4},{12,12},{1,1},{5,9},{9,5},{13,13},{2,2},{6,10},{... | collective-permute-start | bytes 6291464 | tf_op jit(solution)/shard_map/ppermute | solution.py:619
  849.3 131.3 %collective-permute-start.20 = (bf16[2048,256]{1,0:T(8,128)(2,1)}, bf16[2048,256]{1,0:T(8,128)(2,1)}, u32[]{:S(2)}, u32[]{:S(2)}) collective-permute-start(bf16[2048,256]{1,0:T(8,128)(2,1)} %bitcast.5), channel_id=1, source_target_pairs={{0,0},{4,8},{8,4},{12,12},{1,1},{5,9},{9,5},{13,13},{2,2},{6,10},{... | collective-permute-start | bytes 3145736 | tf_op jit(solution)/shard_map/ppermute | solution.py:619
  890.8 92.6 %collective-permute-start.32 = (bf16[1024,512]{1,0:T(8,128)(2,1)}, bf16[1024,512]{1,0:T(8,128)(2,1)}, u32[]{:S(2)}, u32[]{:S(2)}) collective-permute-start(bf16[1024,512]{1,0:T(8,128)(2,1)} %get-tuple-element.33), channel_id=1, source_target_pairs={{4,0},{12,4},{0,8},{8,12},{5,1},{13,5},{1,9},{9,13},{6,2},{14,6},{... | collective-permute-start | bytes 3145736 | tf_op jit(solution)/shard_map/ppermute | solution.py:619
  913.3 89.9 %collective-permute-start.31 = (bf16[1024,512]{1,0:T(8,128)(2,1)S(1)}, bf16[1024,512]{1,0:T(8,128)(2,1)}, u32[]{:S(2)}, u32[]{:S(2)}) collective-permute-start(bf16[1024,512]{1,0:T(8,128)(2,1)S(1)} %get-tuple-element.32), channel_id=1, source_target_pairs={{0,0},{4,8},{8,4},{12,12},{1,1},{5,9},{9,5},{13,13},{2,2},{6,10},{... | collective-permute-start | bytes 3145736 | tf_op jit(solution)/shard_map/ppermute | solution.py:619
  (23 other events, 581.9 us)
Sparse Core Ops, SparseCore 0:
  38.0 77.7 all-gather.2
  117.9 101.1 all-gather.4

commit v3 on v1

--- a/solution.py
+++ b/solution.py
@@ -247,16 +247,1232 @@
     )
 
 
+AXES = ("y", "core", "zh", "zl", "x")
+GROUP = ("core", "zl", "x")
+MESH = pl.DeviceIdType.MESH
+DMA = pltpu.SemaphoreType.DMA
+VMEM_WHOLE = pl.BlockSpec(memory_space=pltpu.VMEM)
+ANYWHERE = pl.BlockSpec(memory_space=pl.ANY)
+
+
+class Place:
+    def __init__(self):
+        self.y, self.c, self.zh, self.zl, self.x = (lax.axis_index(name) for name in AXES)
+        y, c, zh, zl, x = self.y, self.c, self.zh, self.zl, self.x
+        self.sibling = (y, 1 - c, zh, zl, x)
+        self.across = (y, c, zh, zl, 1 - x)
+        self.along = (y, c, zh, 1 - zl, x)
+        self.beyond = (1 - y, c, zh, zl, x)
+        self.far = [(y, core, 1 - zh, zl, x) for core in (0, 1)]
+        self.far_role = (y, zh, 1 - zh, zl, x)
+        self.straight = c == zh
+        self.outer = zl == zh
+        self.order = [2 * y, 2 * y + 1, 2 * (1 - y), 2 * (1 - y) + 1]
+        self.block = c * 4 + zl * 2 + x
+
+    def chip(self, dz, dx):
+        return lax.rem(self.zl + dz, 2) * 2 + lax.rem(self.x + dx, 2)
+
+    def meet(self, greet=None):
+        devices = [self.sibling, self.across, self.along, self.beyond, *self.far]
+        barrier = pltpu.get_barrier_semaphore()
+        for device in devices:
+            pl.semaphore_signal(barrier, inc=1, device_id=device, device_id_type=MESH)
+        more = greet(self, barrier) if greet else 0
+        pl.semaphore_wait(barrier, len(devices) + more)
+
+
+def span(start, size):
+    return pl.ds(pl.multiple_of(start, size), size)
+
+
+def remote(src, dst, send_sem, recv_sem, device):
+    return pltpu.make_async_remote_copy(
+        src_ref=src, dst_ref=dst, send_sem=send_sem, recv_sem=recv_sem, device_id=device, device_id_type=MESH
+    )
+
+
+class Beyond:
+    along_z = False
+
+    def __init__(self, place, src, dst, sem):
+        self.copy = remote(src, dst, sem.at[0], sem.at[2], place.beyond)
+
+    def start(self):
+        self.copy.start()
+
+    def wait_recv(self):
+        self.copy.wait_recv()
+
+    def wait_send(self):
+        self.copy.wait_send()
+
+
+class WeightHalf:
+    along_z = True
+
+    def __init__(self, place, src, dst, sem):
+        c = place.c
+        self.straight = place.straight
+        self.outward = remote(src, dst.at[c], sem.at[0], sem.at[2 + c], place.far_role)
+        self.aside = remote(src, dst.at[c], sem.at[1], sem.at[2 + c], place.sibling)
+        self.here = pltpu.make_async_copy(src, dst.at[c], sem.at[1])
+        self.from_sibling = remote(src, dst.at[1 - c], sem.at[1], sem.at[3 - c], place.sibling)
+        self.from_far = [remote(src, dst.at[i], sem.at[0], sem.at[2 + i], place.far_role) for i in (0, 1)]
+
+    def start(self):
+        self.outward.start()
+
+        @pl.when(self.straight)
+        def _():
+            self.here.start()
+
+        @pl.when(jnp.logical_not(self.straight))
+        def _():
+            self.aside.start()
+
+    def wait_recv(self):
+        @pl.when(self.straight)
+        def _():
+            self.here.wait()
+            self.from_sibling.wait_recv()
+
+        @pl.when(jnp.logical_not(self.straight))
+        def _():
+            for copy in self.from_far:
+                copy.wait_recv()
+
+    def wait_send(self):
+        self.outward.wait_send()
+
+        @pl.when(jnp.logical_not(self.straight))
+        def _():
+            self.aside.wait_send()
+
+
+class GradHalf:
+    along_z = True
+
+    def __init__(self, place, src, dst, sem):
+        c, zh = place.c, place.zh
+        self.straight = place.straight
+        self.here = pltpu.make_async_copy(src.at[c], dst.at[zh], sem.at[0])
+        self.aside = remote(src.at[1 - c], dst.at[zh], sem.at[1], sem.at[2 + zh], place.sibling)
+        self.outward = [remote(src.at[i], dst.at[zh], sem.at[i], sem.at[2 + zh], place.far[i]) for i in (0, 1)]
+        self.from_sibling = remote(src.at[c], dst.at[zh], sem.at[1], sem.at[2 + zh], place.sibling)
+        self.from_far = remote(src.at[c], dst.at[1 - zh], sem.at[0], sem.at[3 - zh], place.far[0])
+
+    def start(self):
+        @pl.when(self.straight)
+        def _():
+            self.here.start()
+            self.aside.start()
+
+        @pl.when(jnp.logical_not(self.straight))
+        def _():
+            for copy in self.outward:
+                copy.start()
+
+    def wait_recv(self):
+        self.from_far.wait_recv()
+
+        @pl.when(self.straight)
+        def _():
+            self.here.wait()
+
+        @pl.when(jnp.logical_not(self.straight))
+        def _():
+            self.from_sibling.wait_recv()
+
+    def wait_send(self):
+        @pl.when(self.straight)
+        def _():
+            self.aside.wait_send()
+
+        @pl.when(jnp.logical_not(self.straight))
+        def _():
+            for copy in self.outward:
+                copy.wait_send()
+
+
+KINDS = {"beyond": Beyond, "weight": WeightHalf, "grad": GradHalf}
+
+
+def moved_shape(kind, src):
+    shape = (2, *src.shape) if kind == "weight" else src.shape
+    return jax.ShapeDtypeStruct(shape, src.dtype)
+
+
+class Under:
+    def __init__(self, place, moves):
+        self.place, self.moves = place, moves
+        self.z = [move for kind, move in moves if move.along_z]
+        self.y = [move for kind, move in moves if not move.along_z and not isinstance(kind, int)]
+        self.follow = [(moves[kind][1], move) for kind, move in moves if isinstance(kind, int)]
+
+    def start_y(self):
+        for move in self.y:
+            move.start()
+
+    def start_z(self, outer=None):
+        def start():
+            for move in self.z:
+                move.start()
+
+        if outer is None:
+            start()
+        else:
+            pl.when(self.place.outer if outer else jnp.logical_not(self.place.outer))(start)
+
+    def start_follow(self):
+        for ahead, move in self.follow:
+            ahead.wait_recv()
+            move.start()
+
+    def end(self, skip=0):
+        done = [ahead for ahead, _ in self.follow]
+        for _, move in self.moves[skip:]:
+            if move not in done:
+                move.wait_recv()
+
+
+def comm_call(
+    body, name, ident, inputs, outs, scratch, moves=(), flops=0, transcendentals=0, spaces=None, greet=None
+):
+    n_in, n_out, n_move = len(inputs), len(outs), len(moves)
+    own_source = [i for i, (kind, _) in enumerate(moves) if not isinstance(kind, int)]
+
+    def kernel(*refs):
+        ins, refs = refs[:n_in], refs[n_in:]
+        sources, refs = refs[:len(own_source)], refs[len(own_source):]
+        results, refs = refs[:n_out], refs[n_out:]
+        targets, refs = refs[:n_move], refs[n_move:]
+        sems, rest = refs[0], refs[1:]
+        place = Place()
+        place.meet(greet)
+        made = []
+        for i, (kind, _) in enumerate(moves):
+            if isinstance(kind, int):
+                made.append((kind, Beyond(place, targets[kind], targets[i], sems.at[i])))
+            else:
+                made.append((kind, KINDS[kind](place, sources[own_source.index(i)], targets[i], sems.at[i])))
+        body(place, ins, results, rest, Under(place, made), targets)
+        for _, move in made:
+            move.wait_send()
+
+    arrays = [*inputs, *(moves[i][1] for i in own_source)]
+    shapes = list(outs)
+    moved = []
+    for kind, array in moves:
+        moved.append(moved[kind] if isinstance(kind, int) else moved_shape(kind, array))
+    shapes += moved
+    in_specs = (spaces or [VMEM_WHOLE] * n_in) + [ANYWHERE] * len(own_source)
+    size = sum(s.size * s.dtype.itemsize for s in (*arrays, *shapes))
+    result = pl.pallas_call(
+        kernel,
+        out_shape=shapes,
+        in_specs=in_specs,
+        out_specs=[VMEM_WHOLE] * (n_out + n_move),
+        scratch_shapes=[DMA((max(n_move, 1), 4)), *scratch],
+        compiler_params=pltpu.CompilerParams(collective_id=ident, has_side_effects=True, vmem_limit_bytes=63 << 20),
+        cost_estimate=pl.CostEstimate(
+            flops=flops + (20 << 30), bytes_accessed=size, transcendentals=transcendentals
+        ),
+        name=name,
+    )(*arrays)
+    return result[:n_out], result[n_out:]
+
+
+def each_rows(count, body, size=32):
+    def step(i, carry):
+        body(span(i * size, size))
+        return carry
+
+    lax.fori_loop(0, count // size, step, 0)
+
+
+def row_norm(values):
+    center = values - jnp.mean(values, axis=-1, keepdims=True)
+    inv_std = lax.rsqrt(jnp.mean(center * center, axis=-1, keepdims=True) + EPSILON)
+    return center * inv_std, inv_std
+
+
+SLICES = 4
+
+
+def reduce_scratch(piece, width):
+    return [
+        pltpu.VMEM((4, piece, width), BF),
+        pltpu.VMEM((4, piece, width), BF),
+        pltpu.VMEM((2, piece, width), F32),
+        pltpu.VMEM((3, piece, width), BF),
+        pltpu.VMEM((3, piece, width), BF),
+        DMA((4,)), DMA((4,)), DMA((3, SLICES)), DMA((3, SLICES)),
+    ]
+
+
+def reduce_body(place, compute, last, scratch, under, started=False, before_wait=None):
+    sib_out, sib_in, own, near_out, near_in, sib_send, sib_recv, near_send, near_recv = scratch
+    piece = own.shape[1]
+    c = place.c
+    if not started:
+        under.start_y()
+        under.start_z(outer=True)
+
+    def sib_copy(step):
+        return remote(sib_out.at[step], sib_in.at[step], sib_send.at[step], sib_recv.at[step], place.sibling)
+
+    size = piece // SLICES
+
+    def near_copy(step, r):
+        device = place.along if step == 2 else place.across
+        rows = span(r * size, size)
+        return remote(
+            near_out.at[step, rows], near_in.at[step, rows], near_send.at[step, r], near_recv.at[step, r], device
+        )
+
+    def finish(step):
+        slot = step % 2
+        sib_copy(step).wait_recv()
+
+        def send(r, carry):
+            if step == 2:
+                near_copy(0, r).wait_recv()
+            rows = span(r * size, size)
+            total = own[slot, rows, :] + sib_in[step, rows, :].astype(F32)
+            if step == 2:
+                total = total + near_in[0, rows, :].astype(F32)
+            near_out[step, rows, :] = total.astype(BF)
+            near_copy(step, r).start()
+            return carry
+
+        lax.fori_loop(0, SLICES, send, 0)
+
+    def step(s, carry):
+        target = place.chip(1 - lax.rem(s, 2), 1 - s // 2)
+        compute((1 - c) * 4 + target, sib_out.at[s])
+        sib_copy(s).start()
+        for index in (0, 1):
+            @pl.when(s == index + 1)
+            def _(index=index):
+                finish(index)
+
+        compute(c * 4 + target, own.at[lax.rem(s, 2)])
+        return carry
+
+    lax.fori_loop(0, 4, step, 0)
+    finish(2)
+    if not started:
+        under.start_z(outer=False)
+        under.start_follow()
+    if before_wait:
+        before_wait()
+    sib_copy(3).wait_recv()
+
+    def arrive(r, carry):
+        near_copy(1, r).wait_recv()
+        near_copy(2, r).wait_recv()
+
+        def final(i, carry):
+            rows = span(r * size + i * 16, 16)
+            total = own[1, rows, :] + sib_in[3, rows, :].astype(F32)
+            last(rows, total + near_in[1, rows, :].astype(F32) + near_in[2, rows, :].astype(F32))
+            return carry
+
+        return lax.fori_loop(0, size // 16, final, carry)
+
+    lax.fori_loop(0, SLICES, arrive, 0)
+    for s in range(4):
+        sib_copy(s).wait_send()
+
+    def sent(r, carry):
+        for s in range(3):
+            near_copy(s, r).wait_send()
+        return carry
+
+    lax.fori_loop(0, SLICES, sent, 0)
+    under.end()
+
+
+def product(place, left_ref, weights, transposed):
+    def compute(owner, out_ref):
+        piece = out_ref.shape[0]
+        left = left_ref[span(owner * piece, piece), :]
+        for weight, index in zip(weights, place.order):
+            size = weight.shape[0] if transposed else weight.shape[1]
+            part = dot(left, weight[...], NT if transposed else NN)
+            out_ref[:, span(index * size, size)] = part.astype(out_ref.dtype)
+
+    return compute
+
+
+def back_rows(base, value, total):
+    normed, inv_std = row_norm(value)
+    mean_grad = jnp.mean(total, axis=-1, keepdims=True)
+    mean_cross = jnp.mean(total * normed, axis=-1, keepdims=True)
+    return base + inv_std * (total - mean_grad - normed * mean_cross)
+
+
+def quarters(first, second):
+    return [first.at[0], first.at[1], second.at[0], second.at[1]]
+
+
+def branch_call(mixed, halves, own_in, moves, ident):
+    piece, width = own_in.shape
+
+    def body(place, ins, outs, scratch, under, targets):
+        mixed_ref, first, second, base_ref = ins
+        total_ref, norm_ref = outs
+
+        def last(rows, total):
+            middle = base_ref[rows, :].astype(F32) + total
+            total_ref[rows, :] = middle
+            norm_ref[rows, :] = row_norm(middle)[0].astype(BF)
+
+        reduce_body(place, product(place, mixed_ref, quarters(first, second), False), last, scratch, under)
+
+    shape = functools.partial(jax.ShapeDtypeStruct, (piece, width))
+    return comm_call(
+        body, "reduce_branch", ident, [mixed, *halves, own_in], [shape(F32), shape(BF)],
+        reduce_scratch(piece, width), moves, flops=2 * mixed.size * width,
+    )
+
+
+def down_call(hidden, firsts, seconds, middle, moves, ident):
+    piece, width = middle.shape
+
+    def body(place, ins, outs, scratch, under, targets):
+        hidden_ref, first_a, first_b, second_a, second_b, base_ref = ins
+        parts = list(zip(quarters(first_a, second_a), quarters(first_b, second_b), place.order))
+
+        def compute(owner, out_ref):
+            rows = span(owner * piece, piece)
+            for upper, lower, index in parts:
+                depth, size = upper.shape
+                part = dot(hidden_ref[rows, 0:depth], upper[...], NN) + dot(hidden_ref[rows, depth:], lower[...], NN)
+                out_ref[:, span(index * size, size)] = part.astype(out_ref.dtype)
+
+        def last(rows, total):
+            outs[0][rows, :] = (base_ref[rows, :] + total).astype(BF)
+
+        reduce_body(place, compute, last, scratch, under)
+
+    return comm_call(
+        body, "reduce_down", ident, [hidden, *firsts, *seconds, middle], [jax.ShapeDtypeStruct((piece, width), BF)],
+        reduce_scratch(piece, width), moves, flops=2 * hidden.size * width,
+    )
+
+
+def input_call(grad_rows, halves, grad_middle, own_in, ready, moves, ident):
+    piece, width = own_in.shape
+
+    def body(place, ins, outs, scratch, under, targets):
+        rows_ref, first, second, base_ref, value_ref, ready_ref = ins
+        spread = Spread(place, ready_ref, outs[1], scratch[:3])
+
+        def last(rows, total):
+            outs[0][rows, :] = back_rows(base_ref[rows, :], value_ref[rows, :].astype(F32), total).astype(BF)
+
+        reduce_body(
+            place, product(place, rows_ref, quarters(first, second), True), last, scratch[3:], under,
+            before_wait=spread.start,
+        )
+        spread.wait()
+
+    return comm_call(
+        body, "reduce_input", ident, [grad_rows, *halves, grad_middle, own_in, ready],
+        [jax.ShapeDtypeStruct((piece, width), BF), spread_shape(ready)],
+        [*spread_scratch(), *reduce_scratch(piece, width)], moves, flops=2 * grad_rows.size * width,
+        greet=spread_greet,
+    )
+
+
+def middle_call(cot, slopes, gates, ups, downs, down_last, moves, middle, ident):
+    piece, width = middle.shape
+    tokens, part_width = cot.shape[0], down_last.shape[1]
+    hidden = 2 * part_width
+    tile = 256
+    tiles = part_width // tile
+
+    def body(place, ins, outs, scratch, under, targets):
+        cot_ref, slopes_ref, ga1, ga2, gb1, gb2, ua1, ua2, ub1, ub2, value_ref, da1, da2, db1 = ins
+        total_ref, branch_ref, grad_ref = outs
+        load_sem, *rest = scratch
+        under.start_y()
+        load = pltpu.make_async_copy(slopes_ref, grad_ref, load_sem.at[0])
+        load.start()
+        load.wait()
+        rows_in = (quarters(da1, da2), quarters(db1, targets[0]))
+
+        def fill(owner, part):
+            rows = span(owner * piece, piece)
+
+            def step(t, carry):
+                grad = None
+                for weight, index in zip(rows_in[part], place.order):
+                    size = weight.shape[1]
+                    term = dot(cot_ref[rows, span(index * size, size)], weight[span(t * tile, tile), :], NT)
+                    grad = term if grad is None else grad + term
+                for offset in (0, hidden):
+                    cols = span(offset + part * part_width + t * tile, tile)
+                    grad_ref[rows, cols] = (grad * grad_ref[rows, cols].astype(F32)).astype(BF)
+                return carry
+
+            lax.fori_loop(0, tiles, step, 0)
+
+        def fill_first(i, carry):
+            fill(i, 0)
+            return carry
+
+        lax.fori_loop(0, tokens // piece, fill_first, 0)
+        under.moves[0][1].wait_recv()
+        columns = [quarters(ga1, ga2), quarters(gb1, gb2), quarters(ua1, ua2), quarters(ub1, ub2)]
+
+        def compute(owner, out_ref):
+            rows = span(owner * piece, piece)
+            fill(owner, 1)
+            for quarter, index in enumerate(place.order):
+                total = None
+                for i, weights in enumerate(columns):
+                    weight = weights[quarter]
+                    size = weight.shape[0]
+                    term = dot(grad_ref[rows, i * part_width:(i + 1) * part_width], weight[...], NT)
+                    total = term if total is None else total + term
+                out_ref[:, span(index * size, size)] = total.astype(out_ref.dtype)
+
+        def last(rows, total):
+            base = cot_ref[own_rows(rows), :].astype(F32)
+            grad = back_rows(base, value_ref[rows, :], total)
+            total_ref[rows, :] = grad
+            branch_ref[rows, :] = grad.astype(BF)
+
+        def own_rows(rows):
+            return pl.ds(pl.multiple_of(place.block * piece + rows.start, 16), rows.size)
+
+        reduce_body(place, compute, last, rest, Under(place, under.moves[1:]), started=True)
+
+    shape = functools.partial(jax.ShapeDtypeStruct, (piece, width))
+    return comm_call(
+        body, "reduce_middle", ident, [cot, slopes, *gates, *ups, middle, *downs, down_last],
+        [shape(F32), shape(BF), jax.ShapeDtypeStruct((tokens, 2 * hidden), BF)],
+        [DMA((1,)), *reduce_scratch(piece, width)],
+        moves, flops=6 * tokens * hidden * width,
+        spaces=[VMEM_WHOLE, ANYWHERE] + [VMEM_WHOLE] * 12,
+    )
+
+
+def gather_scratch():
+    return [DMA((3, SLICES)), DMA((3, SLICES)), DMA((4,)), DMA((4,))]
+
+
+def gather_body(place, own_ref, full, sems, process, under):
+    near_send, near_recv, sib_send, sib_recv = sems
+    piece = own_ref.shape[0]
+    size = piece // SLICES
+    c = place.c
+
+    def near_copy(slot, r, target):
+        where = full.at[span((c * 4 + target) * piece + r * size, size)]
+        device = place.along if slot == 2 else place.across
+        return remote(where, where, near_send.at[slot, r], near_recv.at[slot, r], device)
+
+    def sib_copy(slot, core, target):
+        where = full.at[span((core * 4 + target) * piece, piece)]
+        return remote(where, where, sib_send.at[slot], sib_recv.at[slot], place.sibling)
+
+    def slices(act):
+        def step(r, carry):
+            act(r)
+            return carry
+
+        lax.fori_loop(0, SLICES, step, 0)
+
+    mine, x_chip, z_chip, d_chip = place.chip(0, 0), place.chip(0, 1), place.chip(1, 0), place.chip(1, 1)
+    full[span((c * 4 + mine) * piece, piece), :] = own_ref[...]
+    slices(lambda r: near_copy(2, r, mine).start())
+    slices(lambda r: near_copy(1, r, mine).start())
+    sib_copy(3, c, mine).start()
+    under.start_y()
+    under.start_z()
+
+    def forward(r):
+        near_copy(2, r, z_chip).wait_recv()
+        near_copy(0, r, z_chip).start()
+
+    process(c * 4 + mine)
+    forward(0)
+    sib_copy(3, 1 - c, mine).wait_recv()
+    process((1 - c) * 4 + mine)
+    forward(1)
+    slices(lambda r: near_copy(1, r, x_chip).wait_recv())
+    sib_copy(1, c, x_chip).start()
+    process(c * 4 + x_chip)
+    for r in range(2, SLICES):
+        forward(r)
+    sib_copy(2, c, z_chip).start()
+    sib_copy(1, 1 - c, x_chip).wait_recv()
+    process((1 - c) * 4 + x_chip)
+    process(c * 4 + z_chip)
+    under.start_follow()
+    sib_copy(2, 1 - c, z_chip).wait_recv()
+    process((1 - c) * 4 + z_chip)
+    slices(lambda r: near_copy(0, r, d_chip).wait_recv())
+    sib_copy(0, c, d_chip).start()
+    process(c * 4 + d_chip)
+    sib_copy(0, 1 - c, d_chip).wait_recv()
+    process((1 - c) * 4 + d_chip)
+    for slot in range(3):
+        slices(lambda r: near_copy(slot, r, mine).wait_send())
+    for slot in range(4):
+        sib_copy(slot, c, mine).wait_send()
+
+
+def feed_call(own, tokens, gates, ups, up_last, moves, ident):
+    piece, width = own.shape
+    part = up_last.shape[2]
+    hidden = 2 * part
+    tile = 256
+    tiles = part // tile
+
+    def body(place, ins, outs, scratch, under, targets):
+        own_ref, ga1, ga2, gb1, gb2, ua1, ua2, ub1 = ins
+        full, hidden_ref, slopes_ref = outs
+        columns = (
+            (quarters(ga1, ga2), quarters(ua1, ua2)),
+            (quarters(gb1, gb2), quarters(ub1, targets[0])),
+        )
+        waiting = []
+
+        def fill(owner, which):
+            rows = span(owner * piece, piece)
+            gates, ups = columns[which]
+
+            def step(t, carry):
+                taken = span(t * tile, tile)
+                gate = up = None
+                for gate_weight, up_weight, index in zip(gates, ups, place.order):
+                    size = gate_weight.shape[0]
+                    normed = full[rows, span(index * size, size)]
+                    terms = dot(normed, gate_weight[:, taken], NN), dot(normed, up_weight[:, taken], NN)
+                    gate, up = terms if gate is None else (gate + terms[0], up + terms[1])
+                cols, up_cols = span(which * part + t * tile, tile), span(hidden + which * part + t * tile, tile)
+                sig = 1.0 / (1.0 + jnp.exp(-gate))
+                active = gate * sig
+                hidden_ref[rows, cols] = (active * up).astype(BF)
+                slopes_ref[rows, cols] = (up * sig * (1.0 + gate * (1.0 - sig))).astype(BF)
+                slopes_ref[rows, up_cols] = active.astype(BF)
+                return carry
+
+            lax.fori_loop(0, tiles, step, 0)
+
+        def process(owner):
+            fill(owner, 0)
+            waiting.append(owner)
+            if len(waiting) == 3:
+                under.moves[0][1].wait_recv()
+                for earlier in waiting:
+                    fill(earlier, 1)
+            elif len(waiting) > 3:
+                fill(owner, 1)
+
+        gather_body(place, own_ref, full, scratch, process, under)
+        under.end(skip=1)
+
+    return comm_call(
+        body, "gather_feed", ident, [own, *gates, *ups, up_last],
+        [
+            jax.ShapeDtypeStruct((tokens, width), BF),
+            jax.ShapeDtypeStruct((tokens, hidden), BF),
+            jax.ShapeDtypeStruct((tokens, 2 * hidden), BF),
+        ],
+        gather_scratch(),
+        moves, flops=4 * tokens * hidden * width, transcendentals=tokens * hidden,
+    )
+
+
+def mix_call(own, halves, tokens, moves, ident):
+    width = own.shape[1]
+    inner = halves[0].shape[1]
+
+    def body(place, ins, outs, scratch, under, targets):
+        own_ref, first, second = ins
+        full, mixed_ref = outs
+        piece = own_ref.shape[0]
+
+        def process(owner):
+            rows = span(owner * piece, piece)
+            total = None
+            for weight, index in zip(quarters(first, second), place.order):
+                size = weight.shape[1]
+                part = dot(full[rows, span(index * size, size)], weight[...], NT)
+                total = part if total is None else total + part
+            mixed_ref[rows, :] = total.astype(BF)
+
+        gather_body(place, own_ref, full, scratch, process, under)
+        under.end()
+
+    return comm_call(
+        body, "gather_mix", ident, [own, *halves],
+        [jax.ShapeDtypeStruct((tokens, width), BF), jax.ShapeDtypeStruct((tokens, inner), BF)],
+        gather_scratch(), moves, flops=2 * tokens * inner * width,
+    )
+
+
+class ColumnGather:
+    def __init__(self, place, src, full, sems):
+        self.place, self.src, self.full = place, src, full
+        self.near_send, self.near_recv, self.sib_send, self.sib_recv, self.own = sems
+        self.width = src.shape[1]
+        self.size = src.shape[0] // SLICES
+
+    def where(self, core, target):
+        return span((core * 4 + target) * self.width, self.width)
+
+    def near(self, slot, r, target, first=False):
+        place = self.place
+        rows = pl.ds(r * self.size, self.size)
+        dst = self.full.at[rows, self.where(place.c, target)]
+        src = self.src.at[rows] if first else dst
+        device = place.along if slot == 2 else place.across
+        return remote(src, dst, self.near_send.at[slot, r], self.near_recv.at[slot, r], device)
+
+    def sib(self, slot, core, target, first=False):
+        dst = self.full.at[:, self.where(core, target)]
+        src = self.src if first else dst
+        return remote(src, dst, self.sib_send.at[slot], self.sib_recv.at[slot], self.place.sibling)
+
+    def chips(self):
+        place = self.place
+        return place.chip(0, 0), place.chip(0, 1), place.chip(1, 0), place.chip(1, 1)
+
+    def own_copy(self):
+        return pltpu.make_async_copy(self.src, self.full.at[:, self.where(self.place.c, self.chips()[0])], self.own.at[0])
+
+    def start(self):
+        mine = self.chips()[0]
+        self.own_copy().start()
+        for slot in (2, 1):
+            for r in range(SLICES):
+                self.near(slot, r, mine, True).start()
+        self.sib(3, self.place.c, mine, True).start()
+
+    def forward(self, r):
+        z_chip = self.chips()[2]
+        self.near(2, r, z_chip).wait_recv()
+        self.near(0, r, z_chip).start()
+
+    def finish(self):
+        mine, x_chip, z_chip, d_chip = self.chips()
+        c = self.place.c
+        self.sib(2, c, z_chip).start()
+        for r in range(SLICES):
+            self.near(1, r, x_chip).wait_recv()
+        self.sib(1, c, x_chip).start()
+        for r in range(SLICES):
+            self.near(0, r, d_chip).wait_recv()
+        self.sib(0, c, d_chip).start()
+        self.own_copy().wait()
+        for slot, target in enumerate((d_chip, x_chip, z_chip, mine)):
+            self.sib(slot, 1 - c, target).wait_recv()
+            self.sib(slot, c, mine).wait_send()
+        for slot in range(3):
+            for r in range(SLICES):
+                self.near(slot, r, mine).wait_send()
+
+
+def attend_call(qkv, prefix, cot_block, heads, hd, moves, ident):
+    seq = qkv.shape[0]
+    bq = bk = min(512, seq // 2)
+    scale = hd ** -0.5
+
+    def body(place, ins, outs, scratch, under, targets):
+        qkv_ref, prefix_ref, block_ref = ins
+        mixed_ref, lse_ref, cot_ref = outs
+        gather = ColumnGather(place, block_ref, cot_ref, scratch)
+        gather.start()
+        under.start_y()
+        under.start_z()
+        bound = prefix_ref[0:1, 0:1]
+
+        def head(h):
+            base = h * 3 * hd
+            for i in range(seq // bq):
+                first = i * bq
+                q = qkv_ref[first:first + bq, base:base + hd]
+                total = max(i + 1, seq // 2 // bk)
+
+                def step(masked, j, state, first=first, q=q):
+                    top, tot, acc = state
+                    rows = span(j * bk, bk)
+                    s = dot(q, qkv_ref[rows, base + hd:base + 2 * hd], NT) * scale
+                    if masked:
+                        kp = j * bk + lax.broadcasted_iota(jnp.int32, (bq, bk), 1)
+                        qp = first + lax.broadcasted_iota(jnp.int32, (bq, bk), 0)
+                        s = jnp.where(kp < jnp.maximum(qp + 1, bound), s, NEG)
+                    new = jnp.maximum(top, jnp.max(s, axis=1, keepdims=True))
+                    alpha = jnp.exp(top - new)
+                    p = jnp.exp(s - new)
+                    tot = tot * alpha + jnp.sum(p, axis=1, keepdims=True)
+                    acc = acc * alpha + dot(p.astype(BF), qkv_ref[rows, base + 2 * hd:base + 3 * hd], NN)
+                    return new, tot, acc
+
+                state = (jnp.full((bq, 1), NEG, F32), jnp.zeros((bq, 1), F32), jnp.zeros((bq, hd), F32))
+                state = lax.fori_loop(0, i, functools.partial(step, False), state)
+                top, tot, acc = lax.fori_loop(i, total, functools.partial(step, True), state)
+                mixed_ref[first:first + bq, h * hd:(h + 1) * hd] = (acc / tot).astype(BF)
+                lse = jnp.broadcast_to(top + jnp.log(tot), (bq, 128))
+                lse_ref[h, :, first:first + bq] = lse.T[0:8, :]
+
+        passed = 0
+        for h in range(heads):
+            head(h)
+            if passed < SLICES:
+                gather.forward(passed)
+                passed += 1
+        under.start_follow()
+        for r in range(passed, SLICES):
+            gather.forward(r)
+        gather.finish()
+        under.end()
+
+    return comm_call(
+        body, "attend", ident, [qkv, prefix, cot_block],
+        [
+            jax.ShapeDtypeStruct((seq, heads * hd), BF),
+            jax.ShapeDtypeStruct((heads, 8, seq), F32),
+            jax.ShapeDtypeStruct((seq, cot_block.shape[1] * 8), BF),
+        ],
+        [DMA((3, SLICES)), DMA((3, SLICES)), DMA((4,)), DMA((4,)), DMA((1,))],
+        moves, flops=4 * heads * seq * seq * hd, transcendentals=heads * seq * seq,
+    )
+
+
+def attend_back_call(qkv, mixed, grad_mixed, lse, prefix, tables, heads, hd, moves, ident):
+    seq = qkv.shape[0]
+    bq = bk = min(512, seq // 2)
+    scale = hd ** -0.5
+    half = hd // 2
+
+    def body(place, ins, outs, scratch, under, targets):
+        qkv_ref, o_ref, do_ref, lse_ref, prefix_ref, cos_ref, sin_ref = ins
+        (out_ref,) = outs
+        under.start_y()
+        under.start_z()
+        dk_ref, dv_ref = scratch
+        bound = prefix_ref[0:1, 0:1]
+
+        def unrotate(g, rows):
+            return g * cos_ref[rows, :] - pltpu.roll(g, half, 1) * sin_ref[rows, :]
+
+        def head(h, carry):
+            base = h * 3 * hd
+            own = span(h * hd, hd)
+            dk_ref[...] = jnp.zeros_like(dk_ref)
+            dv_ref[...] = jnp.zeros_like(dv_ref)
+            for i in range(seq // bq):
+                first = i * bq
+                rows = pl.ds(first, bq)
+                q = qkv_ref[rows, span(base, hd)]
+                do = do_ref[rows, own]
+                row_sums = (do.astype(F32) * o_ref[rows, own].astype(F32)).T
+                delta = jnp.sum(row_sums, axis=0, keepdims=True)
+                tops = lse_ref[h, 0:1, first:first + bq]
+                total = max(i + 1, seq // 2 // bk)
+
+                def step(masked, j, dq, first=first, q=q, do=do, delta=delta, tops=tops):
+                    keys = span(j * bk, bk)
+                    k = qkv_ref[keys, span(base + hd, hd)]
+                    v = qkv_ref[keys, span(base + 2 * hd, hd)]
+                    p = jnp.exp(dot(k, q, NT) * scale - tops)
+                    if masked:
+                        kp = j * bk + lax.broadcasted_iota(jnp.int32, (bk, bq), 0)
+                        qp = first + lax.broadcasted_iota(jnp.int32, (bk, bq), 1)
+                        p = jnp.where(kp < jnp.maximum(qp + 1, bound), p, 0.0)
+                    dv_ref[keys, :] += dot(p.astype(BF), do, NN)
+                    ds = (p * (dot(v, do, NT) - delta)).astype(BF)
+                    dk_ref[keys, :] += dot(ds, q, NN)
+                    return dq + dot(ds, k, TN)
+
+                dq = lax.fori_loop(0, i, functools.partial(step, False), jnp.zeros((bq, hd), F32))
+                dq = lax.fori_loop(i, total, functools.partial(step, True), dq)
+                out_ref[rows, span(base, hd)] = unrotate(dq * scale, rows).astype(BF)
+
+            def fin(i, carry):
+                rows = span(i * bq, bq)
+                out_ref[rows, span(base + hd, hd)] = unrotate(dk_ref[rows, :] * scale, rows).astype(BF)
+                out_ref[rows, span(base + 2 * hd, hd)] = dv_ref[rows, :].astype(BF)
+                return carry
+
+            return lax.fori_loop(0, seq // bq, fin, carry)
+
+        lax.fori_loop(0, heads, head, 0)
+        under.start_follow()
+        under.end()
+
+    return comm_call(
+        body, "attend_back", ident, [qkv, mixed, grad_mixed, lse, prefix, *tables],
+        [jax.ShapeDtypeStruct(qkv.shape, BF)],
+        [pltpu.VMEM((seq, hd), F32), pltpu.VMEM((seq, hd), F32)],
+        moves, flops=10 * heads * seq * seq * hd, transcendentals=heads * seq * seq,
+    )
+
+
+def start_call(inputs, cot, tables, moves, heads, hd, ident):
+    tokens, slice_width = inputs.shape
+    width = slice_width * 8
+    piece = tokens // 8
+    chunks = 4
+    size = tokens // chunks
+    half = size // 2
+
+    def body(place, ins, outs, scratch, under, targets):
+        in_ref, cot_ref, cos_ref, sin_ref = ins
+        qkv_ref, normed_ref, own_ref, block_ref, second_qkv, second_out = outs
+        (full, total_ref, swap_send, swap_recv, near_send, near_recv, diag_send, diag_recv, sib_send, sib_recv,
+         y_sems) = scratch
+        c, zl, x = place.c, place.zl, place.x
+        crossed = jnp.logical_not(place.straight)
+        partner = (place.y, 1 - c, 1 - place.zh, zl, x)
+
+        def columns(core, target):
+            return span((core * 4 + target) * slice_width, slice_width)
+
+        mine = place.chip(0, 0)
+        x_chip, z_chip, d_chip = place.chip(0, 1), place.chip(1, 0), place.chip(1, 1)
+
+        def rows_of(r):
+            return pl.ds(r * size, size)
+
+        def swap_copy(r, core):
+            return remote(
+                in_ref.at[rows_of(r)], full.at[rows_of(r), columns(core, mine)], swap_send.at[r], swap_recv.at[r], partner
+            )
+
+        def own_copy(r):
+            return pltpu.make_async_copy(in_ref.at[rows_of(r)], full.at[rows_of(r), columns(c, mine)], swap_send.at[r])
+
+        def cot_swap():
+            return remote(cot_ref, block_ref, swap_send.at[chunks], swap_recv.at[chunks], partner)
+
+        def cot_own():
+            return pltpu.make_async_copy(cot_ref, block_ref, swap_send.at[chunks])
+
+        def near_copy(part, r, target):
+            where = full.at[rows_of(r), columns(c, target)]
+            device = place.across if part == 0 else place.along
+            return remote(where, where, near_send.at[part, r], near_recv.at[part, r], device)
+
+        def diag_copy(r, target):
+            where = full.at[rows_of(r), columns(c, target)]
+            return remote(where, where, diag_send.at[r], diag_recv.at[r], place.across)
+
+        def sib_copy(slot, r, core, target):
+            where = full.at[rows_of(r), columns(core, target)]
+            return remote(where, where, sib_send.at[slot, r], sib_recv.at[slot, r], place.sibling)
+
+        @pl.when(place.straight)
+        def _():
+            for r in range(chunks):
+                own_copy(r).start()
+            cot_own().start()
+
+        @pl.when(crossed)
+        def _():
+            for r in range(chunks):
+                swap_copy(r, 1 - c).start()
+
+        for r in range(chunks):
+            @pl.when(place.straight)
+            def _(r=r):
+                own_copy(r).wait()
+
+            @pl.when(crossed)
+            def _(r=r):
+                swap_copy(r, c).wait_recv()
+
+            near_copy(0, r, mine).start()
+            near_copy(1, r, mine).start()
+            sib_copy(0, r, c, mine).start()
+        for r in range(chunks):
+            near_copy(1, r, z_chip).wait_recv()
+            diag_copy(r, z_chip).start()
+            sib_copy(2, r, c, z_chip).start()
+            near_copy(0, r, x_chip).wait_recv()
+            sib_copy(1, r, c, x_chip).start()
+            if r == 0:
+                under.moves[0][1].start()
+
+        under.moves[0][1].wait_recv()
+        under.moves[1][1].start()
+        pl.when(crossed)(lambda: cot_swap().start())
+        beyond_qkv = Beyond(place, targets[0], second_qkv, y_sems.at[0])
+        beyond_qkv.start()
+        firsts = [targets[0].at[0], targets[0].at[1]]
+        seconds = [second_qkv.at[0], second_qkv.at[1]]
+        depth = firsts[0].shape[0]
+        for r in range(chunks):
+            diag_copy(r, d_chip).wait_recv()
+            sib_copy(3, r, c, d_chip).start()
+            for slot, target in enumerate((mine, x_chip, z_chip, d_chip)):
+                sib_copy(slot, r, 1 - c, target).wait_recv()
+
+            def norm_rows(i, carry, r=r):
+                rows = span(r * size + i * 16, 16)
+                normed_ref[rows, :] = row_norm(full[rows, :].astype(F32))[0].astype(BF)
+                return carry
+
+            lax.fori_loop(0, size // 16, norm_rows, 0)
+            rows = rows_of(r)
+            total = None
+            for weight, index in zip(firsts, place.order[:2]):
+                term = dot(normed_ref[rows, span(index * depth, depth)], weight[...], NN)
+                total = term if total is None else total + term
+            total_ref[rows, :] = total
+        own_ref[...] = full[span(place.block * piece, piece), :]
+        under.moves[1][1].wait_recv()
+        beyond_out = Beyond(place, targets[1], second_out, y_sems.at[1])
+        beyond_out.start()
+        beyond_qkv.wait_recv()
+
+        def project(r, carry):
+            rows = span(r * half, half)
+            total = total_ref[rows, :]
+            for weight, index in zip(seconds, place.order[2:]):
+                total = total + dot(normed_ref[rows, span(index * depth, depth)], weight[...], NN)
+            cos, sin = cos_ref[rows, :], sin_ref[rows, :]
+            for h in range(heads):
+                for part in range(3):
+                    cols = pl.ds((3 * h + part) * hd, hd)
+                    value = total[:, (3 * h + part) * hd:(3 * h + part + 1) * hd]
+                    if part < 2:
+                        value = value * cos + pltpu.roll(value, hd // 2, 1) * sin
+                    qkv_ref[rows, cols] = value.astype(BF)
+            return carry
+
+        lax.fori_loop(0, tokens // half, project, 0)
+        beyond_out.wait_recv()
+
+        @pl.when(place.straight)
+        def _():
+            cot_own().wait()
+
+        @pl.when(crossed)
+        def _():
+            cot_swap().wait_recv()
+            cot_swap().wait_send()
+            for r in range(chunks):
+                swap_copy(r, 1 - c).wait_send()
+
+        beyond_qkv.wait_send()
+        beyond_out.wait_send()
+        for r in range(chunks):
+            near_copy(0, r, mine).wait_send()
+            near_copy(1, r, mine).wait_send()
+            diag_copy(r, z_chip).wait_send()
+            for slot in range(4):
+                sib_copy(slot, r, c, mine).wait_send()
+
+    qkv_half, out_half = (moved_shape(kind, array) for kind, array in moves)
+    inner = qkv_half.shape[2]
+    return comm_call(
+        body, "start", ident, [inputs, cot, *tables],
+        [
+            jax.ShapeDtypeStruct((tokens, inner), BF),
+            jax.ShapeDtypeStruct((tokens, width), BF),
+            jax.ShapeDtypeStruct((piece, width), BF),
+            jax.ShapeDtypeStruct(cot.shape, BF),
+            qkv_half,
+            out_half,
+        ],
+        [
+            pltpu.VMEM((tokens, width), BF), pltpu.VMEM((tokens, inner), F32),
+            DMA((chunks + 1,)), DMA((chunks + 1,)), DMA((2, chunks)), DMA((2, chunks)), DMA((chunks,)),
+            DMA((chunks,)), DMA((4, chunks)), DMA((4, chunks)), DMA((2, 4)),
+        ],
+        moves, flops=2 * tokens * width * inner,
+        spaces=[ANYWHERE, ANYWHERE, VMEM_WHOLE, VMEM_WHOLE],
+    )
+
+
+BLOCKS = [(core, zl, x) for core in (0, 1) for zl in (0, 1) for x in (0, 1)]
+
+
+def spread_greet(place, barrier):
+    for core, zl, x in BLOCKS:
+        mine = jnp.logical_and(place.straight, core * 4 + zl * 2 + x == place.block)
+
+        @pl.when(jnp.logical_not(mine))
+        def _(core=core, zl=zl, x=x):
+            pl.semaphore_signal(
+                barrier, inc=1, device_id=(place.y, core, place.c, zl, x), device_id_type=MESH
+            )
+
+    return 8 - jnp.where(place.straight, 1, 0)
+
+
+def spread_scratch():
+    return [DMA((8,)), DMA((8,)), DMA((1,))]
+
+
+def spread_shape(piece):
+    return jax.ShapeDtypeStruct((piece.shape[0] * 8, piece.shape[1] // 8), piece.dtype)
+
+
+class Spread:
+    def __init__(self, place, src, dst, sems):
+        self.place, self.src, self.dst = place, src, dst
+        self.send, self.recv, self.own = sems
+        self.piece, self.width = src.shape[0], src.shape[1] // 8
+
+    def copy(self, f):
+        place = self.place
+        return remote(
+            self.src.at[:, pl.ds(f * self.width, self.width)], self.dst.at[span(place.block * self.piece, self.piece)],
+            self.send.at[f], self.recv.at[place.block], (place.y, place.zh, *BLOCKS[f]),
+        )
+
+    def incoming(self, f):
+        core, zl, x = BLOCKS[f]
+        place = self.place
+        return remote(
+            self.src.at[:, pl.ds(f * self.width, self.width)], self.dst.at[pl.ds(f * self.piece, self.piece)],
+            self.send.at[f], self.recv.at[f], (place.y, core, place.c, zl, x),
+        )
+
+    def own_copy(self):
+        block = self.place.block
+        return pltpu.make_async_copy(
+            self.src.at[:, span(block * self.width, self.width)], self.dst.at[span(block * self.piece, self.piece)],
+            self.own.at[0],
+        )
+
+    def each(self, act):
+        for f in range(8):
+            mine = jnp.logical_and(self.place.straight, self.place.block == f)
+            pl.when(jnp.logical_not(mine))(functools.partial(act, f))
+
+    def start(self):
+        self.each(lambda f: self.copy(f).start())
+        pl.when(self.place.straight)(lambda: self.own_copy().start())
+
+    def wait(self):
+        self.each(lambda f: self.incoming(f).wait_recv())
+        self.each(lambda f: self.copy(f).wait_send())
+        pl.when(self.place.straight)(lambda: self.own_copy().wait())
+
+
+def finish_call(piece, moves, ident):
+    def body(place, ins, outs, scratch, under, targets):
+        spread = Spread(place, ins[0], outs[0], scratch)
+        spread.start()
+        under.start_z()
+        under.end()
+        spread.wait()
+
+    return comm_call(
+        body, "finish", ident, [piece], [spread_shape(piece)], spread_scratch(), moves, greet=spread_greet,
+    )
+
+
+def local_fine(inputs, prefix_len, w_qkv, w_out, w_up_gate, w_down, cotangent):
+    heads, hd = w_qkv.shape[1], w_qkv.shape[2] // 3
+    hidden_width = w_down.shape[0]
+    tokens = inputs.shape[0]
+    y = lax.axis_index("y")
+    prefix_len = lax.ppermute(prefix_len, ("core", "zh"), [(0, 0), (1, 2), (2, 1), (3, 3)])
+    prefix = jnp.broadcast_to(prefix_len[:, None], (8, 128))
+    cosine, sine = rope_tables(tokens, hd)
+    tables = (jnp.concatenate([cosine, cosine], axis=1), jnp.concatenate([-sine, sine], axis=1))
+    part = hidden_width // 2
+    ga, gb = w_up_gate[:, 0, :part], w_up_gate[:, 0, part:]
+    ua, ub = w_up_gate[:, 1, :part], w_up_gate[:, 1, part:]
+    da, db = w_down[:part], w_down[part:]
+
+    (qkv, normed_in, own_in, cot_block, qkv_2, out_2), (qkv_1, out_1) = start_call(
+        inputs, cotangent, tables, [("weight", w_qkv.reshape(w_qkv.shape[0], -1)), ("weight", w_out)], heads, hd, 1
+    )
+    (mixed, lse, cot_full), (ga_1, gb_1, ga_2) = attend_call(
+        qkv, prefix, cot_block, heads, hd, [("weight", ga), ("weight", gb), (0, None)], 2
+    )
+    (middle, normed_own), (gb_2, ua_1, ub_1, ua_2) = branch_call(
+        mixed, (out_1, out_2), own_in, [("beyond", gb_1), ("weight", ua), ("weight", ub), (1, None)], 3
+    )
+    gates = (ga_1, ga_2, gb_1, gb_2)
+    (normed_mid, hidden, slopes), (ub_2, da_1, db_1, da_2) = feed_call(
+        normed_own, tokens, gates, (ua_1, ua_2), ub_1, [("beyond", ub_1), ("weight", da), ("weight", db), (1, None)], 4
+    )
+
+    def halves(spec, left, right, axis):
+        side = left if axis == 0 else right
+        half = side.shape[1] // 2
+
+        def cut(which):
+            taken = lax.dynamic_slice_in_dim(side, which * half, half, 1)
+            return mm(spec, taken, right) if axis == 0 else mm(spec, left, taken)
+
+        return cut(y), cut(1 - y).astype(BF)
+
+    def joined(own, moved, axis):
+        total = (own + moved.astype(F32)).astype(BF)
+        if axis == 0:
+            return total.reshape(2, total.shape[0] // 2, total.shape[1])
+        return jnp.swapaxes(total.reshape(total.shape[0], 2, total.shape[1] // 2), 0, 1)
+
+    down_own, down_other = halves("tf,td->fd", hidden, cot_full, 1)
+    (grad_middle, branch_own, grad_gate_up), (db_2, down_moved) = middle_call(
+        cot_full, slopes, gates, (ua_1, ua_2, ub_1, ub_2), (da_1, da_2), db_1,
+        [("beyond", db_1), ("beyond", down_other)], middle, 5,
+    )
+    gate_grad, gate_other = halves("td,tf->df", normed_mid, grad_gate_up[:, :hidden_width], 0)
+    up_grad, up_other = halves("td,tf->df", normed_mid, grad_gate_up[:, hidden_width:], 0)
+    (outputs,), (down_final, gate_moved) = down_call(
+        hidden, (da_1, db_1), (da_2, db_2), middle,
+        [("grad", joined(down_own, down_moved, 1)), ("beyond", gate_other)], 6,
+    )
+    (grad_branch, grad_mixed), (gate_final, up_moved) = mix_call(
+        branch_own, (out_1, out_2), tokens,
+        [("grad", joined(gate_grad, gate_moved, 0)), ("beyond", up_other)], 7,
+    )
+    out_grad, out_other = halves("tc,td->cd", mixed, grad_branch, 1)
+    (grad_rows,), (up_final, out_moved) = attend_back_call(
+        qkv, mixed, grad_mixed, lse, prefix, tables, heads, hd,
+        [("grad", joined(up_grad, up_moved, 0)), ("beyond", out_other)], 8,
+    )
+    qkv_grad, qkv_other = halves("td,te->de", normed_in, grad_rows, 0)
+    (input_grad, outputs), (out_final, qkv_moved) = input_call(
+        grad_rows, (qkv_1, qkv_2), grad_middle, own_in, outputs,
+        [("grad", joined(out_grad, out_moved, 1)), ("beyond", qkv_other)], 9,
+    )
+    (input_grad,), (qkv_final,) = finish_call(input_grad, [("grad", joined(qkv_grad, qkv_moved, 0))], 10)
+
+    def summed(parts):
+        return parts[0].astype(F32) + parts[1].astype(F32)
+
+    return (
+        outputs,
+        input_grad.astype(F32),
+        summed(qkv_final).reshape(-1, heads, 3 * hd),
+        summed(out_final),
+        jnp.stack([summed(gate_final), summed(up_final)], axis=1),
+        summed(down_final),
+    )
+
+
 def solution(mesh):
     row_size, col_size = mesh.shape["row"], mesh.shape["col"]
-    col_major = 4
-    shape = (row_size // 2, 2, col_major, col_size // col_major)
-    fine = Mesh(mesh.devices.reshape(shape), ("rmaj", "core", "cmaj", "cmin"))
-    row, col = ("rmaj", "core"), ("cmaj", "cmin")
+    fine = (row_size, col_size) == (4, 8)
+    if fine:
+        names, shape, body = AXES, (2,) * 5, local_fine
+        row, col = AXES[:2], AXES[2:]
+    else:
+        names = ("rmaj", "core", "cmaj", "cmin")
+        shape = (row_size // 2, 2, 4, col_size // 4)
+        body = functools.partial(local, shape[3] == 2)
+        row, col = names[:2], names[2:]
     outs = (P(row, col), P(row, col), P(row, col, None), P(col, row), P(row, None, col), P(col, row))
     return jax.shard_map(
-        functools.partial(local, shape[3] == 2),
-        mesh=fine,
+        body,
+        mesh=Mesh(mesh.devices.reshape(shape), names),
         in_specs=(P(row, col), P(row), P(row, col, None), P(col, row), P(row, None, col), P(col, row), P(row, col)),
         out_specs=outs,
         check_vma=False,

time: 1370 us -> 900 us (0.66)
  waiting for transfers between devices: 987 us -> 0.01 us
  Pallas kernels: 54.4 us -> 767 us
  matrix products: 173 us -> 75 us
  starting transfers between devices: 57.8 us -> 5.74 us
  other arithmetic: 37 us -> 14.1 us
  local copies, waits for them, and re-layouts: 42.6 us -> 28.8 us
    pallas_call x2 -> x10, Pallas kernels: 54.4 us -> 767 us  [comm_call(): pl.pallas_call(kernel, out_shape=shapes, in_specs=in_specs, out_specs=[VM...]
    reduce_scatter x8 -> x0, waiting for transfers between devices: 477 us -> none  [the longest x4 261 us: scatter(): lax.psum_scatter(value.astype(BF), cols, scatter_dimension=0, tiled=True)]
    all_gather x8 -> x0, waiting for transfers between devices: 376 us -> none  [the longest x1 85.1 us: local(): cot_full = lax.all_gather(cotangent, cols, axis=1, tiled=True)]
    ppermute x13 -> x1, waiting for transfers between devices: 135 us -> 0.01 us  [local_fine(): lax.ppermute(prefix_len, ('core', 'zh'), [(0, 0), (1, 2), (2, 1), (3, 3)])]
    dot_general x12 -> x10, matrix products: 173 us -> 75 us  [mm(): return jnp.einsum(spec, left, right, preferred_element_type=F32)]
    ppermute x13 -> x1, starting transfers between devices: 42.1 us -> 5.74 us  [local_fine(): lax.ppermute(prefix_len, ('core', 'zh'), [(0, 0), (1, 2), (2, 1), (3, 3)])]
    reduce_sum x6 -> x0, other arithmetic: 16.7 us -> none  [the longest x2 6.8 us: norm(): center = values - jnp.mean(values, axis=-1, keepdims=True)]
    unnamed x59 -> x31, local copies, waits for them, and re-layouts: 23.8 us -> 8.55 us
  transfers between devices with their start and end apart: 31 -> 1, of which waited for: 21 -> 0; matrix products, arithmetic and copies ran while one was open for 12% -> 2% of each run, Pallas kernels for 2% -> 14%
where the time goes in v3:
time: 900 us; the launch traced here: 891 us
  Pallas kernels  767 us (85%)
  matrix products  75 us (8%)
  local copies, waits for them, and re-layouts  28.8 us (3%)
  other arithmetic  14.1 us (2%)
    pallas_call x10, Pallas kernels, comm_call(): pl.pallas_call(kernel, out_shape=shapes, in_specs=in_specs, out_specs=[VM...  767 us
    dot_general x10, matrix products, mm(): return jnp.einsum(spec, left, right, preferred_element_type=F32)  75 us
  transfers between devices with their start and end apart: 1, of which 0 were waited for; matrix products, arithmetic and copies ran while one was open for 2% of the time, Pallas kernels for 14%

profile of v3, /device:TPU:1, one launch (start us, length us, event | category | flops | bytes accessed | tf_op | source)
XLA Modules:
  0.0 891.3 jit_solution(15790084445488858467)
XLA Ops:
  0.6 5.7 collective-permute-start
  6.4 2.1 copy.34
  8.6 2.2 fusion.73
  10.8 4.2 fusion.72
  15.1 3.7 fusion.61
  18.8 2.8 copy_bitcast_fusion
  24.8 123.3 %start.1 = (bf16[2048,768]{1,0:T(8,128)(2,1)}, bf16[2048,2048]{1,0:T(8,128)(2,1)}, bf16[256,2048]{1,0:T(8,128)(2,1)}, bf16[2048,256]{1,0:T(8,128)(2,1)}, bf16[2,...) custom-call(bf16[2048,256]{1,0:T(8,128)(2,1)} %refs_0_.1, ...), custom_call_target="tpu_custom_call" | custom-call | flops 27917287424 | bytes 23068672 | tf_op jit(solution)/shard_map/start/pallas_call | solution.py:471
  149.3 69.2 %attend.1 = (bf16[2048,256]{1,0:T(8,128)(2,1)}, f32[2,8,2048]{2,1,0:T(8,128)}, bf16[2048,2048]{1,0:T(8,128)(2,1)}, bf16[2,512,512]{2,1,0:T(8,128)(2,1)}, bf16[2,...) custom-call(bf16[2048,768]{1,0:T(8,128)(2,1)} %get-tuple-element.54.refs_0_, ...), custom_call_target="tpu_custom_call" | custom-call | flops 25769803776 | bytes 17960960 | tf_op jit(solution)/shard_map/attend/pallas_call | solution.py:471
  218.5 65.5 %reduce_branch.1 = (f32[256,2048]{1,0:T(8,128)}, bf16[256,2048]{1,0:T(8,128)(2,1)}, bf16[2,512,512]{2,1,0:T(8,128)(2,1)}, bf16[2,512,512]{2,1,0:T(8,128)(2,1)}, ...) custom-call(bf16[2048,256]{1,0:T(8,128)(2,1)} %get-tuple-element.56.refs_0_.refs_1_, ...), custom_call_target="tpu_custom_call" | custom-call | flops 23622320128 | bytes 12582912 | tf_op jit(solution)/shard_map/reduce_branch/pallas_call | solution.py:471
  284.0 89.1 %gather_feed.1 = (bf16[2048,2048]{1,0:T(8,128)(2,1)}, bf16[2048,1024]{1,0:T(8,128)(2,1)}, bf16[2048,2048]{1,0:T(8,128)(2,1)}, bf16[2,512,512]{2,1,0:T(8,128)(2,1...) custom-call(bf16[256,2048]{1,0:T(8,128)(2,1)} %get-tuple-element.62.refs_0_, ...), custom_call_target="tpu_custom_call" | custom-call | flops 38654705664 | bytes 35651584 | tf_op jit(solution)/shard_map/gather_feed/pallas_call | solution.py:471
  373.2 9.4 %fusion.34.refs_15_ = bf16[1024,1024]{1,0:T(8,128)(2,1)} fusion(bf16[2048,1024]{1,0:T(8,128)(2,1)} %get-tuple-element.75.refs_0_, bf16[2048,2048]{1,0:T(8,128)(2,1)} %get-tuple-element.57.refs_0_, s32[]{:T(128)S(6)} %select_n.4), kind=kOutput, calls=%fused_computation.34 | convolution fusion | flops 4296015872 | bytes 10485764 | tf_op jit(solution)/shard_map/tf,td->fd/dot_general | solution.py:165
  382.6 94.0 %reduce_middle.1 = (f32[256,2048]{1,0:T(8,128)}, bf16[256,2048]{1,0:T(8,128)(2,1)}, bf16[2048,2048]{1,0:T(8,128)(2,1)}, bf16[2,512,512]{2,1,0:T(8,128)(2,1)}, bf16[1024,1024]{1,0:T(8,128)(2,1)}) custom-call(bf16[2048,2048]{1,0:T(8,128)(2,1)} %get-tuple-element.57.refs_0_, bf16[2048,2048]{1,0:T(8,128)(2,1)} %get-tuple-element.69.refs_1_, ...), custom_call_target="tpu_custom_call" | custom-call | flops 47244640256 | bytes 48234496 | tf_op jit(solution)/shard_map/reduce_middle/pallas_call | solution.py:471
  476.5 9.5 %fusion.24.refs_7_ = bf16[1024,1024]{1,0:T(8,128)(2,1)} fusion(bf16[2048,2048]{1,0:T(8,128)(2,1)} %get-tuple-element.78, bf16[2048,2048]{1,0:T(8,128)(2,1)} %get-tuple-element.77, s32[]{:T(128)S(6)} %select_n.4), kind=kOutput, calls=%fused_computation.32 | convolution fusion | flops 4296015872 | bytes 10485764 | tf_op jit(solution)/shard_map/td,tf->df/dot_general | solution.py:165
  486.1 8.1 fusion.29.refs_4_
  494.2 5.8 add_convert_fusion.2
  500.0 2.9 copy.24
  502.8 2.6 copy.25
  505.4 71.5 %reduce_down.1 = (bf16[256,2048]{1,0:T(8,128)(2,1)}, bf16[2,1024,512]{2,1,0:T(8,128)(2,1)}, bf16[1024,1024]{1,0:T(8,128)(2,1)}) custom-call(bf16[2048,1024]{1,0:T(8,128)(2,1)} %get-tuple-element.75.refs_0_, bf16[2,512,512]{2,1,0:T(8,128)(2,1)} %get-tuple-element.72.refs_11_.refs_1_, bf16[2,512,512]{2,1,0:T(8,128)(2,1)} %get-tuple-element.74.refs_13_.refs_14_.refs_2_, ...), custom_call_target="tpu_custom_call" | custom-call | flops 30064771072 | bytes 19922944 | tf_op jit(solution)/shard_map/reduce_down/pallas_call | solution.py:471
  576.9 10.1 %add_convert_fusion.1 = bf16[1024,1024]{1,0:T(8,128)(2,1)} fusion(bf16[1024,1024]{1,0:T(8,128)(2,1)} %get-tuple-element.81, bf16[2048,2048]{1,0:T(8,128)(2,1)} %get-tuple-element.78, bf16[2048,2048]{1,0:T(8,128)(2,1)} %get-tuple-element.77, s32[]{:T(128)S(6)} %select_n.5), kind=kOutput, calls=%fused_computation.10 | convolution fusion | flops 4298113024 | bytes 12582916 | tf_op jit(solution)/shard_map/td,tf->df/dot_general | solution.py:165
  588.7 64.4 %gather_mix.1 = (bf16[2048,2048]{1,0:T(8,128)(2,1)}, bf16[2048,256]{1,0:T(8,128)(2,1)}, bf16[2,512,1024]{2,1,0:T(8,128)(2,1)}, bf16[1024,1024]{1,0:T(8,128)(2,1)}) custom-call(bf16[256,2048]{1,0:T(8,128)(2,1)} %get-tuple-element.76.refs_0_, bf16[2,256,512]{2,1,0:T(8,128)(2,1)} %get-tuple-element.58.refs_1_, bf16[2,256,512]{2,1,0:T(8,128)(2,1)} %get-tuple-element.59.refs_2_, ...), custom_call_target="tpu_custom_call" | custom-call | flops 23622320128 | bytes 19922944 | tf_op jit(solution)/shard_map/gather_mix/pallas_call | solution.py:471
  653.1 10.1 %add_convert_fusion = bf16[1024,1024]{1,0:T(8,128)(2,1)} fusion(bf16[1024,1024]{1,0:T(8,128)(2,1)} %get-tuple-element.84, bf16[2048,2048]{1,0:T(8,128)(2,1)} %get-tuple-element.78, bf16[2048,2048]{1,0:T(8,128)(2,1)} %get-tuple-element.77, s32[]{:T(128)S(6)} %select_n.5), kind=kOutput, calls=%fused_computation.9 | convolution fusion | flops 4298113024 | bytes 12582916 | tf_op jit(solution)/shard_map/td,tf->df/dot_general | solution.py:165
  663.2 2.1 fusion.58.refs_8_
  665.3 55.3 %attend_back.1 = (bf16[2048,768]{1,0:T(8,128)(2,1)}, bf16[2,512,1024]{2,1,0:T(8,128)(2,1)}, bf16[256,1024]{1,0:T(8,128)(2,1)}) custom-call(bf16[2048,768]{1,0:T(8,128)(2,1)} %get-tuple-element.54.refs_0_, bf16[2048,256]{1,0:T(8,128)(2,1)} %get-tuple-element.56.refs_0_.refs_1_, bf16[2048,256]{1,0:T(8,128)(2,1)} %get-tuple-element.82.refs_2_, ...), custom_call_target="tpu_custom_call" | custom-call | flops 32212254720 | bytes 15863808 | tf_op jit(solution)/shard_map/attend_back/pallas_call | solution.py:471
  720.5 3.9 fusion.55
  725.6 7.8 fusion.41.refs_7_
  733.5 68.3 %reduce_input.1 = (bf16[256,2048]{1,0:T(8,128)(2,1)}, bf16[2048,256]{1,0:T(8,128)(2,1)}, bf16[2,256,512]{2,1,0:T(8,128)(2,1)}, bf16[1024,768]{1,0:T(8,128)(2,1)}) custom-call(bf16[2048,768]{1,0:T(8,128)(2,1)} %get-tuple-element.86.refs_0_, bf16[2,512,768]{2,1,0:T(8,128)(2,1)} %get-tuple-element.87.refs_1_, bf16[2,512,768]{2,1,0:T(8,128)(2,1)} %get-tuple-element.88.refs_2_, ...), custom_call_target="tpu_custom_call" | custom-call | flops 27917287424 | bytes 16777216 | tf_op jit(solution)/shard_map/reduce_input/pallas_call | solution.py:471
  801.8 8.3 add_convert_fusion.3
  810.9 65.9 %finish.1 = (bf16[2048,256]{1,0:T(8,128)(2,1)}, bf16[2,512,768]{2,1,0:T(8,128)(2,1)}) custom-call(bf16[256,2048]{1,0:T(8,128)(2,1)} %get-tuple-element.94.refs_0_, bf16[2,512,768]{2,1,0:T(8,128)(2,1)} %bitcast.40), custom_call_target="tpu_custom_call" | custom-call | flops 21474836480 | bytes 5242880 | tf_op jit(solution)/shard_map/finish/pallas_call | solution.py:471
  876.9 2.8 convert_element_type.161
  879.9 2.0 add.82
  881.8 2.1 add_bitcast_fusion.1
  885.0 5.2 copy.28
  (43 shorter events, 10.3 us)
Async XLA Ops:
  0.6 10.2 %copy-start = (bf16[512,2,1024]{2,1,0:T(2,128)(2,1)S(1)}, bf16[512,2,1024]{2,1,0:T(2,128)(2,1)}, u32[]{:S(2)}) copy-start(bf16[512,2,1024]{2,1,0:T(2,128)(2,1)} %param.11) | copy-start | bytes 6291460
  0.6 147.5 %collective-permute-start = (s32[1]{0:T(128)}, s32[1]{0:T(128)}, u32[]{:S(2)}, u32[]{:S(2)}) collective-permute-start(s32[1]{0:T(128)} %param.8), channel_id=1, source_target_pairs={{0,0},{4,8},{8,4},{12,12},{1,1},{5,9},{9,5},{13,13},{2,2},{6,10},{... | collective-permute-start | bytes 20 | tf_op jit(solution)/shard_map/ppermute | solution.py:1382
  15.1 6.5 copy-start.1
  476.5 9.5 %copy-start.8 = (bf16[2048,2048]{1,0:T(8,128)(2,1)S(1)}, bf16[2048,2048]{1,0:T(8,128)(2,1)}, u32[]{:S(2)}) copy-start(bf16[2048,2048]{1,0:T(8,128)(2,1)} %get-tuple-element.77) | copy-start | bytes 25165828
  476.5 17.6 %slice-start = ((s8[8388608]{0:T(1024)(128)(4,1)}), s8[4194304]{0:T(1024)(128)(4,1)S(1)}, s32[]{:S(2)}) async-start(s8[8388608]{0:T(1024)(128)(4,1)} %bitcast.41), calls=%async_computation | async-start | bytes 8388608
  486.1 8.1 slice-start.1
  486.1 8.1 copy-start.10
  486.1 8.1 copy-start.11
  576.9 10.1 %copy-start.3 = (bf16[2,1024,512]{2,1,0:T(8,128)(2,1)S(1)}, bf16[2,1024,512]{2,1,0:T(8,128)(2,1)}, u32[]{:S(2)}) copy-start(bf16[2,1024,512]{2,1,0:T(8,128)(2,1)} %get-tuple-element.101) | copy-start | bytes 6291460
  653.1 10.1 %copy-start.7 = (bf16[2048,2048]{1,0:T(8,128)(2,1)S(1)}, bf16[2048,2048]{1,0:T(8,128)(2,1)}, u32[]{:S(2)}) copy-start(bf16[2048,2048]{1,0:T(8,128)(2,1)} %get-tuple-element.85) | copy-start | bytes 25165828
  653.1 10.1 %copy-start.9 = (bf16[2048,256]{1,0:T(8,128)(2,1)S(1)}, bf16[2048,256]{1,0:T(8,128)(2,1)}, u32[]{:S(2)}) copy-start(bf16[2048,256]{1,0:T(8,128)(2,1)} %get-tuple-element.56.refs_0_.refs_1_) | copy-start | bytes 3145732
  801.8 8.3 copy-start.6
  876.9 2.8 copy-start.4
  881.8 2.2 copy-start.2
  885.0 5.3 copy-start.5

commit v4 on v3

--- a/solution.py
+++ b/solution.py
@@ -500,29 +500,27 @@
 SLICES = 4
 
 
+def reduce_sems():
+    return [DMA((4,)), DMA((4,)), DMA((3, SLICES)), DMA((3, SLICES))]
+
+
 def reduce_scratch(piece, width):
-    return [
-        pltpu.VMEM((4, piece, width), BF),
-        pltpu.VMEM((4, piece, width), BF),
-        pltpu.VMEM((2, piece, width), F32),
-        pltpu.VMEM((3, piece, width), BF),
-        pltpu.VMEM((3, piece, width), BF),
-        DMA((4,)), DMA((4,)), DMA((3, SLICES)), DMA((3, SLICES)),
-    ]
-
-
-def reduce_body(place, compute, last, scratch, under, started=False, before_wait=None):
+    return [pltpu.VMEM((count, piece, width), BF) for count in (4, 4, 2, 3, 3)] + reduce_sems()
+
+
+def nothing():
+    pass
+
+
+def reduce_body(place, compute, last, scratch, begin=nothing, before_z=nothing, after_z=nothing):
     sib_out, sib_in, own, near_out, near_in, sib_send, sib_recv, near_send, near_recv = scratch
     piece = own.shape[1]
     c = place.c
-    if not started:
-        under.start_y()
-        under.start_z(outer=True)
+    size = piece // SLICES
+    begin()
 
     def sib_copy(step):
         return remote(sib_out.at[step], sib_in.at[step], sib_send.at[step], sib_recv.at[step], place.sibling)
-
-    size = piece // SLICES
 
     def near_copy(step, r):
         device = place.along if step == 2 else place.across
@@ -539,7 +537,7 @@
             if step == 2:
                 near_copy(0, r).wait_recv()
             rows = span(r * size, size)
-            total = own[slot, rows, :] + sib_in[step, rows, :].astype(F32)
+            total = own[slot, rows, :].astype(F32) + sib_in[step, rows, :].astype(F32)
             if step == 2:
                 total = total + near_in[0, rows, :].astype(F32)
             near_out[step, rows, :] = total.astype(BF)
@@ -561,12 +559,9 @@
         return carry
 
     lax.fori_loop(0, 4, step, 0)
+    before_z()
     finish(2)
-    if not started:
-        under.start_z(outer=False)
-        under.start_follow()
-    if before_wait:
-        before_wait()
+    after_z()
     sib_copy(3).wait_recv()
 
     def arrive(r, carry):
@@ -575,7 +570,7 @@
 
         def final(i, carry):
             rows = span(r * size + i * 16, 16)
-            total = own[1, rows, :] + sib_in[3, rows, :].astype(F32)
+            total = own[1, rows, :].astype(F32) + sib_in[3, rows, :].astype(F32)
             last(rows, total + near_in[1, rows, :].astype(F32) + near_in[2, rows, :].astype(F32))
             return carry
 
@@ -591,7 +586,6 @@
         return carry
 
     lax.fori_loop(0, SLICES, sent, 0)
-    under.end()
 
 
 def product(place, left_ref, weights, transposed):
@@ -617,25 +611,12 @@
     return [first.at[0], first.at[1], second.at[0], second.at[1]]
 
 
-def branch_call(mixed, halves, own_in, moves, ident):
-    piece, width = own_in.shape
-
-    def body(place, ins, outs, scratch, under, targets):
-        mixed_ref, first, second, base_ref = ins
-        total_ref, norm_ref = outs
-
-        def last(rows, total):
-            middle = base_ref[rows, :].astype(F32) + total
-            total_ref[rows, :] = middle
-            norm_ref[rows, :] = row_norm(middle)[0].astype(BF)
-
-        reduce_body(place, product(place, mixed_ref, quarters(first, second), False), last, scratch, under)
-
-    shape = functools.partial(jax.ShapeDtypeStruct, (piece, width))
-    return comm_call(
-        body, "reduce_branch", ident, [mixed, *halves, own_in], [shape(F32), shape(BF)],
-        reduce_scratch(piece, width), moves, flops=2 * mixed.size * width,
-    )
+def beside(under):
+    def begin():
+        under.start_y()
+        under.start_z()
+
+    return dict(begin=begin, after_z=under.start_follow)
 
 
 def down_call(hidden, firsts, seconds, middle, moves, ident):
@@ -655,7 +636,8 @@
         def last(rows, total):
             outs[0][rows, :] = (base_ref[rows, :] + total).astype(BF)
 
-        reduce_body(place, compute, last, scratch, under)
+        reduce_body(place, compute, last, scratch, **beside(under))
+        under.end()
 
     return comm_call(
         body, "reduce_down", ident, [hidden, *firsts, *seconds, middle], [jax.ShapeDtypeStruct((piece, width), BF)],
@@ -673,10 +655,13 @@
         def last(rows, total):
             outs[0][rows, :] = back_rows(base_ref[rows, :], value_ref[rows, :].astype(F32), total).astype(BF)
 
-        reduce_body(
-            place, product(place, rows_ref, quarters(first, second), True), last, scratch[3:], under,
-            before_wait=spread.start,
-        )
+        def after_z():
+            under.start_follow()
+            spread.start()
+
+        hooks = dict(beside(under), after_z=after_z)
+        reduce_body(place, product(place, rows_ref, quarters(first, second), True), last, scratch[3:], **hooks)
+        under.end()
         spread.wait()
 
     return comm_call(
@@ -749,7 +734,8 @@
         def own_rows(rows):
             return pl.ds(pl.multiple_of(place.block * piece + rows.start, 16), rows.size)
 
-        reduce_body(place, compute, last, rest, Under(place, under.moves[1:]), started=True)
+        reduce_body(place, compute, last, rest)
+        under.end(skip=1)
 
     shape = functools.partial(jax.ShapeDtypeStruct, (piece, width))
     return comm_call(
@@ -765,7 +751,7 @@
     return [DMA((3, SLICES)), DMA((3, SLICES)), DMA((4,)), DMA((4,))]
 
 
-def gather_body(place, own_ref, full, sems, process, under):
+def gather_body(place, own_ref, full, sems, process, begin=nothing, follow=nothing):
     near_send, near_recv, sib_send, sib_recv = sems
     piece = own_ref.shape[0]
     size = piece // SLICES
@@ -792,8 +778,7 @@
     slices(lambda r: near_copy(2, r, mine).start())
     slices(lambda r: near_copy(1, r, mine).start())
     sib_copy(3, c, mine).start()
-    under.start_y()
-    under.start_z()
+    begin()
 
     def forward(r):
         near_copy(2, r, z_chip).wait_recv()
@@ -813,7 +798,7 @@
     sib_copy(1, 1 - c, x_chip).wait_recv()
     process((1 - c) * 4 + x_chip)
     process(c * 4 + z_chip)
-    under.start_follow()
+    follow()
     sib_copy(2, 1 - c, z_chip).wait_recv()
     process((1 - c) * 4 + z_chip)
     slices(lambda r: near_copy(0, r, d_chip).wait_recv())
@@ -827,69 +812,6 @@
         sib_copy(slot, c, mine).wait_send()
 
 
-def feed_call(own, tokens, gates, ups, up_last, moves, ident):
-    piece, width = own.shape
-    part = up_last.shape[2]
-    hidden = 2 * part
-    tile = 256
-    tiles = part // tile
-
-    def body(place, ins, outs, scratch, under, targets):
-        own_ref, ga1, ga2, gb1, gb2, ua1, ua2, ub1 = ins
-        full, hidden_ref, slopes_ref = outs
-        columns = (
-            (quarters(ga1, ga2), quarters(ua1, ua2)),
-            (quarters(gb1, gb2), quarters(ub1, targets[0])),
-        )
-        waiting = []
-
-        def fill(owner, which):
-            rows = span(owner * piece, piece)
-            gates, ups = columns[which]
-
-            def step(t, carry):
-                taken = span(t * tile, tile)
-                gate = up = None
-                for gate_weight, up_weight, index in zip(gates, ups, place.order):
-                    size = gate_weight.shape[0]
-                    normed = full[rows, span(index * size, size)]
-                    terms = dot(normed, gate_weight[:, taken], NN), dot(normed, up_weight[:, taken], NN)
-                    gate, up = terms if gate is None else (gate + terms[0], up + terms[1])
-                cols, up_cols = span(which * part + t * tile, tile), span(hidden + which * part + t * tile, tile)
-                sig = 1.0 / (1.0 + jnp.exp(-gate))
-                active = gate * sig
-                hidden_ref[rows, cols] = (active * up).astype(BF)
-                slopes_ref[rows, cols] = (up * sig * (1.0 + gate * (1.0 - sig))).astype(BF)
-                slopes_ref[rows, up_cols] = active.astype(BF)
-                return carry
-
-            lax.fori_loop(0, tiles, step, 0)
-
-        def process(owner):
-            fill(owner, 0)
-            waiting.append(owner)
-            if len(waiting) == 3:
-                under.moves[0][1].wait_recv()
-                for earlier in waiting:
-                    fill(earlier, 1)
-            elif len(waiting) > 3:
-                fill(owner, 1)
-
-        gather_body(place, own_ref, full, scratch, process, under)
-        under.end(skip=1)
-
-    return comm_call(
-        body, "gather_feed", ident, [own, *gates, *ups, up_last],
-        [
-            jax.ShapeDtypeStruct((tokens, width), BF),
-            jax.ShapeDtypeStruct((tokens, hidden), BF),
-            jax.ShapeDtypeStruct((tokens, 2 * hidden), BF),
-        ],
-        gather_scratch(),
-        moves, flops=4 * tokens * hidden * width, transcendentals=tokens * hidden,
-    )
-
-
 def mix_call(own, halves, tokens, moves, ident):
     width = own.shape[1]
     inner = halves[0].shape[1]
@@ -908,7 +830,11 @@
                 total = part if total is None else total + part
             mixed_ref[rows, :] = total.astype(BF)
 
-        gather_body(place, own_ref, full, scratch, process, under)
+        def begin():
+            under.start_y()
+            under.start_z()
+
+        gather_body(place, own_ref, full, scratch, process, begin, under.start_follow)
         under.end()
 
     return comm_call(
@@ -980,73 +906,6 @@
                 self.near(slot, r, mine).wait_send()
 
 
-def attend_call(qkv, prefix, cot_block, heads, hd, moves, ident):
-    seq = qkv.shape[0]
-    bq = bk = min(512, seq // 2)
-    scale = hd ** -0.5
-
-    def body(place, ins, outs, scratch, under, targets):
-        qkv_ref, prefix_ref, block_ref = ins
-        mixed_ref, lse_ref, cot_ref = outs
-        gather = ColumnGather(place, block_ref, cot_ref, scratch)
-        gather.start()
-        under.start_y()
-        under.start_z()
-        bound = prefix_ref[0:1, 0:1]
-
-        def head(h):
-            base = h * 3 * hd
-            for i in range(seq // bq):
-                first = i * bq
-                q = qkv_ref[first:first + bq, base:base + hd]
-                total = max(i + 1, seq // 2 // bk)
-
-                def step(masked, j, state, first=first, q=q):
-                    top, tot, acc = state
-                    rows = span(j * bk, bk)
-                    s = dot(q, qkv_ref[rows, base + hd:base + 2 * hd], NT) * scale
-                    if masked:
-                        kp = j * bk + lax.broadcasted_iota(jnp.int32, (bq, bk), 1)
-                        qp = first + lax.broadcasted_iota(jnp.int32, (bq, bk), 0)
-                        s = jnp.where(kp < jnp.maximum(qp + 1, bound), s, NEG)
-                    new = jnp.maximum(top, jnp.max(s, axis=1, keepdims=True))
-                    alpha = jnp.exp(top - new)
-                    p = jnp.exp(s - new)
-                    tot = tot * alpha + jnp.sum(p, axis=1, keepdims=True)
-                    acc = acc * alpha + dot(p.astype(BF), qkv_ref[rows, base + 2 * hd:base + 3 * hd], NN)
-                    return new, tot, acc
-
-                state = (jnp.full((bq, 1), NEG, F32), jnp.zeros((bq, 1), F32), jnp.zeros((bq, hd), F32))
-                state = lax.fori_loop(0, i, functools.partial(step, False), state)
-                top, tot, acc = lax.fori_loop(i, total, functools.partial(step, True), state)
-                mixed_ref[first:first + bq, h * hd:(h + 1) * hd] = (acc / tot).astype(BF)
-                lse = jnp.broadcast_to(top + jnp.log(tot), (bq, 128))
-                lse_ref[h, :, first:first + bq] = lse.T[0:8, :]
-
-        passed = 0
-        for h in range(heads):
-            head(h)
-            if passed < SLICES:
-                gather.forward(passed)
-                passed += 1
-        under.start_follow()
-        for r in range(passed, SLICES):
-            gather.forward(r)
-        gather.finish()
-        under.end()
-
-    return comm_call(
-        body, "attend", ident, [qkv, prefix, cot_block],
-        [
-            jax.ShapeDtypeStruct((seq, heads * hd), BF),
-            jax.ShapeDtypeStruct((heads, 8, seq), F32),
-            jax.ShapeDtypeStruct((seq, cot_block.shape[1] * 8), BF),
-        ],
-        [DMA((3, SLICES)), DMA((3, SLICES)), DMA((4,)), DMA((4,)), DMA((1,))],
-        moves, flops=4 * heads * seq * seq * hd, transcendentals=heads * seq * seq,
-    )
-
-
 def attend_back_call(qkv, mixed, grad_mixed, lse, prefix, tables, heads, hd, moves, ident):
     seq = qkv.shape[0]
     bq = bk = min(512, seq // 2)
@@ -1117,71 +976,94 @@
     )
 
 
-def start_call(inputs, cot, tables, moves, heads, hd, ident):
+def front_call(inputs, cot, prefix, tables, weights, heads, hd, ident):
+    names = ("qkv", "out", "ga", "gb", "ua", "ub", "da", "db")
     tokens, slice_width = inputs.shape
     width = slice_width * 8
     piece = tokens // 8
-    chunks = 4
-    size = tokens // chunks
-    half = size // 2
-
-    def body(place, ins, outs, scratch, under, targets):
-        in_ref, cot_ref, cos_ref, sin_ref = ins
-        qkv_ref, normed_ref, own_ref, block_ref, second_qkv, second_out = outs
-        (full, total_ref, swap_send, swap_recv, near_send, near_recv, diag_send, diag_recv, sib_send, sib_recv,
-         y_sems) = scratch
+    size = tokens // SLICES
+    inner = weights[0].shape[1]
+    part_width = weights[2].shape[1]
+    hidden = 2 * part_width
+    tile = 256
+    bq = bk = min(512, tokens // 2)
+    scale = hd ** -0.5
+
+    def kernel(in_ref, cot_ref, prefix_ref, cos_ref, sin_ref, *refs):
+        sources, refs = refs[:8], refs[8:]
+        firsts, seconds, refs = refs[:8], refs[8:15], refs[15:]
+        (qkv_ref, mixed_ref, lse_ref, own_in_ref, middle_ref, normed_in_out, cot_out, normed_mid_out, hidden_out,
+         slopes_out), refs = refs[:10], refs[10:]
+        (arena, acc, block_ref, normed_own, w_qkv, w_out, w_ga, w_gb, w_ua, w_ub, z_sems, y_sems, load_sems, out_sems,
+         swap_send, swap_recv, phase, *sems) = refs
+        start_sems, gather_sems, reduce_sems_, feed_sems = sems[:5], sems[5:10], sems[10:14], sems[14:]
+        place = Place()
         c, zl, x = place.c, place.zl, place.x
+        place.meet()
+        z_moves = {n: WeightHalf(place, sources[i], firsts[i], z_sems.at[i]) for i, n in enumerate(names)}
+        y_moves = {n: Beyond(place, firsts[i], seconds[i], y_sems.at[i]) for i, n in enumerate(names[:7])}
+        held = dict(qkv=w_qkv, out=w_out, ga=w_ga, gb=w_gb, ua=w_ua, ub=w_ub)
+
+        def go(name):
+            z_moves[name].start()
+
+        def pass_on(name):
+            z_moves[name].wait_recv()
+            y_moves[name].start()
+
+        def half_load(name, side):
+            i = names.index(name)
+            source = (firsts, seconds)[side][i]
+            return pltpu.make_async_copy(source, held[name].at[side], load_sems.at[i, side])
+
+        def load_first(name):
+            half_load(name, 0).start()
+
+        def load_second(name):
+            y_moves[name].wait_recv()
+            half_load(name, 1).start()
+
+        def parts(name):
+            return [held[name].at[side, i] for side in (0, 1) for i in (0, 1)]
+
+        full, normed = arena.at[pl.ds(0, tokens)], arena.at[pl.ds(tokens, tokens)]
+        gather = ColumnGather(place, in_ref, full, start_sems)
         crossed = jnp.logical_not(place.straight)
         partner = (place.y, 1 - c, 1 - place.zh, zl, x)
-
-        def columns(core, target):
-            return span((core * 4 + target) * slice_width, slice_width)
-
-        mine = place.chip(0, 0)
-        x_chip, z_chip, d_chip = place.chip(0, 1), place.chip(1, 0), place.chip(1, 1)
-
+        mine, x_chip, z_chip, d_chip = gather.chips()
         def rows_of(r):
             return pl.ds(r * size, size)
 
         def swap_copy(r, core):
-            return remote(
-                in_ref.at[rows_of(r)], full.at[rows_of(r), columns(core, mine)], swap_send.at[r], swap_recv.at[r], partner
-            )
+            where = full.at[rows_of(r), gather.where(core, mine)]
+            return remote(in_ref.at[rows_of(r)], where, swap_send.at[r], swap_recv.at[r], partner)
 
         def own_copy(r):
-            return pltpu.make_async_copy(in_ref.at[rows_of(r)], full.at[rows_of(r), columns(c, mine)], swap_send.at[r])
+            where = full.at[rows_of(r), gather.where(c, mine)]
+            return pltpu.make_async_copy(in_ref.at[rows_of(r)], where, swap_send.at[r])
 
         def cot_swap():
-            return remote(cot_ref, block_ref, swap_send.at[chunks], swap_recv.at[chunks], partner)
+            return remote(cot_ref, block_ref, swap_send.at[SLICES], swap_recv.at[SLICES], partner)
 
         def cot_own():
-            return pltpu.make_async_copy(cot_ref, block_ref, swap_send.at[chunks])
-
-        def near_copy(part, r, target):
-            where = full.at[rows_of(r), columns(c, target)]
-            device = place.across if part == 0 else place.along
-            return remote(where, where, near_send.at[part, r], near_recv.at[part, r], device)
-
-        def diag_copy(r, target):
-            where = full.at[rows_of(r), columns(c, target)]
-            return remote(where, where, diag_send.at[r], diag_recv.at[r], place.across)
-
-        def sib_copy(slot, r, core, target):
-            where = full.at[rows_of(r), columns(core, target)]
-            return remote(where, where, sib_send.at[slot, r], sib_recv.at[slot, r], place.sibling)
+            return pltpu.make_async_copy(cot_ref, block_ref, swap_send.at[SLICES])
+
+        def sib(slot, r, core, target):
+            where = full.at[rows_of(r), gather.where(core, target)]
+            return remote(where, where, start_sems[2].at[slot, r], start_sems[3].at[slot, r], place.sibling)
 
         @pl.when(place.straight)
         def _():
-            for r in range(chunks):
+            for r in range(SLICES):
                 own_copy(r).start()
             cot_own().start()
 
         @pl.when(crossed)
         def _():
-            for r in range(chunks):
+            for r in range(SLICES):
                 swap_copy(r, 1 - c).start()
 
-        for r in range(chunks):
+        for r in range(SLICES):
             @pl.when(place.straight)
             def _(r=r):
                 own_copy(r).wait()
@@ -1190,67 +1072,63 @@
             def _(r=r):
                 swap_copy(r, c).wait_recv()
 
-            near_copy(0, r, mine).start()
-            near_copy(1, r, mine).start()
-            sib_copy(0, r, c, mine).start()
-        for r in range(chunks):
-            near_copy(1, r, z_chip).wait_recv()
-            diag_copy(r, z_chip).start()
-            sib_copy(2, r, c, z_chip).start()
-            near_copy(0, r, x_chip).wait_recv()
-            sib_copy(1, r, c, x_chip).start()
+            gather.near(2, r, mine).start()
+            gather.near(1, r, mine).start()
+            sib(3, r, c, mine).start()
+        for r in range(SLICES):
+            gather.forward(r)
+            sib(2, r, c, z_chip).start()
+            gather.near(1, r, x_chip).wait_recv()
+            sib(1, r, c, x_chip).start()
             if r == 0:
-                under.moves[0][1].start()
-
-        under.moves[0][1].wait_recv()
-        under.moves[1][1].start()
+                go("qkv")
+        pass_on("qkv")
+        load_first("qkv")
+        go("out")
         pl.when(crossed)(lambda: cot_swap().start())
-        beyond_qkv = Beyond(place, targets[0], second_qkv, y_sems.at[0])
-        beyond_qkv.start()
-        firsts = [targets[0].at[0], targets[0].at[1]]
-        seconds = [second_qkv.at[0], second_qkv.at[1]]
-        depth = firsts[0].shape[0]
-        for r in range(chunks):
-            diag_copy(r, d_chip).wait_recv()
-            sib_copy(3, r, c, d_chip).start()
-            for slot, target in enumerate((mine, x_chip, z_chip, d_chip)):
-                sib_copy(slot, r, 1 - c, target).wait_recv()
+        half_load("qkv", 0).wait()
+        depth = w_qkv.shape[2]
+        for r in range(SLICES):
+            gather.near(0, r, d_chip).wait_recv()
+            sib(0, r, c, d_chip).start()
+            for slot, target in enumerate((d_chip, x_chip, z_chip, mine)):
+                sib(slot, r, 1 - c, target).wait_recv()
 
             def norm_rows(i, carry, r=r):
                 rows = span(r * size + i * 16, 16)
-                normed_ref[rows, :] = row_norm(full[rows, :].astype(F32))[0].astype(BF)
+                normed[rows, :] = row_norm(full[rows, :].astype(F32))[0].astype(BF)
                 return carry
 
             lax.fori_loop(0, size // 16, norm_rows, 0)
-            rows = rows_of(r)
+            pltpu.make_async_copy(normed.at[rows_of(r)], normed_in_out.at[rows_of(r)], out_sems.at[r]).start()
             total = None
-            for weight, index in zip(firsts, place.order[:2]):
-                term = dot(normed_ref[rows, span(index * depth, depth)], weight[...], NN)
+            for weight, index in zip(parts("qkv")[:2], place.order[:2]):
+                term = dot(normed[rows_of(r), span(index * depth, depth)], weight[...], NN)
                 total = term if total is None else total + term
-            total_ref[rows, :] = total
-        own_ref[...] = full[span(place.block * piece, piece), :]
-        under.moves[1][1].wait_recv()
-        beyond_out = Beyond(place, targets[1], second_out, y_sems.at[1])
-        beyond_out.start()
-        beyond_qkv.wait_recv()
+            acc[rows_of(r), :] = total
+        own_in_ref[...] = full[span(place.block * piece, piece), :]
+        load_second("qkv")
+        half_load("qkv", 1).wait()
+        go("ga")
+        half = size // 2
 
         def project(r, carry):
             rows = span(r * half, half)
-            total = total_ref[rows, :]
-            for weight, index in zip(seconds, place.order[2:]):
-                total = total + dot(normed_ref[rows, span(index * depth, depth)], weight[...], NN)
+            total = acc[rows, :]
+            for weight, index in zip(parts("qkv")[2:], place.order[2:]):
+                total = total + dot(normed[rows, span(index * depth, depth)], weight[...], NN)
             cos, sin = cos_ref[rows, :], sin_ref[rows, :]
             for h in range(heads):
                 for part in range(3):
-                    cols = pl.ds((3 * h + part) * hd, hd)
                     value = total[:, (3 * h + part) * hd:(3 * h + part + 1) * hd]
                     if part < 2:
                         value = value * cos + pltpu.roll(value, hd // 2, 1) * sin
-                    qkv_ref[rows, cols] = value.astype(BF)
+                    qkv_ref[rows, pl.ds((3 * h + part) * hd, hd)] = value.astype(BF)
             return carry
 
         lax.fori_loop(0, tokens // half, project, 0)
-        beyond_out.wait_recv()
+        pass_on("out")
+        load_first("out")
 
         @pl.when(place.straight)
         def _():
@@ -1260,38 +1138,225 @@
         def _():
             cot_swap().wait_recv()
             cot_swap().wait_send()
-            for r in range(chunks):
+            for r in range(SLICES):
                 swap_copy(r, 1 - c).wait_send()
 
-        beyond_qkv.wait_send()
-        beyond_out.wait_send()
-        for r in range(chunks):
-            near_copy(0, r, mine).wait_send()
-            near_copy(1, r, mine).wait_send()
-            diag_copy(r, z_chip).wait_send()
+        cot_gather = ColumnGather(place, block_ref, cot_out, gather_sems)
+        cot_gather.start()
+        bound = prefix_ref[0:1, 0:1]
+
+        def head(h, carry):
+            base = h * 3 * hd
+            for i in range(tokens // bq):
+                first = i * bq
+                q = qkv_ref[first:first + bq, span(base, hd)]
+                count = max(i + 1, tokens // 2 // bk)
+
+                def step(masked, j, state, first=first, q=q):
+                    top, tot, out = state
+                    rows = span(j * bk, bk)
+                    s = dot(q, qkv_ref[rows, span(base + hd, hd)], NT) * scale
+                    if masked:
+                        kp = j * bk + lax.broadcasted_iota(jnp.int32, (bq, bk), 1)
+                        qp = first + lax.broadcasted_iota(jnp.int32, (bq, bk), 0)
+                        s = jnp.where(kp < jnp.maximum(qp + 1, bound), s, NEG)
+                    new = jnp.maximum(top, jnp.max(s, axis=1, keepdims=True))
+                    alpha = jnp.exp(top - new)
+                    p = jnp.exp(s - new)
+                    tot = tot * alpha + jnp.sum(p, axis=1, keepdims=True)
+                    out = out * alpha + dot(p.astype(BF), qkv_ref[rows, span(base + 2 * hd, hd)], NN)
+                    return new, tot, out
+
+                state = (jnp.full((bq, 1), NEG, F32), jnp.zeros((bq, 1), F32), jnp.zeros((bq, hd), F32))
+                state = lax.fori_loop(0, i, functools.partial(step, False), state)
+                top, tot, out = lax.fori_loop(i, count, functools.partial(step, True), state)
+                mixed_ref[first:first + bq, span(h * hd, hd)] = (out / tot).astype(BF)
+                lse = jnp.broadcast_to(top + jnp.log(tot), (bq, 128))
+                lse_ref[h, :, first:first + bq] = lse.T[0:8, :]
+            return carry
+
+        lax.fori_loop(0, heads, head, 0)
+        go("gb")
+        load_second("out")
+        half_load("out", 0).wait()
+        half_load("out", 1).wait()
+        cot_gather.forward(0)
+        pass_on("ga")
+
+        for r in range(SLICES):
+            pltpu.make_async_copy(normed.at[rows_of(r)], normed_in_out.at[rows_of(r)], out_sems.at[r]).wait()
+            for slot in range(3):
+                gather.near(slot, r, mine).wait_send()
             for slot in range(4):
-                sib_copy(slot, r, c, mine).wait_send()
-
-    qkv_half, out_half = (moved_shape(kind, array) for kind, array in moves)
-    inner = qkv_half.shape[2]
-    return comm_call(
-        body, "start", ident, [inputs, cot, *tables],
-        [
-            jax.ShapeDtypeStruct((tokens, inner), BF),
-            jax.ShapeDtypeStruct((tokens, width), BF),
-            jax.ShapeDtypeStruct((piece, width), BF),
-            jax.ShapeDtypeStruct(cot.shape, BF),
-            qkv_half,
-            out_half,
+                sib(slot, r, c, mine).wait_send()
+        for device in (place.sibling, place.across, place.along):
+            pl.semaphore_signal(phase, inc=1, device_id=device, device_id_type=MESH)
+        pl.semaphore_wait(phase, 3)
+
+        class Blocks:
+            def __init__(self, first, count):
+                self.first, self.shape = first, (count, piece, width)
+
+            def rows(self, index):
+                if isinstance(index, tuple):
+                    step, inside, *rest = index
+                    start = (self.first + step) * piece + inside.start
+                    return (pl.ds(pl.multiple_of(start, 16), inside.size), *rest)
+                return (span((self.first + index) * piece, piece),)
+
+            @property
+            def at(self):
+                return At(self)
+
+            def __getitem__(self, index):
+                return arena[self.rows(index)]
+
+            def __setitem__(self, index, value):
+                arena[self.rows(index)] = value
+
+        class At:
+            def __init__(self, blocks):
+                self.blocks = blocks
+
+            def __getitem__(self, index):
+                return arena.at[self.blocks.rows(index)]
+
+        buffers, first = [], 0
+        for count in (4, 4, 2, 3, 3):
+            buffers.append(Blocks(first, count))
+            first += count
+
+        def last(rows, total):
+            middle = own_in_ref[rows, :].astype(F32) + total
+            middle_ref[rows, :] = middle
+            normed_own[rows, :] = row_norm(middle)[0].astype(BF)
+
+        def before_z():
+            go("ua")
+            for r in range(1, SLICES):
+                cot_gather.forward(r)
+
+        def after_z():
+            pass_on("gb")
+            go("ub")
+            load_first("ga")
+            load_first("gb")
+            load_second("ga")
+
+        reduce_body(
+            place, product(place, mixed_ref, parts("out"), False), last, [*buffers, *reduce_sems_],
+            before_z=before_z, after_z=after_z,
+        )
+
+        full = arena.at[pl.ds(2 * tokens, tokens)]
+        slopes_ref = arena.at[pl.ds(0, tokens)]
+        hidden_ref = arena.at[pl.ds(tokens, tokens), pl.ds(0, hidden)]
+        columns = (("ga", "ua"), ("gb", "ub"))
+        waiting = []
+
+        def fill(owner, which):
+            rows = span(owner * piece, piece)
+            gates, ups = (parts(name) for name in columns[which])
+
+            def step(t, carry):
+                taken = span(t * tile, tile)
+                gate = up = None
+                for gate_weight, up_weight, index in zip(gates, ups, place.order):
+                    deep = gate_weight.shape[0]
+                    value = full[rows, span(index * deep, deep)]
+                    terms = dot(value, gate_weight[:, taken], NN), dot(value, up_weight[:, taken], NN)
+                    gate, up = terms if gate is None else (gate + terms[0], up + terms[1])
+                cols = span(which * part_width + t * tile, tile)
+                up_cols = span(hidden + which * part_width + t * tile, tile)
+                sig = 1.0 / (1.0 + jnp.exp(-gate))
+                active = gate * sig
+                hidden_ref[rows, cols] = (active * up).astype(BF)
+                slopes_ref[rows, cols] = (up * sig * (1.0 + gate * (1.0 - sig))).astype(BF)
+                slopes_ref[rows, up_cols] = active.astype(BF)
+                return carry
+
+            lax.fori_loop(0, part_width // tile, step, 0)
+
+        def process(owner):
+            waiting.append(owner)
+            if len(waiting) == 1:
+                for side in (0, 1):
+                    half_load("ga", side).wait()
+                pass_on("ua")
+                load_second("gb")
+                load_first("ua")
+                load_second("ua")
+                for side in (0, 1):
+                    half_load("ua", side).wait()
+            fill(owner, 0)
+            if len(waiting) == 3:
+                for side in (0, 1):
+                    half_load("gb", side).wait()
+                pass_on("ub")
+                load_first("ub")
+                go("db")
+                load_second("ub")
+                for side in (0, 1):
+                    half_load("ub", side).wait()
+                for i, earlier in enumerate(waiting):
+                    fill(earlier, 1)
+            elif len(waiting) > 3:
+                fill(owner, 1)
+
+        gather_body(place, normed_own, full, feed_sems, process, begin=lambda: go("da"))
+        for i, (ref, out) in enumerate(((full, normed_mid_out), (hidden_ref, hidden_out), (slopes_ref, slopes_out))):
+            pltpu.make_async_copy(ref, out, out_sems.at[SLICES + i]).start()
+        pass_on("da")
+        cot_gather.finish()
+        z_moves["db"].wait_recv()
+        y_moves["da"].wait_recv()
+        for i, (ref, out) in enumerate(((full, normed_mid_out), (hidden_ref, hidden_out), (slopes_ref, slopes_out))):
+            pltpu.make_async_copy(ref, out, out_sems.at[SLICES + i]).wait()
+        for move in (*z_moves.values(), *y_moves.values()):
+            move.wait_send()
+
+    def half_shape(weight):
+        return jax.ShapeDtypeStruct((2, *weight.shape), BF)
+
+    shape = jax.ShapeDtypeStruct
+    outs = [
+        *(half_shape(weight) for weight in weights),
+        *(half_shape(weight) for weight in weights[:7]),
+        shape((tokens, inner), BF),
+        shape((tokens, heads * hd), BF),
+        shape((heads, 8, tokens), F32),
+        shape((piece, width), BF),
+        shape((piece, width), F32),
+        shape((tokens, width), BF),
+        shape((tokens, width), BF),
+        shape((tokens, width), BF),
+        shape((tokens, hidden), BF),
+        shape((tokens, 2 * hidden), BF),
+    ]
+    column_sems = [DMA((3, SLICES)), DMA((3, SLICES)), DMA((4,)), DMA((4,)), DMA((1,))]
+    start_sems = [DMA((3, SLICES)), DMA((3, SLICES)), DMA((4, SLICES)), DMA((4, SLICES)), DMA((1,))]
+    result = pl.pallas_call(
+        kernel,
+        out_shape=outs,
+        in_specs=[ANYWHERE, ANYWHERE, VMEM_WHOLE, VMEM_WHOLE, VMEM_WHOLE] + [ANYWHERE] * 8,
+        out_specs=[ANYWHERE] * 15 + [VMEM_WHOLE] * 5 + [ANYWHERE] * 5,
+        scratch_shapes=[
+            pltpu.VMEM((3 * tokens, width), BF),
+            pltpu.VMEM((tokens, inner), F32),
+            pltpu.VMEM((tokens, slice_width), BF),
+            pltpu.VMEM((piece, width), BF),
+            *(pltpu.VMEM((2, 2, *weight.shape), BF) for weight in weights[:6]),
+            DMA((8, 4)), DMA((8, 4)), DMA((8, 2)), DMA((SLICES + 3,)), DMA((SLICES + 1,)), DMA((SLICES + 1,)),
+            pltpu.SemaphoreType.REGULAR,
+            *start_sems, *column_sems, *reduce_sems(), *gather_scratch(),
         ],
-        [
-            pltpu.VMEM((tokens, width), BF), pltpu.VMEM((tokens, inner), F32),
-            DMA((chunks + 1,)), DMA((chunks + 1,)), DMA((2, chunks)), DMA((2, chunks)), DMA((chunks,)),
-            DMA((chunks,)), DMA((4, chunks)), DMA((4, chunks)), DMA((2, 4)),
-        ],
-        moves, flops=2 * tokens * width * inner,
-        spaces=[ANYWHERE, ANYWHERE, VMEM_WHOLE, VMEM_WHOLE],
-    )
+        compiler_params=pltpu.CompilerParams(collective_id=ident, has_side_effects=True, vmem_limit_bytes=63 << 20),
+        cost_estimate=pl.CostEstimate(
+            flops=100 << 30, bytes_accessed=100 << 20, transcendentals=heads * tokens * tokens
+        ),
+        name="front",
+    )(inputs, cot, prefix, *tables, *weights)
+    return result[:8], result[8:15], result[15:]
 
 
 BLOCKS = [(core, zl, x) for core in (0, 1) for zl in (0, 1) for x in (0, 1)]
@@ -1388,19 +1453,12 @@
     ua, ub = w_up_gate[:, 1, :part], w_up_gate[:, 1, part:]
     da, db = w_down[:part], w_down[part:]
 
-    (qkv, normed_in, own_in, cot_block, qkv_2, out_2), (qkv_1, out_1) = start_call(
-        inputs, cotangent, tables, [("weight", w_qkv.reshape(w_qkv.shape[0], -1)), ("weight", w_out)], heads, hd, 1
-    )
-    (mixed, lse, cot_full), (ga_1, gb_1, ga_2) = attend_call(
-        qkv, prefix, cot_block, heads, hd, [("weight", ga), ("weight", gb), (0, None)], 2
-    )
-    (middle, normed_own), (gb_2, ua_1, ub_1, ua_2) = branch_call(
-        mixed, (out_1, out_2), own_in, [("beyond", gb_1), ("weight", ua), ("weight", ub), (1, None)], 3
-    )
+    weights = (w_qkv.reshape(w_qkv.shape[0], -1), w_out, ga, gb, ua, ub, da, db)
+    firsts, seconds, results = front_call(inputs, cotangent, prefix, tables, weights, heads, hd, 1)
+    qkv_1, out_1, ga_1, gb_1, ua_1, ub_1, da_1, db_1 = firsts
+    qkv_2, out_2, ga_2, gb_2, ua_2, ub_2, da_2 = seconds
+    qkv, mixed, lse, own_in, middle, normed_in, cot_full, normed_mid, hidden, slopes = results
     gates = (ga_1, ga_2, gb_1, gb_2)
-    (normed_mid, hidden, slopes), (ub_2, da_1, db_1, da_2) = feed_call(
-        normed_own, tokens, gates, (ua_1, ua_2), ub_1, [("beyond", ub_1), ("weight", da), ("weight", db), (1, None)], 4
-    )
 
     def halves(spec, left, right, axis):
         side = left if axis == 0 else right

time: 900 us -> 855 us (0.950)
  Pallas kernels: 767 us -> 721 us
    pallas_call x10 -> x6, Pallas kernels: 767 us -> 415 us  [comm_call(): pl.pallas_call(kernel, out_shape=shapes, in_specs=in_specs, out_specs=[VM...]
    pallas_call x0 -> x1, Pallas kernels: none -> 306 us  [front_call(): pl.pallas_call(kernel, out_shape=outs, in_specs=[ANYWHERE, ANYWHERE, VMEM...]
  transfers between devices with their start and end apart: 1 -> 1, of which waited for: 0 -> 0; matrix products, arithmetic and copies ran while one was open for 2% -> 2% of each run, Pallas kernels for 14% -> 0%
where the time goes in v4:
time: 855 us; the launch traced here: 846 us
  Pallas kernels  721 us (84%)
  matrix products  75.2 us (9%)
  local copies, waits for them, and re-layouts  28.9 us (3%)
  other arithmetic  14.1 us (2%)
    pallas_call x6, Pallas kernels, comm_call(): pl.pallas_call(kernel, out_shape=shapes, in_specs=in_specs, out_specs=[VM...  415 us
    pallas_call x1, Pallas kernels, front_call(): pl.pallas_call(kernel, out_shape=outs, in_specs=[ANYWHERE, ANYWHERE, VMEM...  306 us
    dot_general x10, matrix products, mm(): return jnp.einsum(spec, left, right, preferred_element_type=F32)  75.2 us
  transfers between devices with their start and end apart: 1, of which 0 were waited for; matrix products, arithmetic and copies ran while one was open for 2% of the time, Pallas kernels for 0%

profile of v4, /device:TPU:1, one launch (start us, length us, event | category | flops | bytes accessed | tf_op | source)
XLA Modules:
  0.0 846.1 jit_solution(7922685001720232353)
XLA Ops:
  0.6 5.7 collective-permute-start
  6.4 2.1 copy.34
  8.6 2.2 fusion.73
  10.8 4.2 fusion.72
  15.1 3.7 fusion.61
  18.8 2.8 copy_bitcast_fusion
  21.6 1.2 copy_bitcast_fusion.2
  22.8 1.9 pad_maximum_fusion.1
  26.0 306.3 %front.1 = (bf16[2,512,768]{2,1,0:T(8,128)(2,1)}, bf16[2,256,512]{2,1,0:T(8,128)(2,1)}, bf16[2,512,512]{2,1,0:T(8,128)(2,1)}, bf16[2,512,512]{2,1,0:T(8,128)(2,1...) custom-call(bf16[2048,256]{1,0:T(8,128)(2,1)} %in_ref.1, ...), custom_call_target="tpu_custom_call" | custom-call | flops 107374182400 | bytes 104857600 | tf_op jit(solution)/shard_map/front/pallas_call | solution.py:1338
  332.2 9.4 %fusion.34.refs_15_ = bf16[1024,1024]{1,0:T(8,128)(2,1)} fusion(bf16[2048,1024]{1,0:T(8,128)(2,1)} %get-tuple-element.68.refs_0_, bf16[2048,2048]{1,0:T(8,128)(2,1)} %get-tuple-element.54.refs_0_, s32[]{:T(128)S(6)} %select_n.4), kind=kOutput, calls=%fused_computation.34 | convolution fusion | flops 4296015872 | bytes 10485764 | tf_op jit(solution)/shard_map/tf,td->fd/dot_general | solution.py:165
  341.6 95.5 %reduce_middle.1 = (f32[256,2048]{1,0:T(8,128)}, bf16[256,2048]{1,0:T(8,128)(2,1)}, bf16[2048,2048]{1,0:T(8,128)(2,1)}, bf16[2,512,512]{2,1,0:T(8,128)(2,1)}, bf16[1024,1024]{1,0:T(8,128)(2,1)}) custom-call(bf16[2048,2048]{1,0:T(8,128)(2,1)} %get-tuple-element.54.refs_0_, bf16[2048,2048]{1,0:T(8,128)(2,1)} %get-tuple-element.55.refs_1_, ...), custom_call_target="tpu_custom_call" | custom-call | flops 47244640256 | bytes 48234496 | tf_op jit(solution)/shard_map/reduce_middle/pallas_call | solution.py:471
  437.2 9.5 %fusion.24.refs_7_ = bf16[1024,1024]{1,0:T(8,128)(2,1)} fusion(bf16[2048,2048]{1,0:T(8,128)(2,1)} %get-tuple-element.73, bf16[2048,2048]{1,0:T(8,128)(2,1)} %get-tuple-element.72, s32[]{:T(128)S(6)} %select_n.4), kind=kOutput, calls=%fused_computation.32 | convolution fusion | flops 4296015872 | bytes 10485764 | tf_op jit(solution)/shard_map/td,tf->df/dot_general | solution.py:165
  446.7 8.1 fusion.29.refs_4_
  454.8 5.9 add_convert_fusion.2
  460.8 2.9 copy.24
  463.6 2.6 copy.25
  466.2 65.9 %reduce_down.1 = (bf16[256,2048]{1,0:T(8,128)(2,1)}, bf16[2,1024,512]{2,1,0:T(8,128)(2,1)}, bf16[1024,1024]{1,0:T(8,128)(2,1)}) custom-call(bf16[2048,1024]{1,0:T(8,128)(2,1)} %get-tuple-element.68.refs_0_, bf16[2,512,512]{2,1,0:T(8,128)(2,1)} %get-tuple-element.65.refs_11_.refs_1_, bf16[2,512,512]{2,1,0:T(8,128)(2,1)} %get-tuple-element.67.refs_13_.refs_14_.refs_2_, ...), custom_call_target="tpu_custom_call" | custom-call | flops 30064771072 | bytes 19922944 | tf_op jit(solution)/shard_map/reduce_down/pallas_call | solution.py:471
  532.1 10.1 %add_convert_fusion.1 = bf16[1024,1024]{1,0:T(8,128)(2,1)} fusion(bf16[1024,1024]{1,0:T(8,128)(2,1)} %get-tuple-element.76, bf16[2048,2048]{1,0:T(8,128)(2,1)} %get-tuple-element.73, bf16[2048,2048]{1,0:T(8,128)(2,1)} %get-tuple-element.72, s32[]{:T(128)S(6)} %select_n.5), kind=kOutput, calls=%fused_computation.10 | convolution fusion | flops 4298113024 | bytes 12582916 | tf_op jit(solution)/shard_map/td,tf->df/dot_general | solution.py:165
  542.3 1.6 add_bitcast_fusion
  543.9 64.4 %gather_mix.1 = (bf16[2048,2048]{1,0:T(8,128)(2,1)}, bf16[2048,256]{1,0:T(8,128)(2,1)}, bf16[2,512,1024]{2,1,0:T(8,128)(2,1)}, bf16[1024,1024]{1,0:T(8,128)(2,1)}) custom-call(bf16[256,2048]{1,0:T(8,128)(2,1)} %get-tuple-element.69.refs_0_, bf16[2,256,512]{2,1,0:T(8,128)(2,1)} %get-tuple-element.70.refs_1_, bf16[2,256,512]{2,1,0:T(8,128)(2,1)} %get-tuple-element.71.refs_2_, ...), custom_call_target="tpu_custom_call" | custom-call | flops 23622320128 | bytes 19922944 | tf_op jit(solution)/shard_map/gather_mix/pallas_call | solution.py:471
  608.3 10.1 %add_convert_fusion = bf16[1024,1024]{1,0:T(8,128)(2,1)} fusion(bf16[1024,1024]{1,0:T(8,128)(2,1)} %get-tuple-element.79, bf16[2048,2048]{1,0:T(8,128)(2,1)} %get-tuple-element.73, bf16[2048,2048]{1,0:T(8,128)(2,1)} %get-tuple-element.72, s32[]{:T(128)S(6)} %select_n.5), kind=kOutput, calls=%fused_computation.9 | convolution fusion | flops 4298113024 | bytes 12582916 | tf_op jit(solution)/shard_map/td,tf->df/dot_general | solution.py:165
  618.4 2.1 fusion.58.refs_8_
  620.4 56.7 %attend_back.1 = (bf16[2048,768]{1,0:T(8,128)(2,1)}, bf16[2,512,1024]{2,1,0:T(8,128)(2,1)}, bf16[256,1024]{1,0:T(8,128)(2,1)}) custom-call(bf16[2048,768]{1,0:T(8,128)(2,1)} %get-tuple-element.52.refs_0_, bf16[2048,256]{1,0:T(8,128)(2,1)} %get-tuple-element.53.refs_1_, bf16[2048,256]{1,0:T(8,128)(2,1)} %get-tuple-element.77.refs_2_, ...), custom_call_target="tpu_custom_call" | custom-call | flops 32212254720 | bytes 15863808 | tf_op jit(solution)/shard_map/attend_back/pallas_call | solution.py:471
  677.2 3.9 fusion.55
  682.3 7.8 fusion.41.refs_7_
  690.1 66.8 %reduce_input.1 = (bf16[256,2048]{1,0:T(8,128)(2,1)}, bf16[2048,256]{1,0:T(8,128)(2,1)}, bf16[2,256,512]{2,1,0:T(8,128)(2,1)}, bf16[1024,768]{1,0:T(8,128)(2,1)}) custom-call(bf16[2048,768]{1,0:T(8,128)(2,1)} %get-tuple-element.81.refs_0_, bf16[2,512,768]{2,1,0:T(8,128)(2,1)} %get-tuple-element.82.refs_1_, bf16[2,512,768]{2,1,0:T(8,128)(2,1)} %get-tuple-element.83.refs_2_, ...), custom_call_target="tpu_custom_call" | custom-call | flops 27917287424 | bytes 16777216 | tf_op jit(solution)/shard_map/reduce_input/pallas_call | solution.py:471
  757.0 8.3 add_convert_fusion.3
  766.1 65.5 %finish.1 = (bf16[2048,256]{1,0:T(8,128)(2,1)}, bf16[2,512,768]{2,1,0:T(8,128)(2,1)}) custom-call(bf16[256,2048]{1,0:T(8,128)(2,1)} %get-tuple-element.90.refs_0_, bf16[2,512,768]{2,1,0:T(8,128)(2,1)} %bitcast.40), custom_call_target="tpu_custom_call" | custom-call | flops 21474836480 | bytes 5242880 | tf_op jit(solution)/shard_map/finish/pallas_call | solution.py:471
  831.6 2.8 convert_element_type.161
  834.6 2.0 add.82
  836.5 2.1 add_bitcast_fusion.1
  839.7 5.2 copy.28
  (40 shorter events, 5.5 us)
Async XLA Ops:
  0.6 10.2 %copy-start = (bf16[512,2,1024]{2,1,0:T(2,128)(2,1)S(1)}, bf16[512,2,1024]{2,1,0:T(2,128)(2,1)}, u32[]{:S(2)}) copy-start(bf16[512,2,1024]{2,1,0:T(2,128)(2,1)} %param.11) | copy-start | bytes 6291460
  0.6 24.1 %collective-permute-start = (s32[1]{0:T(128)}, s32[1]{0:T(128)}, u32[]{:S(2)}, u32[]{:S(2)}) collective-permute-start(s32[1]{0:T(128)} %param.8), channel_id=1, source_target_pairs={{0,0},{4,8},{8,4},{12,12},{1,1},{5,9},{9,5},{13,13},{2,2},{6,10},{... | collective-permute-start | bytes 20 | tf_op jit(solution)/shard_map/ppermute | solution.py:1447
  15.1 6.5 copy-start.1
  437.1 9.5 %copy-start.8 = (bf16[2048,2048]{1,0:T(8,128)(2,1)S(1)}, bf16[2048,2048]{1,0:T(8,128)(2,1)}, u32[]{:S(2)}) copy-start(bf16[2048,2048]{1,0:T(8,128)(2,1)} %get-tuple-element.72) | copy-start | bytes 25165828
  437.2 17.6 %slice-start = ((s8[8388608]{0:T(1024)(128)(4,1)}), s8[4194304]{0:T(1024)(128)(4,1)S(1)}, s32[]{:S(2)}) async-start(s8[8388608]{0:T(1024)(128)(4,1)} %bitcast.41), calls=%async_computation | async-start | bytes 8388608
  446.7 8.1 slice-start.1
  446.7 8.1 copy-start.10
  446.7 8.1 copy-start.11
  532.1 10.1 %copy-start.3 = (bf16[2,1024,512]{2,1,0:T(8,128)(2,1)S(1)}, bf16[2,1024,512]{2,1,0:T(8,128)(2,1)}, u32[]{:S(2)}) copy-start(bf16[2,1024,512]{2,1,0:T(8,128)(2,1)} %get-tuple-element.97) | copy-start | bytes 6291460
  608.2 10.1 %copy-start.7 = (bf16[2048,2048]{1,0:T(8,128)(2,1)S(1)}, bf16[2048,2048]{1,0:T(8,128)(2,1)}, u32[]{:S(2)}) copy-start(bf16[2048,2048]{1,0:T(8,128)(2,1)} %get-tuple-element.80) | copy-start | bytes 25165828
  608.3 10.1 %copy-start.9 = (bf16[2048,256]{1,0:T(8,128)(2,1)S(1)}, bf16[2048,256]{1,0:T(8,128)(2,1)}, u32[]{:S(2)}) copy-start(bf16[2048,256]{1,0:T(8,128)(2,1)} %get-tuple-element.53.refs_1_) | copy-start | bytes 3145732
  756.9 8.3 copy-start.6
  831.6 2.8 copy-start.4
  836.5 2.2 copy-start.2
  839.7 5.3 copy-start.5

commit v5 on v4

--- a/solution.py
+++ b/solution.py
@@ -498,6 +498,8 @@
 
 
 SLICES = 4
+NORM_ROWS = 64
+NORM_UNROLL = 1
 
 
 def reduce_sems():
@@ -642,33 +644,6 @@
     return comm_call(
         body, "reduce_down", ident, [hidden, *firsts, *seconds, middle], [jax.ShapeDtypeStruct((piece, width), BF)],
         reduce_scratch(piece, width), moves, flops=2 * hidden.size * width,
-    )
-
-
-def input_call(grad_rows, halves, grad_middle, own_in, ready, moves, ident):
-    piece, width = own_in.shape
-
-    def body(place, ins, outs, scratch, under, targets):
-        rows_ref, first, second, base_ref, value_ref, ready_ref = ins
-        spread = Spread(place, ready_ref, outs[1], scratch[:3])
-
-        def last(rows, total):
-            outs[0][rows, :] = back_rows(base_ref[rows, :], value_ref[rows, :].astype(F32), total).astype(BF)
-
-        def after_z():
-            under.start_follow()
-            spread.start()
-
-        hooks = dict(beside(under), after_z=after_z)
-        reduce_body(place, product(place, rows_ref, quarters(first, second), True), last, scratch[3:], **hooks)
-        under.end()
-        spread.wait()
-
-    return comm_call(
-        body, "reduce_input", ident, [grad_rows, *halves, grad_middle, own_in, ready],
-        [jax.ShapeDtypeStruct((piece, width), BF), spread_shape(ready)],
-        [*spread_scratch(), *reduce_scratch(piece, width)], moves, flops=2 * grad_rows.size * width,
-        greet=spread_greet,
     )
 
 
@@ -812,38 +787,6 @@
         sib_copy(slot, c, mine).wait_send()
 
 
-def mix_call(own, halves, tokens, moves, ident):
-    width = own.shape[1]
-    inner = halves[0].shape[1]
-
-    def body(place, ins, outs, scratch, under, targets):
-        own_ref, first, second = ins
-        full, mixed_ref = outs
-        piece = own_ref.shape[0]
-
-        def process(owner):
-            rows = span(owner * piece, piece)
-            total = None
-            for weight, index in zip(quarters(first, second), place.order):
-                size = weight.shape[1]
-                part = dot(full[rows, span(index * size, size)], weight[...], NT)
-                total = part if total is None else total + part
-            mixed_ref[rows, :] = total.astype(BF)
-
-        def begin():
-            under.start_y()
-            under.start_z()
-
-        gather_body(place, own_ref, full, scratch, process, begin, under.start_follow)
-        under.end()
-
-    return comm_call(
-        body, "gather_mix", ident, [own, *halves],
-        [jax.ShapeDtypeStruct((tokens, width), BF), jax.ShapeDtypeStruct((tokens, inner), BF)],
-        gather_scratch(), moves, flops=2 * tokens * inner * width,
-    )
-
-
 class ColumnGather:
     def __init__(self, place, src, full, sems):
         self.place, self.src, self.full = place, src, full
@@ -906,74 +849,57 @@
                 self.near(slot, r, mine).wait_send()
 
 
-def attend_back_call(qkv, mixed, grad_mixed, lse, prefix, tables, heads, hd, moves, ident):
-    seq = qkv.shape[0]
+def attend_back_body(qkv_ref, o_ref, do_ref, lse_ref, bound, cos_ref, sin_ref, out_ref, dk_ref, dv_ref, heads, hd):
+    seq = qkv_ref.shape[0]
     bq = bk = min(512, seq // 2)
     scale = hd ** -0.5
     half = hd // 2
 
-    def body(place, ins, outs, scratch, under, targets):
-        qkv_ref, o_ref, do_ref, lse_ref, prefix_ref, cos_ref, sin_ref = ins
-        (out_ref,) = outs
-        under.start_y()
-        under.start_z()
-        dk_ref, dv_ref = scratch
-        bound = prefix_ref[0:1, 0:1]
-
-        def unrotate(g, rows):
-            return g * cos_ref[rows, :] - pltpu.roll(g, half, 1) * sin_ref[rows, :]
-
-        def head(h, carry):
-            base = h * 3 * hd
-            own = span(h * hd, hd)
-            dk_ref[...] = jnp.zeros_like(dk_ref)
-            dv_ref[...] = jnp.zeros_like(dv_ref)
-            for i in range(seq // bq):
-                first = i * bq
-                rows = pl.ds(first, bq)
-                q = qkv_ref[rows, span(base, hd)]
-                do = do_ref[rows, own]
-                row_sums = (do.astype(F32) * o_ref[rows, own].astype(F32)).T
-                delta = jnp.sum(row_sums, axis=0, keepdims=True)
-                tops = lse_ref[h, 0:1, first:first + bq]
-                total = max(i + 1, seq // 2 // bk)
-
-                def step(masked, j, dq, first=first, q=q, do=do, delta=delta, tops=tops):
-                    keys = span(j * bk, bk)
-                    k = qkv_ref[keys, span(base + hd, hd)]
-                    v = qkv_ref[keys, span(base + 2 * hd, hd)]
-                    p = jnp.exp(dot(k, q, NT) * scale - tops)
-                    if masked:
-                        kp = j * bk + lax.broadcasted_iota(jnp.int32, (bk, bq), 0)
-                        qp = first + lax.broadcasted_iota(jnp.int32, (bk, bq), 1)
-                        p = jnp.where(kp < jnp.maximum(qp + 1, bound), p, 0.0)
-                    dv_ref[keys, :] += dot(p.astype(BF), do, NN)
-                    ds = (p * (dot(v, do, NT) - delta)).astype(BF)
-                    dk_ref[keys, :] += dot(ds, q, NN)
-                    return dq + dot(ds, k, TN)
-
-                dq = lax.fori_loop(0, i, functools.partial(step, False), jnp.zeros((bq, hd), F32))
-                dq = lax.fori_loop(i, total, functools.partial(step, True), dq)
-                out_ref[rows, span(base, hd)] = unrotate(dq * scale, rows).astype(BF)
-
-            def fin(i, carry):
-                rows = span(i * bq, bq)
-                out_ref[rows, span(base + hd, hd)] = unrotate(dk_ref[rows, :] * scale, rows).astype(BF)
-                out_ref[rows, span(base + 2 * hd, hd)] = dv_ref[rows, :].astype(BF)
-                return carry
-
-            return lax.fori_loop(0, seq // bq, fin, carry)
-
-        lax.fori_loop(0, heads, head, 0)
-        under.start_follow()
-        under.end()
-
-    return comm_call(
-        body, "attend_back", ident, [qkv, mixed, grad_mixed, lse, prefix, *tables],
-        [jax.ShapeDtypeStruct(qkv.shape, BF)],
-        [pltpu.VMEM((seq, hd), F32), pltpu.VMEM((seq, hd), F32)],
-        moves, flops=10 * heads * seq * seq * hd, transcendentals=heads * seq * seq,
-    )
+    def unrotate(g, rows):
+        return g * cos_ref[rows, :] - pltpu.roll(g, half, 1) * sin_ref[rows, :]
+
+    def head(h, carry):
+        base = h * 3 * hd
+        own = span(h * hd, hd)
+        dk_ref[...] = jnp.zeros_like(dk_ref)
+        dv_ref[...] = jnp.zeros_like(dv_ref)
+        for i in range(seq // bq):
+            first = i * bq
+            rows = pl.ds(first, bq)
+            q = qkv_ref[rows, span(base, hd)]
+            do = do_ref[rows, own]
+            row_sums = (do.astype(F32) * o_ref[rows, own].astype(F32)).T
+            delta = jnp.sum(row_sums, axis=0, keepdims=True)
+            tops = lse_ref[h, 0:1, first:first + bq]
+            total = max(i + 1, seq // 2 // bk)
+
+            def step(masked, j, dq, first=first, q=q, do=do, delta=delta, tops=tops):
+                keys = span(j * bk, bk)
+                k = qkv_ref[keys, span(base + hd, hd)]
+                v = qkv_ref[keys, span(base + 2 * hd, hd)]
+                p = jnp.exp(dot(k, q, NT) * scale - tops)
+                if masked:
+                    kp = j * bk + lax.broadcasted_iota(jnp.int32, (bk, bq), 0)
+                    qp = first + lax.broadcasted_iota(jnp.int32, (bk, bq), 1)
+                    p = jnp.where(kp < jnp.maximum(qp + 1, bound), p, 0.0)
+                dv_ref[keys, :] += dot(p.astype(BF), do, NN)
+                ds = (p * (dot(v, do, NT) - delta)).astype(BF)
+                dk_ref[keys, :] += dot(ds, q, NN)
+                return dq + dot(ds, k, TN)
+
+            dq = lax.fori_loop(0, i, functools.partial(step, False), jnp.zeros((bq, hd), F32))
+            dq = lax.fori_loop(i, total, functools.partial(step, True), dq)
+            out_ref[rows, span(base, hd)] = unrotate(dq * scale, rows).astype(BF)
+
+        def fin(i, carry):
+            rows = span(i * bq, bq)
+            out_ref[rows, span(base + hd, hd)] = unrotate(dk_ref[rows, :] * scale, rows).astype(BF)
+            out_ref[rows, span(base + 2 * hd, hd)] = dv_ref[rows, :].astype(BF)
+            return carry
+
+        return lax.fori_loop(0, seq // bq, fin, carry)
+
+    lax.fori_loop(0, heads, head, 0)
 
 
 def front_call(inputs, cot, prefix, tables, weights, heads, hd, ident):
@@ -994,34 +920,34 @@
         firsts, seconds, refs = refs[:8], refs[8:15], refs[15:]
         (qkv_ref, mixed_ref, lse_ref, own_in_ref, middle_ref, normed_in_out, cot_out, normed_mid_out, hidden_out,
          slopes_out), refs = refs[:10], refs[10:]
-        (arena, acc, block_ref, normed_own, w_qkv, w_out, w_ga, w_gb, w_ua, w_ub, z_sems, y_sems, load_sems, out_sems,
-         swap_send, swap_recv, phase, *sems) = refs
+        arena, acc, block_ref, normed_own, *refs = refs
+        held, refs = dict(zip(names, refs[:8])), refs[8:]
+        z_sems, y_sems, store_sems, out_sems, swap_send, swap_recv, phase, *sems = refs
         start_sems, gather_sems, reduce_sems_, feed_sems = sems[:5], sems[5:10], sems[10:14], sems[14:]
         place = Place()
         c, zl, x = place.c, place.zl, place.x
         place.meet()
-        z_moves = {n: WeightHalf(place, sources[i], firsts[i], z_sems.at[i]) for i, n in enumerate(names)}
-        y_moves = {n: Beyond(place, firsts[i], seconds[i], y_sems.at[i]) for i, n in enumerate(names[:7])}
-        held = dict(qkv=w_qkv, out=w_out, ga=w_ga, gb=w_gb, ua=w_ua, ub=w_ub)
+        z_moves = {n: WeightHalf(place, sources[i], held[n].at[0], z_sems.at[i]) for i, n in enumerate(names)}
+        y_moves = {n: Beyond(place, held[n].at[0], held[n].at[1], y_sems.at[i]) for i, n in enumerate(names[:7])}
 
         def go(name):
             z_moves[name].start()
+
+        def stores(name):
+            i = names.index(name)
+            copies = [pltpu.make_async_copy(held[name].at[0], firsts[i], store_sems.at[i, 0])]
+            if i < 7:
+                copies.append(pltpu.make_async_copy(held[name].at[1], seconds[i], store_sems.at[i, 1]))
+            return copies
 
         def pass_on(name):
             z_moves[name].wait_recv()
             y_moves[name].start()
 
-        def half_load(name, side):
-            i = names.index(name)
-            source = (firsts, seconds)[side][i]
-            return pltpu.make_async_copy(source, held[name].at[side], load_sems.at[i, side])
-
-        def load_first(name):
-            half_load(name, 0).start()
-
-        def load_second(name):
+        def got(name):
             y_moves[name].wait_recv()
-            half_load(name, 1).start()
+            for copy in stores(name):
+                copy.start()
 
         def parts(name):
             return [held[name].at[side, i] for side in (0, 1) for i in (0, 1)]
@@ -1083,11 +1009,9 @@
             if r == 0:
                 go("qkv")
         pass_on("qkv")
-        load_first("qkv")
         go("out")
         pl.when(crossed)(lambda: cot_swap().start())
-        half_load("qkv", 0).wait()
-        depth = w_qkv.shape[2]
+        depth = held["qkv"].shape[2]
         for r in range(SLICES):
             gather.near(0, r, d_chip).wait_recv()
             sib(0, r, c, d_chip).start()
@@ -1095,11 +1019,11 @@
                 sib(slot, r, 1 - c, target).wait_recv()
 
             def norm_rows(i, carry, r=r):
-                rows = span(r * size + i * 16, 16)
+                rows = span(r * size + i * NORM_ROWS, NORM_ROWS)
                 normed[rows, :] = row_norm(full[rows, :].astype(F32))[0].astype(BF)
                 return carry
 
-            lax.fori_loop(0, size // 16, norm_rows, 0)
+            lax.fori_loop(0, size // NORM_ROWS, norm_rows, 0, unroll=NORM_UNROLL)
             pltpu.make_async_copy(normed.at[rows_of(r)], normed_in_out.at[rows_of(r)], out_sems.at[r]).start()
             total = None
             for weight, index in zip(parts("qkv")[:2], place.order[:2]):
@@ -1107,9 +1031,21 @@
                 total = term if total is None else total + term
             acc[rows_of(r), :] = total
         own_in_ref[...] = full[span(place.block * piece, piece), :]
-        load_second("qkv")
-        half_load("qkv", 1).wait()
-        go("ga")
+        pass_on("out")
+
+        cot_gather = ColumnGather(place, block_ref, cot_out, gather_sems)
+
+        def forward_cot():
+            for r in range(SLICES):
+                cot_gather.forward(r)
+
+        @pl.when(place.straight)
+        def _():
+            cot_own().wait()
+            cot_gather.start()
+            go("ga")
+
+        got("qkv")
         half = size // 2
 
         def project(r, carry):
@@ -1127,22 +1063,17 @@
             return carry
 
         lax.fori_loop(0, tokens // half, project, 0)
-        pass_on("out")
-        load_first("out")
-
-        @pl.when(place.straight)
-        def _():
-            cot_own().wait()
-
         @pl.when(crossed)
         def _():
             cot_swap().wait_recv()
+            cot_gather.start()
+            go("ga")
             cot_swap().wait_send()
             for r in range(SLICES):
                 swap_copy(r, 1 - c).wait_send()
 
-        cot_gather = ColumnGather(place, block_ref, cot_out, gather_sems)
-        cot_gather.start()
+        pl.when(place.straight)(forward_cot)
+
         bound = prefix_ref[0:1, 0:1]
 
         def head(h, carry):
@@ -1177,10 +1108,8 @@
 
         lax.fori_loop(0, heads, head, 0)
         go("gb")
-        load_second("out")
-        half_load("out", 0).wait()
-        half_load("out", 1).wait()
-        cot_gather.forward(0)
+        got("out")
+        pl.when(crossed)(forward_cot)
         pass_on("ga")
 
         for r in range(SLICES):
@@ -1231,21 +1160,15 @@
             middle_ref[rows, :] = middle
             normed_own[rows, :] = row_norm(middle)[0].astype(BF)
 
-        def before_z():
+        def after_z():
             go("ua")
-            for r in range(1, SLICES):
-                cot_gather.forward(r)
-
-        def after_z():
+            go("ub")
             pass_on("gb")
-            go("ub")
-            load_first("ga")
-            load_first("gb")
-            load_second("ga")
+            got("ga")
 
         reduce_body(
             place, product(place, mixed_ref, parts("out"), False), last, [*buffers, *reduce_sems_],
-            before_z=before_z, after_z=after_z,
+            after_z=after_z,
         )
 
         full = arena.at[pl.ds(2 * tokens, tokens)]
@@ -1277,43 +1200,40 @@
 
             lax.fori_loop(0, part_width // tile, step, 0)
 
+        def begin():
+            go("da")
+            go("db")
+
         def process(owner):
             waiting.append(owner)
             if len(waiting) == 1:
-                for side in (0, 1):
-                    half_load("ga", side).wait()
                 pass_on("ua")
-                load_second("gb")
-                load_first("ua")
-                load_second("ua")
-                for side in (0, 1):
-                    half_load("ua", side).wait()
+                got("gb")
+                got("ua")
             fill(owner, 0)
             if len(waiting) == 3:
-                for side in (0, 1):
-                    half_load("gb", side).wait()
                 pass_on("ub")
-                load_first("ub")
-                go("db")
-                load_second("ub")
-                for side in (0, 1):
-                    half_load("ub", side).wait()
-                for i, earlier in enumerate(waiting):
+                got("ub")
+                for earlier in waiting:
                     fill(earlier, 1)
             elif len(waiting) > 3:
                 fill(owner, 1)
 
-        gather_body(place, normed_own, full, feed_sems, process, begin=lambda: go("da"))
+        gather_body(place, normed_own, full, feed_sems, process, begin=begin)
         for i, (ref, out) in enumerate(((full, normed_mid_out), (hidden_ref, hidden_out), (slopes_ref, slopes_out))):
             pltpu.make_async_copy(ref, out, out_sems.at[SLICES + i]).start()
         pass_on("da")
         cot_gather.finish()
         z_moves["db"].wait_recv()
-        y_moves["da"].wait_recv()
+        stores("db")[0].start()
+        got("da")
         for i, (ref, out) in enumerate(((full, normed_mid_out), (hidden_ref, hidden_out), (slopes_ref, slopes_out))):
             pltpu.make_async_copy(ref, out, out_sems.at[SLICES + i]).wait()
         for move in (*z_moves.values(), *y_moves.values()):
             move.wait_send()
+        for name in names:
+            for copy in stores(name):
+                copy.wait()
 
     def half_shape(weight):
         return jax.ShapeDtypeStruct((2, *weight.shape), BF)
@@ -1345,7 +1265,8 @@
             pltpu.VMEM((tokens, inner), F32),
             pltpu.VMEM((tokens, slice_width), BF),
             pltpu.VMEM((piece, width), BF),
-            *(pltpu.VMEM((2, 2, *weight.shape), BF) for weight in weights[:6]),
+            *(pltpu.VMEM((2, 2, *weight.shape), BF) for weight in weights[:7]),
+            pltpu.VMEM((1, 2, *weights[7].shape), BF),
             DMA((8, 4)), DMA((8, 4)), DMA((8, 2)), DMA((SLICES + 3,)), DMA((SLICES + 1,)), DMA((SLICES + 1,)),
             pltpu.SemaphoreType.REGULAR,
             *start_sems, *column_sems, *reduce_sems(), *gather_scratch(),
@@ -1426,16 +1347,156 @@
         pl.when(self.place.straight)(lambda: self.own_copy().wait())
 
 
-def finish_call(piece, moves, ident):
-    def body(place, ins, outs, scratch, under, targets):
-        spread = Spread(place, ins[0], outs[0], scratch)
-        spread.start()
-        under.start_z()
-        under.end()
-        spread.wait()
-
-    return comm_call(
-        body, "finish", ident, [piece], [spread_shape(piece)], spread_scratch(), moves, greet=spread_greet,
+def rear_call(branch_own, out_halves, qkv_halves, qkv, mixed, lse, prefix, tables, grad_middle, own_in, ready, normed_in,
+              gate_sum, up_own, up_other, heads, hd, ident):
+    tokens, inner = qkv.shape
+    piece, width = branch_own.shape
+    inner_out = mixed.shape[1]
+    block = width // 4
+    tile = 256
+
+    def kernel(
+        branch_ref, out_1, out_2, qkv_1, qkv_2, qkv_ref, mixed_ref, lse_ref, prefix_ref, cos_ref, sin_ref, middle_ref,
+        own_in_ref, ready_ref, normed_in_ref, gate_ref, up_own_ref, up_other_ref,
+        gate_out, up_out, out_out, qkv_out, ready_out, result_out,
+        full, grad_mixed, grad_rows, flipped, dk_ref, dv_ref, up_moved, out_grads, qkv_grads,
+        y_sems, z_sems, load_sem, *sems
+    ):
+        place = Place()
+        y = place.y
+        reduce_refs, sems = sems[:9], sems[9:]
+        gather_sems, ready_sems, result_sems = sems[:4], sems[4:7], sems[7:10]
+        place.meet(spread_greet)
+        y_up = Beyond(place, up_other_ref, up_moved, y_sems.at[0])
+        y_out = Beyond(place, out_grads.at[0], out_grads.at[2], y_sems.at[1])
+        y_qkv = Beyond(place, qkv_grads.at[0], qkv_grads.at[2], y_sems.at[2])
+        z_gate = GradHalf(place, gate_ref, gate_out, z_sems.at[0])
+        z_up = GradHalf(place, up_moved, up_out, z_sems.at[1])
+        z_out = GradHalf(place, out_grads.at[1], out_out, z_sems.at[2])
+        z_qkv = GradHalf(place, qkv_grads.at[1], qkv_out, z_sems.at[3])
+        y_up.start()
+
+        def add(own, moved, rows):
+            def step(i, carry):
+                where = span(i * 64, 64)
+                for j in (0, 1):
+                    total = own[j, where, :].astype(F32) + moved[j, where, :].astype(F32)
+                    own[j, where, :] = total.astype(BF)
+                return carry
+
+            lax.fori_loop(0, rows // 64, step, 0)
+
+        result_ref = full.at[pl.ds(0, piece)]
+
+        out_parts = quarters(out_1, out_2)
+
+        def process(owner):
+            rows = span(owner * piece, piece)
+            total = None
+            for weight, index in zip(out_parts, place.order):
+                part = dot(full[rows, span(index * block, block)], weight[...], NT)
+                total = part if total is None else total + part
+            grad_mixed[rows, :] = total.astype(BF)
+
+        gather_body(place, branch_ref, full, gather_sems, process, begin=z_gate.start)
+        ready_spread = Spread(place, ready_ref, ready_out, ready_sems)
+        y_up.wait_recv()
+        add(up_moved, up_own_ref, up_own.shape[1])
+        z_up.start()
+        ready_spread.start()
+
+        def flip(source, columns):
+            def step(i, carry):
+                rows = span(i * tile, tile)
+                flipped[0:columns, rows] = source[rows, :].T
+                return carry
+
+            lax.fori_loop(0, tokens // tile, step, 0)
+
+        def weigh(grads, side, which, columns):
+            def step(n, carry):
+                i, m = n // (columns // tile), lax.rem(n, columns // tile)
+                rows = span(m * tile, tile)
+                value = dot(flipped[rows, :], full[:, span((which * 2 + i) * block, block)], NN)
+                grads[side, i, rows, :] = value.astype(BF)
+                return carry
+
+            lax.fori_loop(0, 2 * (columns // tile), step, 0)
+
+        flip(mixed_ref, inner_out)
+        weigh(out_grads, 0, 1 - y, inner_out)
+        y_out.start()
+        weigh(out_grads, 1, y, inner_out)
+        load = pltpu.make_async_copy(normed_in_ref, full, load_sem.at[0])
+        load.start()
+        attend_back_body(
+            qkv_ref, mixed_ref, grad_mixed, lse_ref, prefix_ref[0:1, 0:1], cos_ref, sin_ref, grad_rows, dk_ref, dv_ref,
+            heads, hd,
+        )
+        load.wait()
+
+        def last(rows, total):
+            value = back_rows(middle_ref[rows, :], own_in_ref[rows, :].astype(F32), total)
+            result_ref[rows, :] = value.astype(BF)
+
+        def before_z():
+            flip(grad_rows, inner)
+            weigh(qkv_grads, 0, 1 - y, inner)
+            y_qkv.start()
+
+        def after_z():
+            y_out.wait_recv()
+            add(out_grads.at[1], out_grads.at[2], inner_out)
+            z_out.start()
+            weigh(qkv_grads, 1, y, inner)
+
+        reduce_body(
+            place, product(place, grad_rows, quarters(qkv_1, qkv_2), True), last, reduce_refs,
+            before_z=before_z, after_z=after_z,
+        )
+        result_spread = Spread(place, result_ref, result_out, result_sems)
+        result_spread.start()
+        y_qkv.wait_recv()
+        add(qkv_grads.at[1], qkv_grads.at[2], inner)
+        z_qkv.start()
+        for move in (z_gate, z_up, z_out, z_qkv):
+            move.wait_recv()
+        ready_spread.wait()
+        result_spread.wait()
+        for move in (y_up, y_out, y_qkv, z_gate, z_up, z_out, z_qkv):
+            move.wait_send()
+
+    shape = jax.ShapeDtypeStruct
+    spread = spread_shape(ready)
+    return pl.pallas_call(
+        kernel,
+        out_shape=[
+            shape(gate_sum.shape, BF), shape(up_own.shape, BF), shape((2, inner_out, block), BF),
+            shape((2, inner, block), BF), spread, spread,
+        ],
+        in_specs=[VMEM_WHOLE] * 14 + [ANYWHERE, ANYWHERE, VMEM_WHOLE, ANYWHERE],
+        out_specs=[ANYWHERE] * 6,
+        scratch_shapes=[
+            pltpu.VMEM((tokens, width), BF),
+            pltpu.VMEM((tokens, inner_out), BF),
+            pltpu.VMEM((tokens, inner), BF),
+            pltpu.VMEM((inner, tokens), BF),
+            pltpu.VMEM((tokens, hd), F32),
+            pltpu.VMEM((tokens, hd), F32),
+            pltpu.VMEM(up_own.shape, BF),
+            pltpu.VMEM((3, 2, inner_out, block), BF),
+            pltpu.VMEM((3, 2, inner, block), BF),
+            DMA((3, 4)), DMA((4, 4)), DMA((1,)),
+            *reduce_scratch(piece, width), *gather_scratch(), *spread_scratch(), *spread_scratch(),
+        ],
+        compiler_params=pltpu.CompilerParams(
+            collective_id=ident, has_side_effects=True, vmem_limit_bytes=(64 << 20) - (64 << 10)
+        ),
+        cost_estimate=pl.CostEstimate(flops=100 << 30, bytes_accessed=100 << 20, transcendentals=heads * tokens * tokens),
+        name="rear",
+    )(
+        branch_own, *out_halves, *qkv_halves, qkv, mixed, lse, prefix, *tables, grad_middle, own_in, ready, normed_in,
+        gate_sum, up_own, up_other,
     )
 
 
@@ -1487,21 +1548,13 @@
         hidden, (da_1, db_1), (da_2, db_2), middle,
         [("grad", joined(down_own, down_moved, 1)), ("beyond", gate_other)], 6,
     )
-    (grad_branch, grad_mixed), (gate_final, up_moved) = mix_call(
-        branch_own, (out_1, out_2), tokens,
-        [("grad", joined(gate_grad, gate_moved, 0)), ("beyond", up_other)], 7,
+    def blocks(array):
+        return array.reshape(2, array.shape[0] // 2, array.shape[1])
+
+    gate_final, up_final, out_final, qkv_final, outputs, input_grad = rear_call(
+        branch_own, (out_1, out_2), (qkv_1, qkv_2), qkv, mixed, lse, prefix, tables, grad_middle, own_in, outputs,
+        normed_in, joined(gate_grad, gate_moved, 0), blocks(up_grad.astype(BF)), blocks(up_other), heads, hd, 7,
     )
-    out_grad, out_other = halves("tc,td->cd", mixed, grad_branch, 1)
-    (grad_rows,), (up_final, out_moved) = attend_back_call(
-        qkv, mixed, grad_mixed, lse, prefix, tables, heads, hd,
-        [("grad", joined(up_grad, up_moved, 0)), ("beyond", out_other)], 8,
-    )
-    qkv_grad, qkv_other = halves("td,te->de", normed_in, grad_rows, 0)
-    (input_grad, outputs), (out_final, qkv_moved) = input_call(
-        grad_rows, (qkv_1, qkv_2), grad_middle, own_in, outputs,
-        [("grad", joined(out_grad, out_moved, 1)), ("beyond", qkv_other)], 9,
-    )
-    (input_grad,), (qkv_final,) = finish_call(input_grad, [("grad", joined(qkv_grad, qkv_moved, 0))], 10)
 
     def summed(parts):
         return parts[0].astype(F32) + parts[1].astype(F32)
@@ -1509,7 +1562,7 @@
     return (
         outputs,
         input_grad.astype(F32),
-        summed(qkv_final).reshape(-1, heads, 3 * hd),
+        summed(qkv_final).T.reshape(-1, heads, 3 * hd),
         summed(out_final),
         jnp.stack([summed(gate_final), summed(up_final)], axis=1),
         summed(down_final),

time: 855 us -> 785 us (0.918)
  Pallas kernels: 721 us -> 676 us
  matrix products: 75.2 us -> 48.7 us
    pallas_call x6 -> x2, Pallas kernels: 415 us -> 163 us  [comm_call(): pl.pallas_call(kernel, out_shape=shapes, in_specs=in_specs, out_specs=[VM...]
    pallas_call x0 -> x1, Pallas kernels: none -> 210 us  [rear_call(): pl.pallas_call(kernel, out_shape=[shape(gate_sum.shape, BF), shape(up_own...]
    dot_general x10 -> x6, matrix products: 75.2 us -> 48.7 us  [mm(): return jnp.einsum(spec, left, right, preferred_element_type=F32)]
where the time goes in v5:
time: 785 us; the launch traced here: 775 us
  Pallas kernels  676 us (86%)
  matrix products  48.7 us (6%)
  local copies, waits for them, and re-layouts  27.6 us (4%)
  other arithmetic  15.1 us (2%)
    pallas_call x1, Pallas kernels, front_call(): pl.pallas_call(kernel, out_shape=outs, in_specs=[ANYWHERE, ANYWHERE, VMEM...  303 us
    pallas_call x1, Pallas kernels, rear_call(): pl.pallas_call(kernel, out_shape=[shape(gate_sum.shape, BF), shape(up_own...  210 us
    pallas_call x2, Pallas kernels, comm_call(): pl.pallas_call(kernel, out_shape=shapes, in_specs=in_specs, out_specs=[VM...  163 us
    dot_general x6, matrix products, mm(): return jnp.einsum(spec, left, right, preferred_element_type=F32)  48.7 us
  transfers between devices with their start and end apart: 1, of which 0 were waited for; matrix products, arithmetic and copies ran while one was open for 2% of the time, Pallas kernels for 0%

profile of v5, /device:TPU:1, one launch (start us, length us, event | category | flops | bytes accessed | tf_op | source)
XLA Modules:
  0.0 774.6 jit_solution(4079138132013083979)
XLA Ops:
  0.6 5.7 collective-permute-start
  6.4 2.1 copy.34
  8.6 2.2 fusion.48
  10.8 4.2 fusion.47
  15.0 3.7 fusion.40
  18.8 2.8 copy_bitcast_fusion
  21.6 1.2 copy_bitcast_fusion.2
  22.8 1.9 pad_maximum_fusion.1
  24.7 0.0 collective-permute-done
  24.7 1.1 broadcast_in_dim.5.prefix_ref
  25.9 303.1 %front.1 = (bf16[2,512,768]{2,1,0:T(8,128)(2,1)}, bf16[2,256,512]{2,1,0:T(8,128)(2,1)}, bf16[2,512,512]{2,1,0:T(8,128)(2,1)}, bf16[2,512,512]{2,1,0:T(8,128)(2,1...) custom-call(bf16[2048,256]{1,0:T(8,128)(2,1)} %in_ref.1, ...), custom_call_target="tpu_custom_call" | custom-call | flops 107374182400 | bytes 104857600 | tf_op jit(solution)/shard_map/front/pallas_call | solution.py:1258
  329.0 9.4 %fusion.31.refs_15_ = bf16[1024,1024]{1,0:T(8,128)(2,1)} fusion(bf16[2048,1024]{1,0:T(8,128)(2,1)} %get-tuple-element.59.refs_0_, bf16[2048,2048]{1,0:T(8,128)(2,1)} %get-tuple-element.45.refs_0_, s32[]{:T(128)S(6)} %select_n.4), kind=kOutput, calls=%fused_computation.25 | convolution fusion | flops 4296015872 | bytes 10485764 | tf_op jit(solution)/shard_map/tf,td->fd/dot_general | solution.py:165
  338.3 92.6 %reduce_middle.1 = (f32[256,2048]{1,0:T(8,128)}, bf16[256,2048]{1,0:T(8,128)(2,1)}, bf16[2048,2048]{1,0:T(8,128)(2,1)}, bf16[2,512,512]{2,1,0:T(8,128)(2,1)}, bf16[1024,1024]{1,0:T(8,128)(2,1)}) custom-call(bf16[2048,2048]{1,0:T(8,128)(2,1)} %get-tuple-element.45.refs_0_, bf16[2048,2048]{1,0:T(8,128)(2,1)} %get-tuple-element.46.refs_1_, ...), custom_call_target="tpu_custom_call" | custom-call | flops 47244640256 | bytes 48234496 | tf_op jit(solution)/shard_map/reduce_middle/pallas_call | solution.py:471
  431.0 9.6 %fusion.26 = bf16[1024,1024]{1,0:T(8,128)(2,1)} fusion(bf16[2048,2048]{1,0:T(8,128)(2,1)} %get-tuple-element.73, bf16[2048,2048]{1,0:T(8,128)(2,1)} %get-tuple-element.72, s32[]{:T(128)S(6)} %select_n.4), kind=kOutput, calls=%fused_computation.24 | convolution fusion | flops 4296015872 | bytes 10485764 | tf_op jit(solution)/shard_map/td,tf->df/dot_general | solution.py:165
  440.6 8.1 %fusion.16.refs_7_ = bf16[1024,1024]{1,0:T(8,128)(2,1)} fusion(bf16[2048,2048]{1,0:T(8,128)(2,1)} %get-tuple-element.73, bf16[2048,2048]{1,0:T(8,128)(2,1)S(1)} %copy-done.6, s32[]{:T(128)S(6)} %select_n.4), kind=kOutput, calls=%fused_computation.22 | convolution fusion | flops 4296015872 | bytes 10485764 | tf_op jit(solution)/shard_map/td,tf->df/dot_general | solution.py:165
  448.7 5.9 fusion.21
  454.7 5.8 add_convert_fusion.1
  460.4 2.9 copy.25
  463.3 2.6 copy.26
  465.8 70.1 %reduce_down.1 = (bf16[256,2048]{1,0:T(8,128)(2,1)}, bf16[2,1024,512]{2,1,0:T(8,128)(2,1)}, bf16[1024,1024]{1,0:T(8,128)(2,1)}) custom-call(bf16[2048,1024]{1,0:T(8,128)(2,1)} %get-tuple-element.59.refs_0_, bf16[2,512,512]{2,1,0:T(8,128)(2,1)} %get-tuple-element.56.refs_11_.refs_1_, bf16[2,512,512]{2,1,0:T(8,128)(2,1)} %get-tuple-element.58.refs_13_.refs_14_.refs_2_, ...), custom_call_target="tpu_custom_call" | custom-call | flops 30064771072 | bytes 19922944 | tf_op jit(solution)/shard_map/reduce_down/pallas_call | solution.py:471
  535.9 10.0 %add_convert_fusion = bf16[1024,1024]{1,0:T(8,128)(2,1)} fusion(bf16[1024,1024]{1,0:T(8,128)(2,1)} %get-tuple-element.76, bf16[2048,2048]{1,0:T(8,128)(2,1)} %get-tuple-element.73, bf16[2048,2048]{1,0:T(8,128)(2,1)} %get-tuple-element.72, s32[]{:T(128)S(6)} %select_n.5), kind=kOutput, calls=%fused_computation.1 | convolution fusion | flops 4298113024 | bytes 12582916 | tf_op jit(solution)/shard_map/td,tf->df/dot_general | solution.py:165
  545.9 210.4 %rear.1 = (bf16[2,512,1024]{2,1,0:T(8,128)(2,1)}, bf16[2,512,1024]{2,1,0:T(8,128)(2,1)}, bf16[2,256,512]{2,1,0:T(8,128)(2,1)}, bf16[2,768,512]{2,1,0:T(8,128)(2,...) custom-call(bf16[256,2048]{1,0:T(8,128)(2,1)} %get-tuple-element.60.branch_ref, ...), custom_call_target="tpu_custom_call" | custom-call | flops 107374182400 | bytes 104857600 | tf_op jit(solution)/shard_map/rear/pallas_call | solution.py:1471
  756.3 2.0 add_bitcast_fusion.3
  758.3 1.6 convert_add_fusion
  759.9 2.1 copy.27
  762.0 1.5 convert_element_type.131
  763.5 1.9 add_bitcast_fusion.2
  765.4 0.4 add_bitcast_fusion.1
  765.8 0.5 pad_maximum_fusion
  766.3 5.2 copy.28
  771.6 1.6 add_bitcast_fusion
  773.2 1.0 copy.40
  (30 shorter events, 0.1 us)
Async XLA Ops:
  0.6 10.2 %copy-start = (bf16[512,2,1024]{2,1,0:T(2,128)(2,1)S(1)}, bf16[512,2,1024]{2,1,0:T(2,128)(2,1)}, u32[]{:S(2)}) copy-start(bf16[512,2,1024]{2,1,0:T(2,128)(2,1)} %param.11) | copy-start | bytes 6291460
  0.6 24.1 %collective-permute-start = (s32[1]{0:T(128)}, s32[1]{0:T(128)}, u32[]{:S(2)}, u32[]{:S(2)}) collective-permute-start(s32[1]{0:T(128)} %param.8), channel_id=1, source_target_pairs={{0,0},{4,8},{8,4},{12,12},{1,1},{5,9},{9,5},{13,13},{2,2},{6,10},{... | collective-permute-start | bytes 20 | tf_op jit(solution)/shard_map/ppermute | solution.py:1508
  15.0 6.5 copy-start.1
  430.9 9.6 %copy-start.6 = (bf16[2048,2048]{1,0:T(8,128)(2,1)S(1)}, bf16[2048,2048]{1,0:T(8,128)(2,1)}, u32[]{:S(2)}) copy-start(bf16[2048,2048]{1,0:T(8,128)(2,1)} %get-tuple-element.72) | copy-start | bytes 25165828
  431.0 17.7 %slice-start = ((s8[8388608]{0:T(1024)(128)(4,1)}), s8[4194304]{0:T(1024)(128)(4,1)S(1)}, s32[]{:S(2)}) async-start(s8[8388608]{0:T(1024)(128)(4,1)} %bitcast.39), calls=%async_computation | async-start | bytes 8388608
  440.6 8.1 %slice-start.1 = ((s8[8388608]{0:T(1024)(128)(4,1)}), s8[4194304]{0:T(1024)(128)(4,1)S(1)}, s32[]{:S(2)}) async-start(s8[8388608]{0:T(1024)(128)(4,1)} %bitcast.39), calls=%async_computation.1 | async-start | bytes 8388608
  440.6 14.1 %slice-start.2 = ((s8[8388608]{0:T(1024)(128)(4,1)}), s8[4194304]{0:T(1024)(128)(4,1)S(1)}, s32[]{:S(2)}) async-start(s8[8388608]{0:T(1024)(128)(4,1)} %bitcast.41), calls=%async_computation.2 | async-start | bytes 8388608
  448.7 6.0 slice-start.3
  448.7 6.0 copy-start.7
  448.7 6.0 copy-start.8
  756.3 5.7 copy-start.4
  762.0 3.4 copy-start.3
  766.3 5.3 copy-start.2
  771.6 1.6 copy-start.5

commit v6 on v5

--- a/solution.py
+++ b/solution.py
@@ -514,7 +514,7 @@
     pass
 
 
-def reduce_body(place, compute, last, scratch, begin=nothing, before_z=nothing, after_z=nothing):
+def reduce_body(place, compute, last, scratch, begin=nothing, before_z=nothing, after_z=nothing, split=0):
     sib_out, sib_in, own, near_out, near_in, sib_send, sib_recv, near_send, near_recv = scratch
     piece = own.shape[1]
     c = place.c
@@ -524,8 +524,8 @@
     def sib_copy(step):
         return remote(sib_out.at[step], sib_in.at[step], sib_send.at[step], sib_recv.at[step], place.sibling)
 
-    def near_copy(step, r):
-        device = place.along if step == 2 else place.across
+    def near_copy(step, r, turned=False):
+        device = place.along if step == 2 or turned else place.across
         rows = span(r * size, size)
         return remote(
             near_out.at[step, rows], near_in.at[step, rows], near_send.at[step, r], near_recv.at[step, r], device
@@ -535,18 +535,20 @@
         slot = step % 2
         sib_copy(step).wait_recv()
 
-        def send(r, carry):
-            if step == 2:
+        def send(joins, turned, r, carry):
+            if joins:
                 near_copy(0, r).wait_recv()
             rows = span(r * size, size)
             total = own[slot, rows, :].astype(F32) + sib_in[step, rows, :].astype(F32)
-            if step == 2:
+            if joins:
                 total = total + near_in[0, rows, :].astype(F32)
             near_out[step, rows, :] = total.astype(BF)
-            near_copy(step, r).start()
+            near_copy(step, r, turned).start()
             return carry
 
-        lax.fori_loop(0, SLICES, send, 0)
+        lax.fori_loop(0, SLICES - split, functools.partial(send, step == 2, False), 0)
+        if split:
+            lax.fori_loop(SLICES - split, SLICES, functools.partial(send, step == 1, step == 0), 0)
 
     def step(s, carry):
         target = place.chip(1 - lax.rem(s, 2), 1 - s // 2)
@@ -621,11 +623,74 @@
     return dict(begin=begin, after_z=under.start_follow)
 
 
-def down_call(hidden, firsts, seconds, middle, moves, ident):
+class Turned:
+    def __init__(self, source, stage, sems, flipped):
+        self.source, self.stage, self.sems, self.flipped = source, stage, sems, flipped
+        self.tile = stage.shape[1]
+        self.count = flipped.shape[1] // self.tile
+
+    def load(self, i):
+        slot = lax.rem(i, 2)
+        rows = span(i * self.tile, self.tile)
+        return pltpu.make_async_copy(self.source.at[rows], self.stage.at[slot], self.sems.at[slot])
+
+    def turn(self):
+        def step(i, carry):
+            self.load(i).wait()
+
+            @pl.when(i + 1 < self.count)
+            def _():
+                self.load(i + 1).start()
+
+            self.flipped[:, span(i * self.tile, self.tile)] = self.stage[lax.rem(i, 2)].T
+            return carry
+
+        self.load(0).start()
+        lax.fori_loop(0, self.count, step, 0)
+
+    def times(self, right, out, first, offset):
+        block, columns = out.shape[1:]
+        half = columns // 2
+        each = block // self.tile
+
+        def step(n, carry):
+            m, t = n // 2, lax.rem(n, 2)
+            left = self.flipped[span(first + m * self.tile, self.tile), :]
+            value = dot(left, right[:, span(offset + t * half, half)], NN)
+            out[m // each, span(lax.rem(m, each) * self.tile, self.tile), span(t * half, half)] = value.astype(BF)
+            return carry
+
+        lax.fori_loop(0, 4 * each, step, 0)
+
+
+def down_call(hidden, firsts, seconds, middle, owns, moved, normed, grads, gate_other, ident):
     piece, width = middle.shape
-
-    def body(place, ins, outs, scratch, under, targets):
-        hidden_ref, first_a, first_b, second_a, second_b, base_ref = ins
+    tokens, both = grads.shape
+    part_width = both // 2
+    block = width // 4
+    tile = 256
+
+    def kernel(
+        hidden_ref, first_a, first_b, second_a, second_b, base_ref, own_0, own_1, moved_0, moved_1, grads_ref, normed_ref, gate_other,
+        result_ref, down_out, gate_out, up_own_out, up_other_out,
+        down_sum, stage, flipped, gate_moved, kept, spare,
+        y_sems, z_sems, load_sems, store_sems, *reduce_refs
+    ):
+        place = Place()
+        place.meet()
+        y = place.y
+
+        turned = Turned(normed_ref, stage, load_sems, flipped)
+        for j, (own, came) in enumerate(((own_0, moved_0), (own_1, moved_1))):
+            def step(i, carry, j=j, own=own, came=came):
+                rows = span(i * 64, 64)
+                down_sum[j, rows, :] = (own[rows, :].astype(F32) + came[rows, :].astype(F32)).astype(BF)
+                return carry
+
+            lax.fori_loop(0, own_0.shape[0] // 64, step, 0)
+        z_down = GradHalf(place, down_sum, down_out, z_sems.at[0])
+        y_gate = Beyond(place, gate_other, gate_moved, y_sems.at[0])
+        y_gate.start()
         parts = list(zip(quarters(first_a, second_a), quarters(first_b, second_b), place.order))
 
         def compute(owner, out_ref):
@@ -636,18 +701,58 @@
                 out_ref[:, span(index * size, size)] = part.astype(out_ref.dtype)
 
         def last(rows, total):
-            outs[0][rows, :] = (base_ref[rows, :] + total).astype(BF)
-
-        reduce_body(place, compute, last, scratch, **beside(under))
-        under.end()
-
-    return comm_call(
-        body, "reduce_down", ident, [hidden, *firsts, *seconds, middle], [jax.ShapeDtypeStruct((piece, width), BF)],
-        reduce_scratch(piece, width), moves, flops=2 * hidden.size * width,
-    )
-
-
-def middle_call(cot, slopes, gates, ups, downs, down_last, moves, middle, ident):
+            result_ref[rows, :] = (base_ref[rows, :] + total).astype(BF)
+
+        def store(out, ref, i):
+            return pltpu.make_async_copy(ref, out, store_sems.at[i])
+
+        def after_z():
+            turned.times(grads_ref, spare, (1 - y) * (width // 2), part_width)
+            store(up_other_out, spare, 0).start()
+            turned.times(grads_ref, kept, y * (width // 2), 0)
+            store(up_other_out, spare, 0).wait()
+            turned.times(grads_ref, spare, y * (width // 2), part_width)
+            store(up_own_out, spare, 1).start()
+
+        reduce_body(place, compute, last, reduce_refs, begin=z_down.start, before_z=turned.turn, after_z=after_z)
+        y_gate.wait_recv()
+        for i in (0, 1):
+            def add(n, carry, i=i):
+                rows = span(n * 64, 64)
+                kept[i, rows, :] = (kept[i, rows, :].astype(F32) + gate_moved[i, rows, :].astype(F32)).astype(BF)
+                return carry
+
+            lax.fori_loop(0, block // 64, add, 0)
+        store(gate_out, kept, 2).start()
+        z_down.wait_recv()
+        store(up_own_out, spare, 1).wait()
+        store(gate_out, kept, 2).wait()
+        for move in (z_down, y_gate):
+            move.wait_send()
+
+    shape = jax.ShapeDtypeStruct
+    half = shape((2, block, part_width), BF)
+    down_shape = (2, *owns[0].shape)
+    held = pltpu.VMEM(half.shape, BF)
+    return pl.pallas_call(
+        kernel,
+        out_shape=[shape((piece, width), BF), shape(down_shape, BF), half, half, half],
+        in_specs=[VMEM_WHOLE] * 11 + [ANYWHERE] * 2,
+        out_specs=[VMEM_WHOLE] + [ANYWHERE] * 4,
+        scratch_shapes=[
+            pltpu.VMEM(down_shape, BF),
+            pltpu.VMEM((2, tile, width), BF),
+            pltpu.VMEM((width, tokens), BF),
+            held, held, held,
+            DMA((1, 4)), DMA((1, 4)), DMA((2,)), DMA((3,)), *reduce_scratch(piece, width),
+        ],
+        compiler_params=pltpu.CompilerParams(collective_id=ident, has_side_effects=True, vmem_limit_bytes=63 << 20),
+        cost_estimate=pl.CostEstimate(flops=60 << 30, bytes_accessed=60 << 20, transcendentals=0),
+        name="reduce_down",
+    )(hidden, *firsts, *seconds, middle, *owns, *moved, grads, normed, gate_other)
+
+
+def middle_call(cot, slopes, gates, ups, downs, down_last, normed, moves, middle, ident):
     piece, width = middle.shape
     tokens, part_width = cot.shape[0], down_last.shape[1]
     hidden = 2 * part_width
@@ -655,13 +760,19 @@
     tiles = part_width // tile
 
     def body(place, ins, outs, scratch, under, targets):
-        cot_ref, slopes_ref, ga1, ga2, gb1, gb2, ua1, ua2, ub1, ub2, value_ref, da1, da2, db1 = ins
-        total_ref, branch_ref, grad_ref = outs
-        load_sem, *rest = scratch
+        cot_hbm, slopes_ref, normed_ref, ga1, ga2, gb1, gb2, ua1, ua2, ub1, ub2, value_ref, da1, da2, db1 = ins
+        total_ref, branch_ref, grad_ref, gate_other = outs
+        load_sem, cot_ref, base_ref, stage, *rest = scratch
         under.start_y()
-        load = pltpu.make_async_copy(slopes_ref, grad_ref, load_sem.at[0])
-        load.start()
-        load.wait()
+        loads = [
+            pltpu.make_async_copy(slopes_ref, grad_ref, load_sem.at[0]),
+            pltpu.make_async_copy(cot_hbm, cot_ref, load_sem.at[1]),
+        ]
+        for load in loads:
+            load.start()
+        for load in loads:
+            load.wait()
+        base_ref[...] = cot_ref[span(place.block * piece, piece), :]
         rows_in = (quarters(da1, da2), quarters(db1, targets[0]))
 
         def fill(owner, part):
@@ -701,24 +812,33 @@
                 out_ref[:, span(index * size, size)] = total.astype(out_ref.dtype)
 
         def last(rows, total):
-            base = cot_ref[own_rows(rows), :].astype(F32)
+            base = base_ref[rows, :].astype(F32)
             grad = back_rows(base, value_ref[rows, :], total)
             total_ref[rows, :] = grad
             branch_ref[rows, :] = grad.astype(BF)
 
-        def own_rows(rows):
-            return pl.ds(pl.multiple_of(place.block * piece + rows.start, 16), rows.size)
-
-        reduce_body(place, compute, last, rest)
+        turned = Turned(normed_ref, stage, load_sem, cot_ref)
+
+        def after_z():
+            turned.turn()
+            turned.times(grad_ref, gate_other, (1 - place.y) * (width // 2), 0)
+
+        reduce_body(place, compute, last, rest, after_z=after_z, split=2)
         under.end(skip=1)
 
     shape = functools.partial(jax.ShapeDtypeStruct, (piece, width))
     return comm_call(
-        body, "reduce_middle", ident, [cot, slopes, *gates, *ups, middle, *downs, down_last],
-        [shape(F32), shape(BF), jax.ShapeDtypeStruct((tokens, 2 * hidden), BF)],
-        [DMA((1,)), *reduce_scratch(piece, width)],
+        body, "reduce_middle", ident, [cot, slopes, normed, *gates, *ups, middle, *downs, down_last],
+        [
+            shape(F32), shape(BF), jax.ShapeDtypeStruct((tokens, 2 * hidden), BF),
+            jax.ShapeDtypeStruct((2, width // 4, hidden), BF),
+        ],
+        [
+            DMA((2,)), pltpu.VMEM((tokens, width), BF), pltpu.VMEM((piece, width), BF), pltpu.VMEM((2, tile, width), BF),
+            *reduce_scratch(piece, width),
+        ],
         moves, flops=6 * tokens * hidden * width,
-        spaces=[VMEM_WHOLE, ANYWHERE] + [VMEM_WHOLE] * 12,
+        spaces=[ANYWHERE] * 3 + [VMEM_WHOLE] * 12,
     )
 
 
@@ -726,15 +846,15 @@
     return [DMA((3, SLICES)), DMA((3, SLICES)), DMA((4,)), DMA((4,))]
 
 
-def gather_body(place, own_ref, full, sems, process, begin=nothing, follow=nothing):
+def gather_body(place, own_ref, full, sems, process, begin=nothing, follow=nothing, split=0):
     near_send, near_recv, sib_send, sib_recv = sems
     piece = own_ref.shape[0]
     size = piece // SLICES
     c = place.c
 
-    def near_copy(slot, r, target):
+    def near_copy(slot, r, target, turned=False):
         where = full.at[span((c * 4 + target) * piece + r * size, size)]
-        device = place.along if slot == 2 else place.across
+        device = place.along if slot == 2 or turned else place.across
         return remote(where, where, near_send.at[slot, r], near_recv.at[slot, r], device)
 
     def sib_copy(slot, core, target):
@@ -757,14 +877,22 @@
 
     def forward(r):
         near_copy(2, r, z_chip).wait_recv()
-        near_copy(0, r, z_chip).start()
+        if r < SLICES - split:
+            near_copy(0, r, z_chip).start()
 
     process(c * 4 + mine)
     forward(0)
     sib_copy(3, 1 - c, mine).wait_recv()
     process((1 - c) * 4 + mine)
     forward(1)
-    slices(lambda r: near_copy(1, r, x_chip).wait_recv())
+
+    def arrived(r):
+        near_copy(1, r, x_chip).wait_recv()
+
+    for r in range(SLICES):
+        arrived(r)
+        if r >= SLICES - split:
+            near_copy(0, r, x_chip, True).start()
     sib_copy(1, c, x_chip).start()
     process(c * 4 + x_chip)
     for r in range(2, SLICES):
@@ -935,10 +1063,11 @@
 
         def stores(name):
             i = names.index(name)
-            copies = [pltpu.make_async_copy(held[name].at[0], firsts[i], store_sems.at[i, 0])]
-            if i < 7:
-                copies.append(pltpu.make_async_copy(held[name].at[1], seconds[i], store_sems.at[i, 1]))
-            return copies
+            return [
+                pltpu.make_async_copy(held[name].at[side], out[i], store_sems.at[i, side])
+                for side, out in enumerate((firsts, seconds[:7]))
+                if i < len(out)
+            ]
 
         def pass_on(name):
             z_moves[name].wait_recv()
@@ -1168,7 +1297,7 @@
 
         reduce_body(
             place, product(place, mixed_ref, parts("out"), False), last, [*buffers, *reduce_sems_],
-            after_z=after_z,
+            after_z=after_z, split=0,
         )
 
         full = arena.at[pl.ds(2 * tokens, tokens)]
@@ -1219,7 +1348,7 @@
             elif len(waiting) > 3:
                 fill(owner, 1)
 
-        gather_body(place, normed_own, full, feed_sems, process, begin=begin)
+        gather_body(place, normed_own, full, feed_sems, process, begin=begin, split=0)
         for i, (ref, out) in enumerate(((full, normed_mid_out), (hidden_ref, hidden_out), (slopes_ref, slopes_out))):
             pltpu.make_async_copy(ref, out, out_sems.at[SLICES + i]).start()
         pass_on("da")
@@ -1398,7 +1527,7 @@
                 total = part if total is None else total + part
             grad_mixed[rows, :] = total.astype(BF)
 
-        gather_body(place, branch_ref, full, gather_sems, process, begin=z_gate.start)
+        gather_body(place, branch_ref, full, gather_sems, process, begin=z_gate.start, split=0)
         ready_spread = Spread(place, ready_ref, ready_out, ready_sems)
         y_up.wait_recv()
         add(up_moved, up_own_ref, up_own.shape[1])
@@ -1452,7 +1581,7 @@
 
         reduce_body(
             place, product(place, grad_rows, quarters(qkv_1, qkv_2), True), last, reduce_refs,
-            before_z=before_z, after_z=after_z,
+            before_z=before_z, after_z=after_z, split=0,
         )
         result_spread = Spread(place, result_ref, result_out, result_sems)
         result_spread.start()
@@ -1521,39 +1650,24 @@
     qkv, mixed, lse, own_in, middle, normed_in, cot_full, normed_mid, hidden, slopes = results
     gates = (ga_1, ga_2, gb_1, gb_2)
 
-    def halves(spec, left, right, axis):
-        side = left if axis == 0 else right
-        half = side.shape[1] // 2
-
-        def cut(which):
-            taken = lax.dynamic_slice_in_dim(side, which * half, half, 1)
-            return mm(spec, taken, right) if axis == 0 else mm(spec, left, taken)
-
-        return cut(y), cut(1 - y).astype(BF)
-
-    def joined(own, moved, axis):
-        total = (own + moved.astype(F32)).astype(BF)
-        if axis == 0:
-            return total.reshape(2, total.shape[0] // 2, total.shape[1])
-        return jnp.swapaxes(total.reshape(total.shape[0], 2, total.shape[1] // 2), 0, 1)
-
-    down_own, down_other = halves("tf,td->fd", hidden, cot_full, 1)
-    (grad_middle, branch_own, grad_gate_up), (db_2, down_moved) = middle_call(
-        cot_full, slopes, gates, (ua_1, ua_2, ub_1, ub_2), (da_1, da_2), db_1,
-        [("beyond", db_1), ("beyond", down_other)], middle, 5,
+    block = cot_full.shape[1] // 4
+
+    def down_block(index):
+        cut = lax.dynamic_slice_in_dim(cot_full, index * block, block, 1)
+        return mm("tf,td->fd", hidden, cut).astype(BF)
+
+    owns = [down_block(2 * y + i) for i in (0, 1)]
+    others = [down_block(2 * (1 - y) + i) for i in (0, 1)]
+    (grad_middle, branch_own, grad_gate_up, gate_other), (db_2, *moved) = middle_call(
+        cot_full, slopes, gates, (ua_1, ua_2, ub_1, ub_2), (da_1, da_2), db_1, normed_mid,
+        [("beyond", db_1), *(("beyond", other) for other in others)], middle, 5,
     )
-    gate_grad, gate_other = halves("td,tf->df", normed_mid, grad_gate_up[:, :hidden_width], 0)
-    up_grad, up_other = halves("td,tf->df", normed_mid, grad_gate_up[:, hidden_width:], 0)
-    (outputs,), (down_final, gate_moved) = down_call(
-        hidden, (da_1, db_1), (da_2, db_2), middle,
-        [("grad", joined(down_own, down_moved, 1)), ("beyond", gate_other)], 6,
+    outputs, down_final, gate_sum, up_own, up_other = down_call(
+        hidden, (da_1, db_1), (da_2, db_2), middle, owns, moved, normed_mid, grad_gate_up, gate_other, 6
     )
-    def blocks(array):
-        return array.reshape(2, array.shape[0] // 2, array.shape[1])
-
     gate_final, up_final, out_final, qkv_final, outputs, input_grad = rear_call(
         branch_own, (out_1, out_2), (qkv_1, qkv_2), qkv, mixed, lse, prefix, tables, grad_middle, own_in, outputs,
-        normed_in, joined(gate_grad, gate_moved, 0), blocks(up_grad.astype(BF)), blocks(up_other), heads, hd, 7,
+        normed_in, gate_sum, up_own, up_other, heads, hd, 7,
     )
 
     def summed(parts):

time: 785 us -> 758 us (0.966)
  matrix products: 48.7 us -> 19.4 us
  Pallas kernels: 676 us -> 687 us
    pallas_call x0 -> x1, Pallas kernels: none -> 81.3 us  [down_call(): pl.pallas_call(kernel, out_shape=[shape((piece, width), BF), shape(down_s...]
    pallas_call x2 -> x1, Pallas kernels: 163 us -> 92.2 us  [comm_call(): pl.pallas_call(kernel, out_shape=shapes, in_specs=in_specs, out_specs=[VM...]
    dot_general x6 -> x4, matrix products: 48.7 us -> 19.4 us  [mm(): return jnp.einsum(spec, left, right, preferred_element_type=F32)]
where the time goes in v6:
time: 758 us; the launch traced here: 748 us
  Pallas kernels  687 us (91%)
  local copies, waits for them, and re-layouts  20.7 us (3%)
  matrix products  19.4 us (3%)
  other arithmetic  14.2 us (2%)
    pallas_call x1, Pallas kernels, front_call(): pl.pallas_call(kernel, out_shape=outs, in_specs=[ANYWHERE, ANYWHERE, VMEM...  303 us
    pallas_call x1, Pallas kernels, rear_call(): pl.pallas_call(kernel, out_shape=[shape(gate_sum.shape, BF), shape(up_own...  211 us
    pallas_call x1, Pallas kernels, comm_call(): pl.pallas_call(kernel, out_shape=shapes, in_specs=in_specs, out_specs=[VM...  92.2 us
    pallas_call x1, Pallas kernels, down_call(): pl.pallas_call(kernel, out_shape=[shape((piece, width), BF), shape(down_s...  81.3 us
    dot_general x4, matrix products, mm(): return jnp.einsum(spec, left, right, preferred_element_type=F32)  19.4 us
  transfers between devices with their start and end apart: 1, of which 0 were waited for; matrix products, arithmetic and copies ran while one was open for 2% of the time, Pallas kernels for 0%

profile of v6, /device:TPU:1, one launch (start us, length us, event | category | flops | bytes accessed | tf_op | source)
XLA Modules:
  0.0 748.3 jit_solution(15650491862718970805)
XLA Ops:
  0.6 5.6 collective-permute-start
  6.3 2.1 copy.23
  8.4 5.2 fusion.25
  13.7 1.1 fusion.26
  14.8 3.7 fusion.20
  18.5 1.2 copy_bitcast_fusion.2
  19.7 1.3 copy_bitcast_fusion
  21.0 1.9 pad_maximum_fusion.1
  22.9 0.0 collective-permute-done
  22.9 1.3 broadcast_in_dim.5.prefix_ref
  24.2 302.8 %front.1 = (bf16[2,512,768]{2,1,0:T(8,128)(2,1)}, bf16[2,256,512]{2,1,0:T(8,128)(2,1)}, bf16[2,512,512]{2,1,0:T(8,128)(2,1)}, bf16[2,512,512]{2,1,0:T(8,128)(2,1...) custom-call(bf16[2048,256]{1,0:T(8,128)(2,1)} %in_ref.1, ...), custom_call_target="tpu_custom_call" | custom-call | flops 107374182400 | bytes 104857600 | tf_op jit(solution)/shard_map/front/pallas_call | solution.py:1387
  327.0 0.0 slice-start
  327.1 0.0 copy-start.6
  327.1 6.3 fusion.8.refs_16_
  333.4 6.3 fusion.11.refs_17_
  339.8 0.0 copy-done.6
  339.8 3.3 fusion.14.own_0
  343.1 3.4 fusion.17.own_1
  346.5 92.2 %reduce_middle.1 = (f32[256,2048]{1,0:T(8,128)}, bf16[256,2048]{1,0:T(8,128)(2,1)}, bf16[2048,2048]{1,0:T(8,128)(2,1)}, bf16[2,512,1024]{2,1,0:T(8,128)(2,1)}, b...) custom-call(bf16[2048,2048]{1,0:T(8,128)(2,1)} %get-tuple-element.49.refs_0_, ...), custom_call_target="tpu_custom_call" | custom-call | flops 47244640256 | bytes 58720256 | tf_op jit(solution)/shard_map/reduce_middle/pallas_call | solution.py:471
  438.7 81.3 %reduce_down.1 = (bf16[256,2048]{1,0:T(8,128)(2,1)}, bf16[2,1024,512]{2,1,0:T(8,128)(2,1)}, bf16[2,512,1024]{2,1,0:T(8,128)(2,1)}, bf16[2,512,1024]{2,1,0:T(8,128)(2,1)}, bf16[2,512,1024]{2,1,0:T(8,128)(2,1)}) custom-call(bf16[2048,1024]{1,0:T(8,128)(2,1)} %get-tuple-element.64.hidden_ref, bf16[2,512,512]{2,1,0:T(8,128)(2,1)} %get-tuple-element.61.refs_12_.first_a, ...), custom_call_target="tpu_custom_call" | custom-call | flops 64424509440 | bytes 62914560 | tf_op jit(solution)/shard_map/reduce_down/pallas_call | solution.py:737
  520.1 211.1 %rear.1 = (bf16[2,512,1024]{2,1,0:T(8,128)(2,1)}, bf16[2,512,1024]{2,1,0:T(8,128)(2,1)}, bf16[2,256,512]{2,1,0:T(8,128)(2,1)}, bf16[2,768,512]{2,1,0:T(8,128)(2,...) custom-call(bf16[256,2048]{1,0:T(8,128)(2,1)} %get-tuple-element.65.branch_ref, ...), custom_call_target="tpu_custom_call" | custom-call | flops 107374182400 | bytes 104857600 | tf_op jit(solution)/shard_map/rear/pallas_call | solution.py:1600
  731.2 2.8 convert_element_type.115
  734.0 0.2 convert_add_fusion
  734.2 2.1 copy.17
  736.3 0.9 add_bitcast_fusion.3
  737.2 2.1 add_bitcast_fusion.1
  739.3 0.1 copy-done.1
  739.4 0.4 add_bitcast_fusion.2
  739.8 0.5 pad_maximum_fusion
  740.3 5.2 copy.18
  745.6 1.6 add_bitcast_fusion
  747.2 1.0 copy.29
  (17 shorter events, 0.0 us)
Async XLA Ops:
  0.6 22.3 %collective-permute-start = (s32[1]{0:T(128)}, s32[1]{0:T(128)}, u32[]{:S(2)}, u32[]{:S(2)}) collective-permute-start(s32[1]{0:T(128)} %param.8), channel_id=1, source_target_pairs={{0,0},{4,8},{8,4},{12,12},{1,1},{5,9},{9,5},{13,13},{2,2},{6,10},{... | collective-permute-start | bytes 20 | tf_op jit(solution)/shard_map/ppermute | solution.py:1637
  8.4 5.3 copy-start.3
  327.0 12.7 %slice-start = ((s8[8388608]{0:T(1024)(128)(4,1)}), s8[4194304]{0:T(1024)(128)(4,1)S(1)}, s32[]{:S(2)}) async-start(s8[8388608]{0:T(1024)(128)(4,1)} %bitcast.31), calls=%async_computation | async-start | bytes 8388608
  327.1 12.7 %copy-start.6 = (bf16[2048,1024]{1,0:T(8,128)(2,1)S(1)}, bf16[2048,1024]{1,0:T(8,128)(2,1)}, u32[]{:S(2)}) copy-start(bf16[2048,1024]{1,0:T(8,128)(2,1)} %get-tuple-element.64.hidden_ref) | copy-start | bytes 12582916
  333.4 6.3 slice-start.1
  731.1 2.8 copy-start.2
  734.2 2.1 copy-start.5
  737.2 2.2 copy-start.1
  740.3 5.3 copy-start
  745.6 1.6 copy-start.4

commit v7 on v6

--- a/solution.py
+++ b/solution.py
@@ -474,7 +474,9 @@
         in_specs=in_specs,
         out_specs=[VMEM_WHOLE] * (n_out + n_move),
         scratch_shapes=[DMA((max(n_move, 1), 4)), *scratch],
-        compiler_params=pltpu.CompilerParams(collective_id=ident, has_side_effects=True, vmem_limit_bytes=63 << 20),
+        compiler_params=pltpu.CompilerParams(
+            collective_id=ident, has_side_effects=True, vmem_limit_bytes=(64 << 20) - (64 << 10)
+        ),
         cost_estimate=pl.CostEstimate(
             flops=flops + (20 << 30), bytes_accessed=size, transcendentals=transcendentals
         ),
@@ -615,6 +617,11 @@
     return [first.at[0], first.at[1], second.at[0], second.at[1]]
 
 
+def both_halves(cos_ref, sin_ref, rows):
+    cos, sin = cos_ref[rows, :], sin_ref[rows, :]
+    return jnp.concatenate([cos, cos], axis=1), jnp.concatenate([-sin, sin], axis=1)
+
+
 def beside(under):
     def begin():
         under.start_y()
@@ -626,12 +633,12 @@
 class Turned:
     def __init__(self, source, stage, sems, flipped):
         self.source, self.stage, self.sems, self.flipped = source, stage, sems, flipped
-        self.tile = stage.shape[1]
-        self.count = flipped.shape[1] // self.tile
+        self.tile, self.strip = 256, stage.shape[1]
+        self.count = flipped.shape[1] // self.strip
 
     def load(self, i):
         slot = lax.rem(i, 2)
-        rows = span(i * self.tile, self.tile)
+        rows = span(i * self.strip, self.strip)
         return pltpu.make_async_copy(self.source.at[rows], self.stage.at[slot], self.sems.at[slot])
 
     def turn(self):
@@ -642,7 +649,7 @@
             def _():
                 self.load(i + 1).start()
 
-            self.flipped[:, span(i * self.tile, self.tile)] = self.stage[lax.rem(i, 2)].T
+            self.flipped[:, span(i * self.strip, self.strip)] = self.stage[lax.rem(i, 2)].T
             return carry
 
         self.load(0).start()
@@ -663,7 +670,7 @@
         lax.fori_loop(0, 4 * each, step, 0)
 
 
-def down_call(hidden, firsts, seconds, middle, owns, moved, normed, grads, gate_other, ident):
+def down_call(hidden, firsts, seconds, middle, own, moved, normed, grads, gate_other, ident):
     piece, width = middle.shape
     tokens, both = grads.shape
     part_width = both // 2
@@ -671,7 +678,7 @@
     tile = 256
 
     def kernel(
-        hidden_ref, first_a, first_b, second_a, second_b, base_ref, own_0, own_1, moved_0, moved_1, grads_ref, normed_ref, gate_other,
+        hidden_ref, first_a, first_b, second_a, second_b, base_ref, own_ref, moved_ref, grads_ref, normed_ref, gate_other,
         result_ref, down_out, gate_out, up_own_out, up_other_out,
         down_sum, stage, flipped, gate_moved, kept, spare,
         y_sems, z_sems, load_sems, store_sems, *reduce_refs
@@ -681,13 +688,16 @@
         y = place.y
 
         turned = Turned(normed_ref, stage, load_sems, flipped)
-        for j, (own, came) in enumerate(((own_0, moved_0), (own_1, moved_1))):
-            def step(i, carry, j=j, own=own, came=came):
-                rows = span(i * 64, 64)
-                down_sum[j, rows, :] = (own[rows, :].astype(F32) + came[rows, :].astype(F32)).astype(BF)
+        for j in (0, 1):
+            cols = pl.ds(j * block, block)
+
+            def step(i, carry, j=j, cols=cols):
+                upper, rows = i // (own_ref.shape[1] // 64), span(lax.rem(i, own_ref.shape[1] // 64) * 64, 64)
+                total = own_ref[upper, rows, cols].astype(F32) + moved_ref[upper, rows, cols].astype(F32)
+                down_sum[j, span(i * 64, 64), :] = total.astype(BF)
                 return carry
 
-            lax.fori_loop(0, own_0.shape[0] // 64, step, 0)
+            lax.fori_loop(0, down_sum.shape[1] // 64, step, 0)
         z_down = GradHalf(place, down_sum, down_out, z_sems.at[0])
         y_gate = Beyond(place, gate_other, gate_moved, y_sems.at[0])
         y_gate.start()
@@ -707,6 +717,7 @@
             return pltpu.make_async_copy(ref, out, store_sems.at[i])
 
         def after_z():
+            turned.turn()
             turned.times(grads_ref, spare, (1 - y) * (width // 2), part_width)
             store(up_other_out, spare, 0).start()
             turned.times(grads_ref, kept, y * (width // 2), 0)
@@ -714,7 +725,7 @@
             turned.times(grads_ref, spare, y * (width // 2), part_width)
             store(up_own_out, spare, 1).start()
 
-        reduce_body(place, compute, last, reduce_refs, begin=z_down.start, before_z=turned.turn, after_z=after_z)
+        reduce_body(place, compute, last, reduce_refs, begin=z_down.start, after_z=after_z)
         y_gate.wait_recv()
         for i in (0, 1):
             def add(n, carry, i=i):
@@ -732,12 +743,12 @@
 
     shape = jax.ShapeDtypeStruct
     half = shape((2, block, part_width), BF)
-    down_shape = (2, *owns[0].shape)
+    down_shape = (2, hidden.shape[1], block)
     held = pltpu.VMEM(half.shape, BF)
     return pl.pallas_call(
         kernel,
         out_shape=[shape((piece, width), BF), shape(down_shape, BF), half, half, half],
-        in_specs=[VMEM_WHOLE] * 11 + [ANYWHERE] * 2,
+        in_specs=[VMEM_WHOLE] * 9 + [ANYWHERE] * 2,
         out_specs=[VMEM_WHOLE] + [ANYWHERE] * 4,
         scratch_shapes=[
             pltpu.VMEM(down_shape, BF),
@@ -749,10 +760,10 @@
         compiler_params=pltpu.CompilerParams(collective_id=ident, has_side_effects=True, vmem_limit_bytes=63 << 20),
         cost_estimate=pl.CostEstimate(flops=60 << 30, bytes_accessed=60 << 20, transcendentals=0),
         name="reduce_down",
-    )(hidden, *firsts, *seconds, middle, *owns, *moved, grads, normed, gate_other)
-
-
-def middle_call(cot, slopes, gates, ups, downs, down_last, normed, moves, middle, ident):
+    )(hidden, *firsts, *seconds, middle, own, moved, grads, normed, gate_other)
+
+
+def middle_call(cot, slopes, hidden_rows, gates, ups, downs, down_last, normed, moves, middle, ident):
     piece, width = middle.shape
     tokens, part_width = cot.shape[0], down_last.shape[1]
     hidden = 2 * part_width
@@ -760,9 +771,10 @@
     tiles = part_width // tile
 
     def body(place, ins, outs, scratch, under, targets):
-        cot_hbm, slopes_ref, normed_ref, ga1, ga2, gb1, gb2, ua1, ua2, ub1, ub2, value_ref, da1, da2, db1 = ins
-        total_ref, branch_ref, grad_ref, gate_other = outs
-        load_sem, cot_ref, base_ref, stage, *rest = scratch
+        cot_hbm, slopes_ref, normed_ref, hidden_ref, ga1, ga2, gb1, gb2, ua1, ua2, ub1, ub2, value_ref, da1, da2, db1 = ins
+        total_ref, branch_ref, grad_ref, gate_other, down_own, down_moved = outs
+        load_sem, cot_ref, stage, down_other, y_sem, turned_hidden, *rest = scratch
+        strip = stage.shape[1]
         under.start_y()
         loads = [
             pltpu.make_async_copy(slopes_ref, grad_ref, load_sem.at[0]),
@@ -772,7 +784,43 @@
             load.start()
         for load in loads:
             load.wait()
-        base_ref[...] = cot_ref[span(place.block * piece, piece), :]
+        base_ref = stage.at[0]
+
+        def hidden_load(i):
+            slot = lax.rem(i, 2)
+            return pltpu.make_async_copy(
+                hidden_ref.at[span(i * strip, strip)], stage.at[slot, :, pl.ds(0, hidden)], load_sem.at[slot]
+            )
+
+        def turn(i, carry):
+            hidden_load(i).wait()
+
+            @pl.when(i + 1 < tokens // strip)
+            def _():
+                hidden_load(i + 1).start()
+
+            value = stage[lax.rem(i, 2), :, 0:hidden].T
+            for j in range(hidden // tile):
+                turned_hidden[j, :, span(i * strip, strip)] = value[j * tile:(j + 1) * tile]
+            return carry
+
+        def down_half(out, which):
+            half = width // 4
+            each = hidden // 2 // tile
+
+            def step(n, carry):
+                m, t = n // 2, lax.rem(n, 2)
+                value = dot(turned_hidden[m], cot_ref[:, span(which * 2 * half + t * half, half)], NN)
+                out[m // each, span(lax.rem(m, each) * tile, tile), span(t * half, half)] = value.astype(BF)
+                return carry
+
+            lax.fori_loop(0, 2 * (hidden // tile), step, 0)
+
+        hidden_load(0).start()
+        lax.fori_loop(0, tokens // strip, turn, 0)
+        down_half(down_other, 1 - place.y)
+        y_down = Beyond(place, down_other, down_moved, y_sem)
+        y_down.start()
         rows_in = (quarters(da1, da2), quarters(db1, targets[0]))
 
         def fill(owner, part):
@@ -820,25 +868,35 @@
         turned = Turned(normed_ref, stage, load_sem, cot_ref)
 
         def after_z():
+            down_half(down_own, place.y)
             turned.turn()
+            base_load = pltpu.make_async_copy(cot_hbm.at[span(place.block * piece, piece)], base_ref, load_sem.at[0])
+            base_load.start()
             turned.times(grad_ref, gate_other, (1 - place.y) * (width // 2), 0)
+            base_load.wait()
 
         reduce_body(place, compute, last, rest, after_z=after_z, split=2)
         under.end(skip=1)
+        y_down.wait_recv()
+        y_down.wait_send()
 
     shape = functools.partial(jax.ShapeDtypeStruct, (piece, width))
+    down_half_shape = jax.ShapeDtypeStruct((2, hidden // 2, width // 2), BF)
     return comm_call(
-        body, "reduce_middle", ident, [cot, slopes, normed, *gates, *ups, middle, *downs, down_last],
+        body, "reduce_middle", ident, [cot, slopes, normed, hidden_rows, *gates, *ups, middle, *downs, down_last],
         [
             shape(F32), shape(BF), jax.ShapeDtypeStruct((tokens, 2 * hidden), BF),
             jax.ShapeDtypeStruct((2, width // 4, hidden), BF),
+            down_half_shape,
+            down_half_shape,
         ],
         [
-            DMA((2,)), pltpu.VMEM((tokens, width), BF), pltpu.VMEM((piece, width), BF), pltpu.VMEM((2, tile, width), BF),
-            *reduce_scratch(piece, width),
+            DMA((2,)), pltpu.VMEM((tokens, width), BF), pltpu.VMEM((2, piece, width), BF),
+            pltpu.VMEM(down_half_shape.shape, BF), DMA((4,)),
+            pltpu.VMEM((hidden // tile, tile, tokens), BF), *reduce_scratch(piece, width),
         ],
         moves, flops=6 * tokens * hidden * width,
-        spaces=[ANYWHERE] * 3 + [VMEM_WHOLE] * 12,
+        spaces=[ANYWHERE] * 4 + [VMEM_WHOLE] * 12,
     )
 
 
@@ -984,7 +1042,8 @@
     half = hd // 2
 
     def unrotate(g, rows):
-        return g * cos_ref[rows, :] - pltpu.roll(g, half, 1) * sin_ref[rows, :]
+        cos, sin = both_halves(cos_ref, sin_ref, rows)
+        return g * cos - pltpu.roll(g, half, 1) * sin
 
     def head(h, carry):
         base = h * 3 * hd
@@ -1182,7 +1241,7 @@
             total = acc[rows, :]
             for weight, index in zip(parts("qkv")[2:], place.order[2:]):
                 total = total + dot(normed[rows, span(index * depth, depth)], weight[...], NN)
-            cos, sin = cos_ref[rows, :], sin_ref[rows, :]
+            cos, sin = both_halves(cos_ref, sin_ref, rows)
             for h in range(heads):
                 for part in range(3):
                     value = total[:, (3 * h + part) * hd:(3 * h + part + 1) * hd]
@@ -1329,10 +1388,6 @@
 
             lax.fori_loop(0, part_width // tile, step, 0)
 
-        def begin():
-            go("da")
-            go("db")
-
         def process(owner):
             waiting.append(owner)
             if len(waiting) == 1:
@@ -1341,6 +1396,8 @@
                 got("ua")
             fill(owner, 0)
             if len(waiting) == 3:
+                go("da")
+                go("db")
                 pass_on("ub")
                 got("ub")
                 for earlier in waiting:
@@ -1348,7 +1405,7 @@
             elif len(waiting) > 3:
                 fill(owner, 1)
 
-        gather_body(place, normed_own, full, feed_sems, process, begin=begin, split=0)
+        gather_body(place, normed_own, full, feed_sems, process)
         for i, (ref, out) in enumerate(((full, normed_mid_out), (hidden_ref, hidden_out), (slopes_ref, slopes_out))):
             pltpu.make_async_copy(ref, out, out_sems.at[SLICES + i]).start()
         pass_on("da")
@@ -1636,8 +1693,7 @@
     y = lax.axis_index("y")
     prefix_len = lax.ppermute(prefix_len, ("core", "zh"), [(0, 0), (1, 2), (2, 1), (3, 3)])
     prefix = jnp.broadcast_to(prefix_len[:, None], (8, 128))
-    cosine, sine = rope_tables(tokens, hd)
-    tables = (jnp.concatenate([cosine, cosine], axis=1), jnp.concatenate([-sine, sine], axis=1))
+    tables = rope_tables(tokens, hd)
     part = hidden_width // 2
     ga, gb = w_up_gate[:, 0, :part], w_up_gate[:, 0, part:]
     ua, ub = w_up_gate[:, 1, :part], w_up_gate[:, 1, part:]
@@ -1650,20 +1706,12 @@
     qkv, mixed, lse, own_in, middle, normed_in, cot_full, normed_mid, hidden, slopes = results
     gates = (ga_1, ga_2, gb_1, gb_2)
 
-    block = cot_full.shape[1] // 4
-
-    def down_block(index):
-        cut = lax.dynamic_slice_in_dim(cot_full, index * block, block, 1)
-        return mm("tf,td->fd", hidden, cut).astype(BF)
-
-    owns = [down_block(2 * y + i) for i in (0, 1)]
-    others = [down_block(2 * (1 - y) + i) for i in (0, 1)]
-    (grad_middle, branch_own, grad_gate_up, gate_other), (db_2, *moved) = middle_call(
-        cot_full, slopes, gates, (ua_1, ua_2, ub_1, ub_2), (da_1, da_2), db_1, normed_mid,
-        [("beyond", db_1), *(("beyond", other) for other in others)], middle, 5,
+    (grad_middle, branch_own, grad_gate_up, gate_other, down_own, down_moved), (db_2,) = middle_call(
+        cot_full, slopes, hidden, gates, (ua_1, ua_2, ub_1, ub_2), (da_1, da_2), db_1, normed_mid,
+        [("beyond", db_1)], middle, 5,
     )
     outputs, down_final, gate_sum, up_own, up_other = down_call(
-        hidden, (da_1, db_1), (da_2, db_2), middle, owns, moved, normed_mid, grad_gate_up, gate_other, 6
+        hidden, (da_1, db_1), (da_2, db_2), middle, down_own, down_moved, normed_mid, grad_gate_up, gate_other, 6
     )
     gate_final, up_final, out_final, qkv_final, outputs, input_grad = rear_call(
         branch_own, (out_1, out_2), (qkv_1, qkv_2), qkv, mixed, lse, prefix, tables, grad_middle, own_in, outputs,

time: 758 us -> 735 us (0.970)
  matrix products: 19.4 us -> 0 us
    dot_general x4 -> x0, matrix products: 19.4 us -> none  [mm(): return jnp.einsum(spec, left, right, preferred_element_type=F32)]
where the time goes in v7:
time: 735 us; the launch traced here: 728 us
  Pallas kernels  687 us (93%)
  local copies, waits for them, and re-layouts  20.2 us (3%)
  other arithmetic  13.4 us (2%)
    pallas_call x1, Pallas kernels, front_call(): pl.pallas_call(kernel, out_shape=outs, in_specs=[ANYWHERE, ANYWHERE, VMEM...  301 us
    pallas_call x1, Pallas kernels, rear_call(): pl.pallas_call(kernel, out_shape=[shape(gate_sum.shape, BF), shape(up_own...  211 us
    pallas_call x1, Pallas kernels, comm_call(): pl.pallas_call(kernel, out_shape=shapes, in_specs=in_specs, out_specs=[VM...  98.9 us
    pallas_call x1, Pallas kernels, down_call(): pl.pallas_call(kernel, out_shape=[shape((piece, width), BF), shape(down_s...  76.3 us
  transfers between devices with their start and end apart: 1, of which 0 were waited for; matrix products, arithmetic and copies ran while one was open for 2% of the time, Pallas kernels for 0%

profile of v7, /device:TPU:1, one launch (start us, length us, event | category | flops | bytes accessed | tf_op | source)
XLA Modules:
  0.0 727.7 jit_solution(18192491188888654084)
XLA Ops:
  0.6 0.0 copy-start.5
  0.6 0.0 copy-start
  0.7 5.9 collective-permute-start
  6.6 2.1 copy.23
  8.7 0.0 copy-done.5
  8.7 1.0 fusion.1
  9.7 0.0 copy-done
  9.7 2.9 fusion
  12.7 5.5 multiply_sine_fusion
  18.2 1.3 copy_bitcast_fusion
  19.5 1.2 copy_bitcast_fusion.2
  20.7 0.0 collective-permute-done
  20.7 1.2 broadcast_in_dim.5.prefix_ref
  21.9 300.8 %front.1 = (bf16[2,512,768]{2,1,0:T(8,128)(2,1)}, bf16[2,256,512]{2,1,0:T(8,128)(2,1)}, bf16[2,512,512]{2,1,0:T(8,128)(2,1)}, bf16[2,512,512]{2,1,0:T(8,128)(2,1...) custom-call(bf16[2048,256]{1,0:T(8,128)(2,1)} %in_ref.1, ...), custom_call_target="tpu_custom_call" | custom-call | flops 107374182400 | bytes 104857600 | tf_op jit(solution)/shard_map/front/pallas_call | solution.py:1444
  322.7 98.9 %reduce_middle.1 = (f32[256,2048]{1,0:T(8,128)}, bf16[256,2048]{1,0:T(8,128)(2,1)}, bf16[2048,2048]{1,0:T(8,128)(2,1)}, bf16[2,512,1024]{2,1,0:T(8,128)(2,1)}, b...) custom-call(bf16[2048,2048]{1,0:T(8,128)(2,1)} %get-tuple-element.49.refs_0_, ...), custom_call_target="tpu_custom_call" | custom-call | flops 47244640256 | bytes 62914560 | tf_op jit(solution)/shard_map/reduce_middle/pallas_call | solution.py:471
  421.6 76.3 %reduce_down.1 = (bf16[256,2048]{1,0:T(8,128)(2,1)}, bf16[2,1024,512]{2,1,0:T(8,128)(2,1)}, bf16[2,512,1024]{2,1,0:T(8,128)(2,1)}, bf16[2,512,1024]{2,1,0:T(8,128)(2,1)}, bf16[2,512,1024]{2,1,0:T(8,128)(2,1)}) custom-call(bf16[2048,1024]{1,0:T(8,128)(2,1)} %get-tuple-element.52.refs_3_.hidden_ref, bf16[2,512,512]{2,1,0:T(8,128)(2,1)} %get-tuple-element.62.refs_13_.first_a, ...), custom_call_target="tpu_custom_call" | custom-call | flops 64424509440 | bytes 62914560 | tf_op jit(solution)/shard_map/reduce_down/pallas_call | solution.py:748
  498.0 211.2 %rear.1 = (bf16[2,512,1024]{2,1,0:T(8,128)(2,1)}, bf16[2,512,1024]{2,1,0:T(8,128)(2,1)}, bf16[2,256,512]{2,1,0:T(8,128)(2,1)}, bf16[2,768,512]{2,1,0:T(8,128)(2,...) custom-call(bf16[256,2048]{1,0:T(8,128)(2,1)} %get-tuple-element.65.branch_ref, ...), custom_call_target="tpu_custom_call" | custom-call | flops 107374182400 | bytes 104857600 | tf_op jit(solution)/shard_map/rear/pallas_call | solution.py:1657
  709.2 1.9 add_bitcast_fusion.3
  711.1 1.6 convert_add_fusion
  712.7 0.0 copy-start.4
  712.7 2.1 copy.17
  714.8 0.0 copy-done.4
  714.8 1.5 convert_element_type.99
  716.3 0.9 copy-done.3
  717.1 0.4 add_bitcast_fusion.2
  717.5 1.2 copy-done.2
  718.7 0.4 add_bitcast_fusion.1
  719.1 0.5 pad_maximum_fusion
  719.6 0.0 copy-start.1
  719.6 5.2 copy.18
  724.9 1.6 add_bitcast_fusion
  726.5 1.0 copy.29
  (7 shorter events, 0.0 us)
Async XLA Ops:
  0.6 8.1 %copy-start.5 = (bf16[1024,512]{1,0:T(8,128)(2,1)S(1)}, bf16[1024,512]{1,0:T(8,128)(2,1)}, u32[]{:S(2)}) copy-start(bf16[1024,512]{1,0:T(8,128)(2,1)} %param.12) | copy-start | bytes 3145732
  0.6 9.1 %copy-start = (bf16[512,2,1024]{2,1,0:T(2,128)(2,1)S(1)}, bf16[512,2,1024]{2,1,0:T(2,128)(2,1)}, u32[]{:S(2)}) copy-start(bf16[512,2,1024]{2,1,0:T(2,128)(2,1)} %param.11) | copy-start | bytes 6291460
  0.7 20.1 %collective-permute-start = (s32[1]{0:T(128)}, s32[1]{0:T(128)}, u32[]{:S(2)}, u32[]{:S(2)}) collective-permute-start(s32[1]{0:T(128)} %param.8), channel_id=1, source_target_pairs={{0,0},{4,8},{8,4},{12,12},{1,1},{5,9},{9,5},{13,13},{2,2},{6,10},{... | collective-permute-start | bytes 20 | tf_op jit(solution)/shard_map/ppermute | solution.py:1694
  712.7 2.1 copy-start.4
  714.8 2.3 copy-start.3
  717.1 1.6 copy-start.2
  719.6 5.3 copy-start.1
  724.9 1.6 copy-start.6

commit v8 on v7

--- a/solution.py
+++ b/solution.py
@@ -1589,7 +1589,6 @@
         y_up.wait_recv()
         add(up_moved, up_own_ref, up_own.shape[1])
         z_up.start()
-        ready_spread.start()
 
         def flip(source, columns):
             def step(i, carry):
@@ -1620,17 +1619,16 @@
             heads, hd,
         )
         load.wait()
+        ready_spread.start()
 
         def last(rows, total):
             value = back_rows(middle_ref[rows, :], own_in_ref[rows, :].astype(F32), total)
             result_ref[rows, :] = value.astype(BF)
 
-        def before_z():
+        def after_z():
             flip(grad_rows, inner)
             weigh(qkv_grads, 0, 1 - y, inner)
             y_qkv.start()
-
-        def after_z():
             y_out.wait_recv()
             add(out_grads.at[1], out_grads.at[2], inner_out)
             z_out.start()
@@ -1638,7 +1636,7 @@
 
         reduce_body(
             place, product(place, grad_rows, quarters(qkv_1, qkv_2), True), last, reduce_refs,
-            before_z=before_z, after_z=after_z, split=0,
+            after_z=after_z, split=0,
         )
         result_spread = Spread(place, result_ref, result_out, result_sems)
         result_spread.start()

time: 735 us -> 733 us (level)
  no operation moved by 1% of the time
where the time goes in v8:
time: 733 us; the launch traced here: 725 us
  Pallas kernels  685 us (93%)
  local copies, waits for them, and re-layouts  20.2 us (3%)
  other arithmetic  13.4 us (2%)
    pallas_call x1, Pallas kernels, front_call(): pl.pallas_call(kernel, out_shape=outs, in_specs=[ANYWHERE, ANYWHERE, VMEM...  301 us
    pallas_call x1, Pallas kernels, rear_call(): pl.pallas_call(kernel, out_shape=[shape(gate_sum.shape, BF), shape(up_own...  209 us
    pallas_call x1, Pallas kernels, comm_call(): pl.pallas_call(kernel, out_shape=shapes, in_specs=in_specs, out_specs=[VM...  98.9 us
    pallas_call x1, Pallas kernels, down_call(): pl.pallas_call(kernel, out_shape=[shape((piece, width), BF), shape(down_s...  76.3 us
  transfers between devices with their start and end apart: 1, of which 0 were waited for; matrix products, arithmetic and copies ran while one was open for 2% of the time, Pallas kernels for 0%

profile of v8, /device:TPU:1, one launch (start us, length us, event | category | flops | bytes accessed | tf_op | source)
XLA Modules:
  0.0 725.5 jit_solution(12894525858905386698)
XLA Ops:
  0.6 0.0 copy-start.5
  0.6 0.0 copy-start
  0.7 5.9 collective-permute-start
  6.6 2.1 copy.23
  8.7 0.0 copy-done.5
  8.7 1.0 fusion.1
  9.7 0.0 copy-done
  9.7 2.9 fusion
  12.7 5.5 multiply_sine_fusion
  18.2 1.3 copy_bitcast_fusion
  19.5 1.2 copy_bitcast_fusion.2
  20.7 0.0 collective-permute-done
  20.7 1.2 broadcast_in_dim.5.prefix_ref
  21.9 300.8 %front.1 = (bf16[2,512,768]{2,1,0:T(8,128)(2,1)}, bf16[2,256,512]{2,1,0:T(8,128)(2,1)}, bf16[2,512,512]{2,1,0:T(8,128)(2,1)}, bf16[2,512,512]{2,1,0:T(8,128)(2,1...) custom-call(bf16[2048,256]{1,0:T(8,128)(2,1)} %in_ref.1, ...), custom_call_target="tpu_custom_call" | custom-call | flops 107374182400 | bytes 104857600 | tf_op jit(solution)/shard_map/front/pallas_call | solution.py:1444
  322.7 98.9 %reduce_middle.1 = (f32[256,2048]{1,0:T(8,128)}, bf16[256,2048]{1,0:T(8,128)(2,1)}, bf16[2048,2048]{1,0:T(8,128)(2,1)}, bf16[2,512,1024]{2,1,0:T(8,128)(2,1)}, b...) custom-call(bf16[2048,2048]{1,0:T(8,128)(2,1)} %get-tuple-element.49.refs_0_, ...), custom_call_target="tpu_custom_call" | custom-call | flops 47244640256 | bytes 62914560 | tf_op jit(solution)/shard_map/reduce_middle/pallas_call | solution.py:471
  421.6 76.3 %reduce_down.1 = (bf16[256,2048]{1,0:T(8,128)(2,1)}, bf16[2,1024,512]{2,1,0:T(8,128)(2,1)}, bf16[2,512,1024]{2,1,0:T(8,128)(2,1)}, bf16[2,512,1024]{2,1,0:T(8,128)(2,1)}, bf16[2,512,1024]{2,1,0:T(8,128)(2,1)}) custom-call(bf16[2048,1024]{1,0:T(8,128)(2,1)} %get-tuple-element.52.refs_3_.hidden_ref, bf16[2,512,512]{2,1,0:T(8,128)(2,1)} %get-tuple-element.62.refs_13_.first_a, ...), custom_call_target="tpu_custom_call" | custom-call | flops 64424509440 | bytes 62914560 | tf_op jit(solution)/shard_map/reduce_down/pallas_call | solution.py:748
  498.0 209.0 %rear.1 = (bf16[2,512,1024]{2,1,0:T(8,128)(2,1)}, bf16[2,512,1024]{2,1,0:T(8,128)(2,1)}, bf16[2,256,512]{2,1,0:T(8,128)(2,1)}, bf16[2,768,512]{2,1,0:T(8,128)(2,...) custom-call(bf16[256,2048]{1,0:T(8,128)(2,1)} %get-tuple-element.65.branch_ref, ...), custom_call_target="tpu_custom_call" | custom-call | flops 107374182400 | bytes 104857600 | tf_op jit(solution)/shard_map/rear/pallas_call | solution.py:1655
  706.9 1.9 add_bitcast_fusion.3
  708.8 1.6 convert_add_fusion
  710.4 0.0 copy-start.4
  710.5 2.1 copy.17
  712.5 0.0 copy-done.4
  712.5 1.5 convert_element_type.99
  714.0 0.9 copy-done.3
  714.9 0.4 add_bitcast_fusion.2
  715.3 1.2 copy-done.2
  716.5 0.4 add_bitcast_fusion.1
  716.9 0.5 pad_maximum_fusion
  717.4 5.2 copy.18
  722.6 1.6 add_bitcast_fusion
  724.3 0.0 copy-done.6
  724.3 1.0 copy.29
  (7 shorter events, 0.0 us)
Async XLA Ops:
  0.6 8.1 %copy-start.5 = (bf16[1024,512]{1,0:T(8,128)(2,1)S(1)}, bf16[1024,512]{1,0:T(8,128)(2,1)}, u32[]{:S(2)}) copy-start(bf16[1024,512]{1,0:T(8,128)(2,1)} %param.12) | copy-start | bytes 3145732
  0.6 9.1 %copy-start = (bf16[512,2,1024]{2,1,0:T(2,128)(2,1)S(1)}, bf16[512,2,1024]{2,1,0:T(2,128)(2,1)}, u32[]{:S(2)}) copy-start(bf16[512,2,1024]{2,1,0:T(2,128)(2,1)} %param.11) | copy-start | bytes 6291460
  0.7 20.1 %collective-permute-start = (s32[1]{0:T(128)}, s32[1]{0:T(128)}, u32[]{:S(2)}, u32[]{:S(2)}) collective-permute-start(s32[1]{0:T(128)} %param.8), channel_id=1, source_target_pairs={{0,0},{4,8},{8,4},{12,12},{1,1},{5,9},{9,5},{13,13},{2,2},{6,10},{... | collective-permute-start | bytes 20 | tf_op jit(solution)/shard_map/ppermute | solution.py:1692
  710.4 2.1 copy-start.4
  712.5 2.3 copy-start.3
  714.9 1.6 copy-start.2
  717.4 5.3 copy-start.1
  722.6 1.6 copy-start.6

commit v9 on v8

--- a/solution.py
+++ b/solution.py
@@ -1397,12 +1397,13 @@
             fill(owner, 0)
             if len(waiting) == 3:
                 go("da")
-                go("db")
                 pass_on("ub")
                 got("ub")
                 for earlier in waiting:
                     fill(earlier, 1)
             elif len(waiting) > 3:
+                if len(waiting) == 4:
+                    go("db")
                 fill(owner, 1)
 
         gather_body(place, normed_own, full, feed_sems, process)

time: 733 us -> 737 us (level)
  no operation moved by 1% of the time
where the time goes in v9:
time: 737 us; the launch traced here: 729 us
  Pallas kernels  689 us (93%)
  local copies, waits for them, and re-layouts  20.2 us (3%)
  other arithmetic  13.4 us (2%)
    pallas_call x1, Pallas kernels, front_call(): pl.pallas_call(kernel, out_shape=outs, in_specs=[ANYWHERE, ANYWHERE, VMEM...  306 us
    pallas_call x1, Pallas kernels, rear_call(): pl.pallas_call(kernel, out_shape=[shape(gate_sum.shape, BF), shape(up_own...  209 us
    pallas_call x1, Pallas kernels, comm_call(): pl.pallas_call(kernel, out_shape=shapes, in_specs=in_specs, out_specs=[VM...  98.9 us
    pallas_call x1, Pallas kernels, down_call(): pl.pallas_call(kernel, out_shape=[shape((piece, width), BF), shape(down_s...  74.9 us
  transfers between devices with their start and end apart: 1, of which 0 were waited for; matrix products, arithmetic and copies ran while one was open for 2% of the time, Pallas kernels for 0%

profile of v9, /device:TPU:1, one launch (start us, length us, event | category | flops | bytes accessed | tf_op | source)
XLA Modules:
  0.0 729.5 jit_solution(8380531483350771423)
XLA Ops:
  0.6 0.0 copy-start.5
  0.6 0.0 copy-start
  0.7 5.9 collective-permute-start
  6.6 2.1 copy.23
  8.7 0.0 copy-done.5
  8.7 1.0 fusion.1
  9.7 0.0 copy-done
  9.7 2.9 fusion
  12.7 5.5 multiply_sine_fusion
  18.2 1.3 copy_bitcast_fusion
  19.5 1.2 copy_bitcast_fusion.2
  20.7 0.0 collective-permute-done
  20.7 1.2 broadcast_in_dim.5.prefix_ref
  21.9 306.1 %front.1 = (bf16[2,512,768]{2,1,0:T(8,128)(2,1)}, bf16[2,256,512]{2,1,0:T(8,128)(2,1)}, bf16[2,512,512]{2,1,0:T(8,128)(2,1)}, bf16[2,512,512]{2,1,0:T(8,128)(2,1...) custom-call(bf16[2048,256]{1,0:T(8,128)(2,1)} %in_ref.1, ...), custom_call_target="tpu_custom_call" | custom-call | flops 107374182400 | bytes 104857600 | tf_op jit(solution)/shard_map/front/pallas_call | solution.py:1445
  328.0 98.9 %reduce_middle.1 = (f32[256,2048]{1,0:T(8,128)}, bf16[256,2048]{1,0:T(8,128)(2,1)}, bf16[2048,2048]{1,0:T(8,128)(2,1)}, bf16[2,512,1024]{2,1,0:T(8,128)(2,1)}, b...) custom-call(bf16[2048,2048]{1,0:T(8,128)(2,1)} %get-tuple-element.49.refs_0_, ...), custom_call_target="tpu_custom_call" | custom-call | flops 47244640256 | bytes 62914560 | tf_op jit(solution)/shard_map/reduce_middle/pallas_call | solution.py:471
  426.9 74.9 %reduce_down.1 = (bf16[256,2048]{1,0:T(8,128)(2,1)}, bf16[2,1024,512]{2,1,0:T(8,128)(2,1)}, bf16[2,512,1024]{2,1,0:T(8,128)(2,1)}, bf16[2,512,1024]{2,1,0:T(8,128)(2,1)}, bf16[2,512,1024]{2,1,0:T(8,128)(2,1)}) custom-call(bf16[2048,1024]{1,0:T(8,128)(2,1)} %get-tuple-element.52.refs_3_.hidden_ref, bf16[2,512,512]{2,1,0:T(8,128)(2,1)} %get-tuple-element.62.refs_13_.first_a, ...), custom_call_target="tpu_custom_call" | custom-call | flops 64424509440 | bytes 62914560 | tf_op jit(solution)/shard_map/reduce_down/pallas_call | solution.py:748
  501.8 209.1 %rear.1 = (bf16[2,512,1024]{2,1,0:T(8,128)(2,1)}, bf16[2,512,1024]{2,1,0:T(8,128)(2,1)}, bf16[2,256,512]{2,1,0:T(8,128)(2,1)}, bf16[2,768,512]{2,1,0:T(8,128)(2,...) custom-call(bf16[256,2048]{1,0:T(8,128)(2,1)} %get-tuple-element.65.branch_ref, ...), custom_call_target="tpu_custom_call" | custom-call | flops 107374182400 | bytes 104857600 | tf_op jit(solution)/shard_map/rear/pallas_call | solution.py:1656
  711.0 1.9 add_bitcast_fusion.3
  712.9 1.6 convert_add_fusion
  714.5 0.0 copy-start.4
  714.5 2.1 copy.17
  716.5 0.0 copy-done.4
  716.5 1.5 convert_element_type.99
  718.0 0.9 copy-done.3
  718.9 0.4 add_bitcast_fusion.2
  719.3 1.2 copy-done.2
  720.5 0.4 add_bitcast_fusion.1
  720.9 0.5 pad_maximum_fusion
  721.4 5.2 copy.18
  726.6 1.6 add_bitcast_fusion
  728.3 0.0 copy-done.6
  728.3 1.0 copy.29
  (7 shorter events, 0.0 us)
Async XLA Ops:
  0.6 8.1 %copy-start.5 = (bf16[1024,512]{1,0:T(8,128)(2,1)S(1)}, bf16[1024,512]{1,0:T(8,128)(2,1)}, u32[]{:S(2)}) copy-start(bf16[1024,512]{1,0:T(8,128)(2,1)} %param.12) | copy-start | bytes 3145732
  0.6 9.1 %copy-start = (bf16[512,2,1024]{2,1,0:T(2,128)(2,1)S(1)}, bf16[512,2,1024]{2,1,0:T(2,128)(2,1)}, u32[]{:S(2)}) copy-start(bf16[512,2,1024]{2,1,0:T(2,128)(2,1)} %param.11) | copy-start | bytes 6291460
  0.7 20.1 %collective-permute-start = (s32[1]{0:T(128)}, s32[1]{0:T(128)}, u32[]{:S(2)}, u32[]{:S(2)}) collective-permute-start(s32[1]{0:T(128)} %param.8), channel_id=1, source_target_pairs={{0,0},{4,8},{8,4},{12,12},{1,1},{5,9},{9,5},{13,13},{2,2},{6,10},{... | collective-permute-start | bytes 20 | tf_op jit(solution)/shard_map/ppermute | solution.py:1693
  714.5 2.1 copy-start.4
  716.5 2.3 copy-start.3
  718.9 1.6 copy-start.2
  721.4 5.3 copy-start.1
  726.6 1.6 copy-start.6
